TPU v7x, 32 devices: a whole 2x2x4 slice. The times are simulated.
32 devices in a mesh: dp: 4 (over z), row: 2 (over y), col: 4 (over x, core).
Axes of the slice: x: 2, y: 2, z: 4, core: 2. Of those that a mesh axis runs over, the one named last changes fastest.
Arguments:
- layer_input: float32 [1024, 16384], P(('row', 'col'), 'dp'), may hold values from -6 to 6
- teacher: float32 [1024, 16384], P(('row', 'col'), 'dp'), may hold values from -6 to 6
- block_len: int32 [8], P('dp'), may hold values from 1 to 2048, as said below
- block_first: int32 [8], P('dp'), may hold values from 0 to 1, as said below
- norm_gain: float32 [1024], P(('row', 'col')), may hold values from 0.5 to 1.5
- norm_bias: float32 [1024], P(('row', 'col')), may hold values from -3 to 3
- ema_rate: float32 [1024, 16], P(('row', 'col')), may hold values from 0.002 to 0.1
- ema_angle: float32 [1024, 16], P(('row', 'col')), may hold values from 0 to 0.6
- ema_input: float32 [1024, 16], P(('row', 'col')), may hold values from -3 to 3
- ema_out_real: float32 [1024, 16], P(('row', 'col')), may hold values from -1 to 1
- ema_out_imag: float32 [1024, 16], P(('row', 'col')), may hold values from -1 to 1
- ema_skip: float32 [1024], P(('row', 'col')), may hold values from 0.5 to 1.5
- w_value: bfloat16 [2, 4, 128, 2048], P(None, 'col', None, 'row'), may hold values from -0.1875 to 0.1875
- w_shared: bfloat16 [2, 4, 128, 256], P(None, 'col', None, 'row'), may hold values from -0.1875 to 0.1875
- w_reset: bfloat16 [2, 4, 128, 2048], P(None, 'col', None, 'row'), may hold values from -0.1875 to 0.1875
- w_hidden: bfloat16 [2, 4, 128, 1024], P(None, 'col', None, 'row'), may hold values from -0.1875 to 0.1875
- w_update: bfloat16 [2, 4, 128, 1024], P(None, 'col', None, 'row'), may hold values from -0.1875 to 0.1875
- query_gain: float32 [256], P(('row', 'col')), may hold values from -3 to 3
- query_bias: float32 [256], P(('row', 'col')), may hold values from -3 to 3
- key_gain: float32 [256], P(('row', 'col')), may hold values from -3 to 3
- w_output: bfloat16 [2, 4, 256, 1024], P(None, 'col', None, 'row'), may hold values from -0.5 to 0.5
- final_gain: float32 [1024], P(('row', 'col')), may hold values from 0.5 to 1.5
- final_bias: float32 [1024], P(('row', 'col')), may hold values from -3 to 3
- w_gate: bfloat16 [2, 4, 128, 2560], P(None, 'col', None, 'row'), may hold values from -0.1875 to 0.1875
- w_up: bfloat16 [2, 4, 128, 2560], P(None, 'col', None, 'row'), may hold values from -0.1875 to 0.1875
- w_down: bfloat16 [2, 4, 320, 1024], P(None, 'col', None, 'row'), may hold values from -0.125 to 0.125
Outputs:
- layer_output: float32 [1024, 16384], P(('row', 'col'), 'dp')
- loss: float32 [], replicated
- input_grad: float32 [1024, 16384], P(('row', 'col'), 'dp')
- grad_norm_gain: float32 [1024], P(('row', 'col'))
- grad_norm_bias: float32 [1024], P(('row', 'col'))
- grad_ema_rate: float32 [1024, 16], P(('row', 'col'))
- grad_ema_angle: float32 [1024, 16], P(('row', 'col'))
- grad_ema_input: float32 [1024, 16], P(('row', 'col'))
- grad_ema_out_real: float32 [1024, 16], P(('row', 'col'))
- grad_ema_out_imag: float32 [1024, 16], P(('row', 'col'))
- grad_ema_skip: float32 [1024], P(('row', 'col'))
- grad_w_value: float32 [2, 4, 128, 2048], P(None, 'col', None, 'row')
- grad_w_shared: float32 [2, 4, 128, 256], P(None, 'col', None, 'row')
- grad_w_reset: float32 [2, 4, 128, 2048], P(None, 'col', None, 'row')
- grad_w_hidden: float32 [2, 4, 128, 1024], P(None, 'col', None, 'row')
- grad_w_update: float32 [2, 4, 128, 1024], P(None, 'col', None, 'row')
- grad_query_gain: float32 [256], P(('row', 'col'))
- grad_query_bias: float32 [256], P(('row', 'col'))
- grad_key_gain: float32 [256], P(('row', 'col'))
- grad_w_output: float32 [2, 4, 256, 1024], P(None, 'col', None, 'row')
- grad_final_gain: float32 [1024], P(('row', 'col'))
- grad_final_bias: float32 [1024], P(('row', 'col'))
- grad_w_gate: float32 [2, 4, 128, 2560], P(None, 'col', None, 'row')
- grad_w_up: float32 [2, 4, 128, 2560], P(None, 'col', None, 'row')
- grad_w_down: float32 [2, 4, 320, 1024], P(None, 'col', None, 'row')
Inputs may be any that keep to these rules, and one draw needn't show every extreme that they name: `block_len`: the slots of each dp index form 2 aligned blocks of 2048; a sequence takes a run of whole blocks beginning at a block whose block_first is 1, and block 0 of every dp index begins one; every block except the last of a sequence of two or more blocks has all 2048 slots valid; the valid slots of a block come first. `block_first`: 1 where a block begins a sequence, 0 where it continues one.
All inputs are finite; a program needn't handle non-finite values.
Results may differ from a plain program's by a relative error of at most 0.014.
Values may be sent and summed in bfloat16 or wider, within the bound.
A program may use at most 384 MiB of HBM per device.

v0:
```python
from functools import partial

import jax
import jax.numpy as jnp
from jax import lax
from jax.sharding import PartitionSpec as P

D = 1024
Z = 256
SPAN = 2048
GS = 32


EPSILON = 1e-05
NEGATIVE = -1000000000.0
PRECISE = lax.Precision.HIGHEST


def running_sums(values, first_flags, block_rows):
    height = values.shape[0]
    blocked = values.reshape(height, -1, block_rows)
    inside = jnp.cumsum(blocked, axis=2)
    totals = inside[:, :, -1]

    def carry_step(carried, scan_item):
        block_total, reset_flag = scan_item
        begin_sum = carried * (1.0 - reset_flag)
        return (begin_sum + block_total, begin_sum)

    unused, starts = lax.scan(
        carry_step, jnp.zeros((height,), jnp.float32), (totals.T, first_flags)
    )
    return (inside + starts.T[:, :, None]).reshape(height, -1)


def step_norm(layer_in, norm_gain, norm_bias, first_flags):
    channels, length = layer_in.shape
    grouped = layer_in.reshape(channels // GS, GS, length)
    sum_one = running_sums(jnp.sum(grouped, axis=1), first_flags, SPAN)
    sum_two = running_sums(jnp.sum(grouped * grouped, axis=1), first_flags, SPAN)
    counted = running_sums(jnp.ones((1, length), jnp.float32), first_flags, SPAN) * GS
    mean_val = sum_one / counted
    var_val = sum_two / counted - mean_val * mean_val
    centred = (grouped - mean_val[:, None, :]) * lax.rsqrt(var_val + EPSILON)[:, None, :]
    return centred.reshape(channels, length) * norm_gain[:, None] + norm_bias[:, None]


def silu_slope(pre_act):
    logistic = jax.nn.sigmoid(pre_act)
    return logistic * (1.0 + pre_act * (1.0 - logistic))


def contract_first(left_in, right_in):
    return lax.dot_general(
        left_in, right_in, (((0,), (0,)), ((), ())), preferred_element_type=jnp.float32
    )


def contract_last(left_in, right_in):
    return lax.dot_general(
        left_in, right_in, (((1,), (1,)), ((), ())), preferred_element_type=jnp.float32
    )


def ema_blocks(normed, ema_rate, ema_angle, ema_input, ema_out_real, ema_out_imag, piece_resets):
    piece_len = min(128, SPAN)
    channels, slot_count = normed.shape
    decay_rate = 1.0 - ema_rate
    in_coeff = jnp.sqrt(2.0 * ema_rate) * ema_input
    powers = jnp.arange(piece_len + 1, dtype=jnp.float32)[:, None, None]
    magnitude = jnp.exp(powers * jnp.log(decay_rate)[None])
    phases = powers * ema_angle[None]
    power_re = magnitude * jnp.cos(phases)
    power_im = magnitude * jnp.sin(phases)
    mixed_re = ema_out_real[None] * power_re - ema_out_imag[None] * power_im
    mixed_im = ema_out_real[None] * power_im + ema_out_imag[None] * power_re
    kernel = jnp.sum(in_coeff[None] * mixed_re[:piece_len], axis=2)
    offsets = jnp.arange(piece_len)[:, None] - jnp.arange(piece_len)[None, :]
    toeplitz = jnp.where(offsets[None] >= 0, kernel.T[:, jnp.maximum(offsets, 0)], 0.0)
    pieces = normed.reshape(channels, -1, piece_len)
    inside = jnp.einsum("cts,cbs->cbt", toeplitz, pieces, precision=PRECISE)
    back_re = power_re[:piece_len][::-1] * in_coeff[None]
    back_im = power_im[:piece_len][::-1] * in_coeff[None]
    ends_re = jnp.einsum("scj,cbs->cbj", back_re, pieces, precision=PRECISE)
    ends_im = jnp.einsum("scj,cbs->cbj", back_im, pieces, precision=PRECISE)
    keeping = (1.0 - piece_resets)[None, :, None]
    step_re = keeping * power_re[piece_len][:, None, :]
    step_im = keeping * power_im[piece_len][:, None, :]

    def combine(earlier, following):
        head_mre, head_mim, head_are, head_aim = earlier
        tail_mre, tail_mim, tail_are, tail_aim = following
        return (
            tail_mre * head_mre - tail_mim * head_mim,
            tail_mre * head_mim + tail_mim * head_mre,
            tail_mre * head_are - tail_mim * head_aim + tail_are,
            tail_mre * head_aim + tail_mim * head_are + tail_aim,
        )

    scanned = lax.associative_scan(combine, (step_re, step_im, ends_re, ends_im), axis=1)
    state_re = (
        jnp.concatenate([jnp.zeros_like(ends_re[:, :1]), scanned[2][:, :-1]], axis=1) * keeping
    )
    state_im = (
        jnp.concatenate([jnp.zeros_like(ends_im[:, :1]), scanned[3][:, :-1]], axis=1) * keeping
    )
    across = jnp.einsum("tcj,cbj->cbt", mixed_re[1:], state_re, precision=PRECISE) - jnp.einsum(
        "tcj,cbj->cbt", mixed_im[1:], state_im, precision=PRECISE
    )
    return (inside + across).reshape(channels, slot_count)


def front_piece(
    first_flags,
    piece_resets,
    layer_in,
    norm_gain,
    norm_bias,
    ema_rate,
    ema_angle,
    ema_input,
    ema_out_real,
    ema_out_imag,
    ema_skip,
):
    normed = step_norm(layer_in, norm_gain, norm_bias, first_flags)
    smoothed = ema_blocks(
        normed, ema_rate, ema_angle, ema_input, ema_out_real, ema_out_imag, piece_resets
    )
    return (normed, jax.nn.silu(smoothed + ema_skip[:, None] * normed))


def prepare(value_pre, shared, query_gain, query_bias, key_gain):
    return (
        jax.nn.silu(value_pre),
        shared * query_gain[:, None] + query_bias[:, None],
        shared * key_gain[:, None],
    )


def forward_products(sources, link_list):
    gathered = lax.all_gather(sources, "row", axis=1, tiled=True)
    columns = lax.axis_size("col")
    partials = []
    for member_slot, weight in link_list:
        matrix = weight.reshape(-1, weight.shape[-1])
        product = contract_first(matrix, gathered[member_slot])
        partials.append(product.reshape(columns, -1, product.shape[-1]))
    reduced = lax.psum_scatter(
        jnp.concatenate(partials, axis=1), "col", scatter_dimension=0, tiled=True
    )[0]
    results = []
    offset = 0
    for partial_in in partials:
        height = partial_in.shape[1]
        results.append(reduced[offset : offset + height])
        offset += height
    return (gathered, results)


def backward_products(grad_list, members, link_list):
    heights = [grad_piece.shape[0] for grad_piece in grad_list]
    everyone = lax.all_gather(jnp.concatenate(grad_list, axis=0)[None], "col", axis=0, tiled=True)
    columns = everyone.shape[0]
    gathered_grads = []
    offset = 0
    for height in heights:
        gathered_grads.append(everyone[:, offset : offset + height].reshape(columns * height, -1))
        offset += height
    input_parts = [None for member in members]
    weight_grads = []
    for grad_slot, member_slot, weight in link_list:
        matrix = weight.reshape(-1, weight.shape[-1])
        product = jnp.dot(matrix, gathered_grads[grad_slot], preferred_element_type=jnp.float32)
        if input_parts[member_slot] is None:
            input_parts[member_slot] = product
        else:
            input_parts[member_slot] = input_parts[member_slot] + product
        weight_grads.append(
            contract_last(members[member_slot], gathered_grads[grad_slot]).reshape(weight.shape)
        )
    row_devices = lax.axis_size("row")
    stacked = jnp.concatenate(
        [partial_in.reshape(row_devices, -1, partial_in.shape[-1]) for partial_in in input_parts],
        axis=1,
    )
    reduced = lax.psum_scatter(stacked, "row", scatter_dimension=0, tiled=True)[0]
    results = []
    offset = 0
    for member in members:
        height = member.shape[0] // row_devices
        results.append(reduced[offset : offset + height])
        offset += height
    return (results, weight_grads)


def attend_block(query_blk, key_blk, value_blk, causal, score_scale):
    scores = jnp.where(causal, contract_first(query_blk, key_blk) * score_scale, NEGATIVE)
    top_score = jnp.max(scores, axis=1, keepdims=True)
    exponent = jnp.exp(scores - top_score)
    row_total = jnp.sum(exponent, axis=1, keepdims=True)
    prob_rows = (exponent / row_total).astype(jnp.bfloat16)
    return (contract_last(value_blk, prob_rows), (top_score + jnp.log(row_total))[:, 0])


def attend_back(query_blk, key_blk, value_blk, grad_blk, logsum, causal, score_scale):
    scores = jnp.where(causal, contract_first(query_blk, key_blk) * score_scale, NEGATIVE)
    prob_rows = jnp.exp(scores - logsum[:, None])
    prob_grad = contract_first(grad_blk, value_blk)
    row_dot = jnp.sum(prob_rows * prob_grad, axis=1, keepdims=True)
    score_grad = (prob_rows * (prob_grad - row_dot)).astype(jnp.bfloat16)
    query_grad = contract_last(key_blk, score_grad) * score_scale
    key_grad = jnp.dot(query_blk, score_grad, preferred_element_type=jnp.float32) * score_scale
    value_grad = jnp.dot(
        grad_blk, prob_rows.astype(jnp.bfloat16), preferred_element_type=jnp.float32
    )
    return (query_grad, key_grad, value_grad)


def shards(
    layer_input,
    teacher,
    block_len,
    block_first,
    norm_gain,
    norm_bias,
    ema_rate,
    ema_angle,
    ema_input,
    ema_out_real,
    ema_out_imag,
    ema_skip,
    w_value,
    w_shared,
    w_reset,
    w_hidden,
    w_update,
    query_gain,
    query_bias,
    key_gain,
    w_output,
    final_gain,
    final_bias,
    w_gate,
    w_up,
    w_down,
):
    slot_count = layer_input.shape[1]
    blocks_here = slot_count // SPAN
    piece_len = min(128, SPAN)
    per_block = SPAN // piece_len
    position = jnp.arange(slot_count)
    valid_mask = (position % SPAN < jnp.repeat(block_len, SPAN)).astype(jnp.float32)
    first_flags = block_first.astype(jnp.float32)
    piece_resets = jnp.repeat(first_flags, per_block) * (
        jnp.arange(slot_count // piece_len) % per_block == 0
    )
    front_out, front_pull = jax.vjp(
        partial(front_piece, first_flags, piece_resets),
        layer_input,
        norm_gain,
        norm_bias,
        ema_rate,
        ema_angle,
        ema_input,
        ema_out_real,
        ema_out_imag,
        ema_skip,
    )
    normed, mixed_act = front_out
    sources = jnp.stack([normed, mixed_act]).astype(jnp.bfloat16)
    gathered_front, front_results = forward_products(
        sources, [(0, w_value), (1, w_shared), (1, w_reset), (1, w_hidden), (1, w_update)]
    )
    value_pre, shared, reset_pre, hidden_pre, update_pre = front_results
    prep_out, prep_pull = jax.vjp(prepare, value_pre, shared, query_gain, query_bias, key_gain)
    values_act, queries, keys_act = prep_out
    values_low = values_act.astype(jnp.bfloat16)
    gathered_qk = lax.all_gather(
        jnp.stack([queries, keys_act]).astype(jnp.bfloat16), ("row", "col"), axis=1, tiled=True
    )
    query_all = gathered_qk[0]
    key_all = gathered_qk[1]
    score_scale = Z ** (-0.5)
    causal = jnp.arange(SPAN)[:, None] >= jnp.arange(SPAN)[None, :]
    attended_parts = []
    logsums = []
    for block_id in range(blocks_here):
        window = slice(block_id * SPAN, (block_id + 1) * SPAN)
        block_out, block_lse = attend_block(
            query_all[:, window], key_all[:, window], values_low[:, window], causal, score_scale
        )
        attended_parts.append(block_out)
        logsums.append(block_lse)
    attended = jnp.concatenate(attended_parts, axis=1)
    reset_act = jax.nn.silu(reset_pre)
    att_in = (attended * reset_act).astype(jnp.bfloat16)
    gathered_att, output_results = forward_products(att_in[None], [(0, w_output)])
    summed = hidden_pre + output_results[0]
    hidden_act = jax.nn.silu(summed)
    gate_act = jax.nn.sigmoid(update_pre)
    first_out = layer_input + gate_act * (hidden_act - layer_input)
    norm_stats = lax.psum(
        (jnp.sum(first_out, axis=0), jnp.sum(first_out * first_out, axis=0)), ("row", "col")
    )
    mean_val = norm_stats[0] / D
    inv_std = lax.rsqrt(norm_stats[1] / D - mean_val * mean_val + EPSILON)
    unit_norm = (first_out - mean_val) * inv_std
    final_norm = unit_norm * final_gain[:, None] + final_bias[:, None]
    gathered_norm, ffn_results = forward_products(
        final_norm.astype(jnp.bfloat16)[None], [(0, w_gate), (0, w_up)]
    )
    norm_source = gathered_norm[0]
    gate_pre, up_pre = ffn_results
    inner_act = jax.nn.silu(gate_pre) * up_pre
    gathered_inner, down_results = forward_products(
        inner_act.astype(jnp.bfloat16)[None], [(0, w_down)]
    )
    layer_output = first_out + down_results[0]
    out_error = (layer_output - teacher) * valid_mask
    loss_parts = lax.psum(
        (jnp.sum(out_error * out_error), jnp.sum(valid_mask)), ("dp", "row", "col")
    )
    valid_total = loss_parts[1] / (lax.axis_size("row") * lax.axis_size("col"))
    loss_value = loss_parts[0] / (2.0 * valid_total * D)
    out_grad = out_error * (slot_count * lax.axis_size("dp") / valid_total)
    inner_parts, down_grads = backward_products(
        [out_grad.astype(jnp.bfloat16)], [gathered_inner[0]], [(0, 0, w_down)]
    )
    inner_grad = inner_parts[0]
    gate_grad = (inner_grad * up_pre * silu_slope(gate_pre)).astype(jnp.bfloat16)
    up_grad = (inner_grad * jax.nn.silu(gate_pre)).astype(jnp.bfloat16)
    norm_parts, ffn_grads = backward_products(
        [gate_grad, up_grad], [norm_source], [(0, 0, w_gate), (1, 0, w_up)]
    )
    norm_grad = norm_parts[0]
    final_gain_grad = jnp.sum(norm_grad * unit_norm, axis=1)
    final_bias_grad = jnp.sum(norm_grad, axis=1)
    unit_grad = norm_grad * final_gain[:, None]
    back_stats = (
        lax.psum(jnp.sum(unit_grad, axis=0).astype(jnp.bfloat16), ("row", "col")).astype(
            jnp.float32
        ),
        lax.psum(
            jnp.sum(unit_grad * unit_norm, axis=0).astype(jnp.bfloat16), ("row", "col")
        ).astype(jnp.float32),
    )
    first_grad = out_grad + inv_std * (
        unit_grad - back_stats[0] / D - unit_norm * back_stats[1] / D
    )
    ffn_sums = (down_grads[0], ffn_grads[0], ffn_grads[1], final_gain_grad, final_bias_grad)
    residual_grad = first_grad * (1.0 - gate_act)
    update_grad = (first_grad * (hidden_act - layer_input) * gate_act * (1.0 - gate_act)).astype(
        jnp.bfloat16
    )
    summed_grad = (first_grad * gate_act * silu_slope(summed)).astype(jnp.bfloat16)
    mix_parts, mixer_grads = backward_products(
        [summed_grad], [gathered_att[0], gathered_front[1]], [(0, 0, w_output), (0, 1, w_hidden)]
    )
    att_grad = mix_parts[0]
    mixed_grad_one = mix_parts[1]
    attended_grad = (att_grad * reset_act).astype(jnp.bfloat16)
    reset_grad = (att_grad * attended * silu_slope(reset_pre)).astype(jnp.bfloat16)
    query_parts = []
    key_parts = []
    value_parts = []
    for block_id in range(blocks_here):
        window = slice(block_id * SPAN, (block_id + 1) * SPAN)
        query_grad, key_grad, value_grad = attend_back(
            query_all[:, window],
            key_all[:, window],
            values_low[:, window],
            attended_grad[:, window],
            logsums[block_id],
            causal,
            score_scale,
        )
        query_parts.append(query_grad)
        key_parts.append(key_grad)
        value_parts.append(value_grad)
    qk_grads = lax.psum_scatter(
        jnp.stack(
            [jnp.concatenate(query_parts, axis=1), jnp.concatenate(key_parts, axis=1)]
        ).astype(jnp.bfloat16),
        ("row", "col"),
        scatter_dimension=1,
        tiled=True,
    ).astype(jnp.float32)
    prep_grads = prep_pull((jnp.concatenate(value_parts, axis=1), qk_grads[0], qk_grads[1]))
    value_pre_grad, shared_grad, query_gain_grad, query_bias_grad, key_gain_grad = prep_grads
    mixer_sums = (mixer_grads[0], mixer_grads[1], query_gain_grad, query_bias_grad, key_gain_grad)
    front_parts, front_grads = backward_products(
        [
            value_pre_grad.astype(jnp.bfloat16),
            shared_grad.astype(jnp.bfloat16),
            reset_grad,
            update_grad,
        ],
        [gathered_front[0], gathered_front[1]],
        [(0, 0, w_value), (1, 1, w_shared), (2, 1, w_reset), (3, 1, w_update)],
    )
    input_pulls = front_pull((front_parts[0], front_parts[1] + mixed_grad_one))
    input_grad = residual_grad + input_pulls[0]
    final_sums = (
        lax.psum(ffn_sums[0].astype(jnp.bfloat16), "dp").astype(jnp.float32),
        lax.psum(ffn_sums[1].astype(jnp.bfloat16), "dp").astype(jnp.float32),
        lax.psum(ffn_sums[2].astype(jnp.bfloat16), "dp").astype(jnp.float32),
        lax.psum(ffn_sums[3].astype(jnp.bfloat16), "dp").astype(jnp.float32),
        lax.psum(ffn_sums[4].astype(jnp.bfloat16), "dp").astype(jnp.float32),
        lax.psum(mixer_sums[0].astype(jnp.bfloat16), "dp").astype(jnp.float32),
        lax.psum(mixer_sums[1].astype(jnp.bfloat16), "dp").astype(jnp.float32),
        lax.psum(mixer_sums[2].astype(jnp.bfloat16), "dp").astype(jnp.float32),
        lax.psum(mixer_sums[3].astype(jnp.bfloat16), "dp").astype(jnp.float32),
        lax.psum(mixer_sums[4].astype(jnp.bfloat16), "dp").astype(jnp.float32),
        lax.psum(front_grads[0].astype(jnp.bfloat16), "dp").astype(jnp.float32),
        lax.psum(front_grads[1].astype(jnp.bfloat16), "dp").astype(jnp.float32),
        lax.psum(front_grads[2].astype(jnp.bfloat16), "dp").astype(jnp.float32),
        lax.psum(front_grads[3].astype(jnp.bfloat16), "dp").astype(jnp.float32),
        lax.psum(input_pulls[1].astype(jnp.bfloat16), "dp").astype(jnp.float32),
        lax.psum(input_pulls[2].astype(jnp.bfloat16), "dp").astype(jnp.float32),
        lax.psum(input_pulls[3].astype(jnp.bfloat16), "dp").astype(jnp.float32),
        lax.psum(input_pulls[4].astype(jnp.bfloat16), "dp").astype(jnp.float32),
        lax.psum(input_pulls[5].astype(jnp.bfloat16), "dp").astype(jnp.float32),
        lax.psum(input_pulls[6].astype(jnp.bfloat16), "dp").astype(jnp.float32),
        lax.psum(input_pulls[7].astype(jnp.bfloat16), "dp").astype(jnp.float32),
        lax.psum(input_pulls[8].astype(jnp.bfloat16), "dp").astype(jnp.float32),
    )
    return (
        layer_output,
        loss_value,
        input_grad,
        final_sums[14],
        final_sums[15],
        final_sums[16],
        final_sums[17],
        final_sums[18],
        final_sums[19],
        final_sums[20],
        final_sums[21],
        final_sums[10],
        final_sums[11],
        final_sums[12],
        final_sums[6],
        final_sums[13],
        final_sums[7],
        final_sums[8],
        final_sums[9],
        final_sums[5],
        final_sums[3],
        final_sums[4],
        final_sums[1],
        final_sums[2],
        final_sums[0],
    )


def solution(mesh):
    in_specs = (
        P(("row", "col"), "dp"),
        P(("row", "col"), "dp"),
        P("dp"),
        P("dp"),
        P(("row", "col")),
        P(("row", "col")),
        P(("row", "col"), None),
        P(("row", "col"), None),
        P(("row", "col"), None),
        P(("row", "col"), None),
        P(("row", "col"), None),
        P(("row", "col")),
        P(None, "col", None, "row"),
        P(None, "col", None, "row"),
        P(None, "col", None, "row"),
        P(None, "col", None, "row"),
        P(None, "col", None, "row"),
        P(("row", "col")),
        P(("row", "col")),
        P(("row", "col")),
        P(None, "col", None, "row"),
        P(("row", "col")),
        P(("row", "col")),
        P(None, "col", None, "row"),
        P(None, "col", None, "row"),
        P(None, "col", None, "row"),
    )
    out_specs = (
        P(("row", "col"), "dp"),
        P(),
        P(("row", "col"), "dp"),
        P(("row", "col")),
        P(("row", "col")),
        P(("row", "col"), None),
        P(("row", "col"), None),
        P(("row", "col"), None),
        P(("row", "col"), None),
        P(("row", "col"), None),
        P(("row", "col")),
        P(None, "col", None, "row"),
        P(None, "col", None, "row"),
        P(None, "col", None, "row"),
        P(None, "col", None, "row"),
        P(None, "col", None, "row"),
        P(("row", "col")),
        P(("row", "col")),
        P(("row", "col")),
        P(None, "col", None, "row"),
        P(("row", "col")),
        P(("row", "col")),
        P(None, "col", None, "row"),
        P(None, "col", None, "row"),
        P(None, "col", None, "row"),
    )
    return jax.shard_map(shards, mesh=mesh, in_specs=in_specs, out_specs=out_specs, check_vma=False)
```

profile of v0, /device:TPU:0, one launch (start us, length us, event | category | flops | bytes accessed | tf_op | source)
XLA Modules:
  0.0 3267.8 jit_solution(358749562177663341)
XLA Ops:
  36.2 10.4 fusion.94
  65.4 8.6 slice.508
  92.5 8.8 slice.516
  241.2 65.2 %gather_fusion = f32[16384,128]{1,0:T(8,128)} fusion(f32[128,128]{0,1:T(8,128)S(1)} %bitcast.593, s32[16384]{0:T(1024)S(1)} %copy-done.155), kind=kCustom, calls=%fused_computation | custom fusion | bytes 16842752 | tf_op jit(solution)/shard_map/jvp()/gather | solution.py:79
  306.4 9.9 select_bitcast_fusion
  316.3 9.3 copy.369
  325.6 15.5 fusion.234
  349.6 59.6 %all-gather.15.cloned.1.call-done = bf16[2,256,4096]{2,1,0:T(8,128)(2,1)} async-done(((bf16[2,128,4096]{2,1,0:T(8,128)(2,1)}), bf16[2,256,4096]{2,1,0:T(8,128)(2,1)}) %all-gather.15.cloned.1.call-update) | async-done | bytes 4194320 | tf_op jit(solution)/shard_map/all_gather | solution.py:142
  440.6 356.9 %reduce-scatter.10.cloned.1.call-done = f32[1,800,4096]{2,1,0:T(8,128)} async-done(((f32[4,800,4096]{2,1,0:T(8,128)}), f32[1,800,4096]{2,1,0:T(8,128)}) %reduce-scatter.10.cloned.1.call-update) | async-done | bytes 13107216 | tf_op jit(solution)/shard_map/reduce_scatter | solution.py:149
  802.9 34.0 %all-gather.17.cloned.1.call-done = bf16[2,256,4096]{2,1,0:T(8,128)(2,1)} async-done(((bf16[2,32,4096]{2,1,0:T(8,128)(2,1)}), bf16[2,256,4096]{2,1,0:T(8,128)(2,1)}) %all-gather.17.cloned.1.call-update) | async-done | bytes 4194320 | tf_op jit(solution)/shard_map/all_gather | solution.py:279
  870.9 8.8 fusion.11
  892.5 56.8 %all-gather.19.cloned.1.call-done = bf16[1,512,4096]{2,1,0:T(8,128)(2,1)} async-done(((bf16[1,256,4096]{2,1,0:T(8,128)(2,1)}), bf16[1,512,4096]{2,1,0:T(8,128)(2,1)}) %all-gather.19.cloned.1.call-update) | async-done | bytes 4194320 | tf_op jit(solution)/shard_map/all_gather | solution.py:142
  957.4 71.8 %reduce-scatter.12.cloned.1.call-done = f32[1,128,4096]{2,1,0:T(8,128)} async-done(((f32[4,128,4096]{2,1,0:T(8,128)}), f32[1,128,4096]{2,1,0:T(8,128)}) %reduce-scatter.12.cloned.1.call-update) | async-done | bytes 2097168 | tf_op jit(solution)/shard_map/reduce_scatter | solution.py:149
  1034.7 23.1 all-reduce.104
  1060.8 32.5 all-gather.23.cloned.1.call-done
  1093.3 10.5 fusion.235
  1103.8 8.6 fusion.236
  1112.4 28.3 pad_maximum_fusion
  1140.8 288.9 %reduce-scatter.14.cloned.1.call-done = f32[1,640,4096]{2,1,0:T(8,128)} async-done(((f32[4,640,4096]{2,1,0:T(8,128)}), f32[1,640,4096]{2,1,0:T(8,128)}) %reduce-scatter.14.cloned.1.call-update) | async-done | bytes 10485776 | tf_op jit(solution)/shard_map/reduce_scatter | solution.py:149
  1435.8 68.5 %all-gather.21.cloned.1.call-done = bf16[1,640,4096]{2,1,0:T(8,128)(2,1)} async-done(((bf16[1,320,4096]{2,1,0:T(8,128)(2,1)}), bf16[1,640,4096]{2,1,0:T(8,128)(2,1)}) %all-gather.21.cloned.1.call-update) | async-done | bytes 5242896 | tf_op jit(solution)/shard_map/all_gather | solution.py:142
  1504.3 9.4 fusion.31
  1515.1 70.5 %reduce-scatter.16.cloned.1.call-done = f32[1,128,4096]{2,1,0:T(8,128)} async-done(((f32[4,128,4096]{2,1,0:T(8,128)}), f32[1,128,4096]{2,1,0:T(8,128)}) %reduce-scatter.16.cloned.1.call-update) | async-done | bytes 2097168 | tf_op jit(solution)/shard_map/reduce_scatter | solution.py:149
  1590.9 39.6 %all-reduce.103 = (f32[]{:T(128)}, f32[]{:T(128)}) all-reduce(f32[]{:T(128)} %fusion.191, f32[]{:T(128)} %get-tuple-element.732), channel_id=1, replica_groups=mesh['dp'=4,'row'=2,'col'=4] {'dp','row','col'}, use_global_device_ids=true, to_apply=%region_29.30 | all-reduce | flops 2 | bytes 16 | tf_op jit(solution)/shard_map/psum | solution.py:321
  1634.8 35.5 %all-gather.25.cloned.1.call-done = bf16[512,4096]{1,0:T(8,128)(2,1)} async-done(((bf16[128,4096]{1,0:T(8,128)(2,1)}), bf16[512,4096]{1,0:T(8,128)(2,1)}) %all-gather.25.cloned.1.call-update) | async-done | bytes 4194320 | tf_op jit(solution)/shard_map/all_gather | solution.py:163
  1670.3 9.2 fusion.237
  1679.5 122.0 %reduce-scatter.18.cloned.1.call-done = f32[1,320,4096]{2,1,0:T(8,128)} async-done(((f32[2,320,4096]{2,1,0:T(8,128)}), f32[1,320,4096]{2,1,0:T(8,128)}) %reduce-scatter.18.cloned.1.call-update) | async-done | bytes 5242896 | tf_op jit(solution)/shard_map/reduce_scatter | solution.py:187
  1811.8 131.3 %all-gather.27.cloned.1.call-done = bf16[2560,4096]{1,0:T(8,128)(2,1)} async-done(((bf16[640,4096]{1,0:T(8,128)(2,1)}), bf16[2560,4096]{1,0:T(8,128)(2,1)}) %all-gather.27.cloned.1.call-update) | async-done | bytes 20971536 | tf_op jit(solution)/shard_map/all_gather | solution.py:163
  1962.8 54.4 %reduce-scatter.20.cloned.1.call-done = f32[1,128,4096]{2,1,0:T(8,128)} async-done(((f32[2,128,4096]{2,1,0:T(8,128)}), f32[1,128,4096]{2,1,0:T(8,128)}) %reduce-scatter.20.cloned.1.call-update) | async-done | bytes 2097168 | tf_op jit(solution)/shard_map/reduce_scatter | solution.py:187
  2020.7 23.1 all-reduce.105
  2057.2 34.6 %all-gather.29.cloned.1.call-done = bf16[512,4096]{1,0:T(8,128)(2,1)} async-done(((bf16[128,4096]{1,0:T(8,128)(2,1)}), bf16[512,4096]{1,0:T(8,128)(2,1)}) %all-gather.29.cloned.1.call-update) | async-done | bytes 4194320 | tf_op jit(solution)/shard_map/all_gather | solution.py:163
  2104.7 143.9 %reduce-scatter.22.cloned.1.call-done = f32[1,384,4096]{2,1,0:T(8,128)} async-done(((f32[2,384,4096]{2,1,0:T(8,128)}), f32[1,384,4096]{2,1,0:T(8,128)}) %reduce-scatter.22.cloned.1.call-update) | async-done | bytes 6291472 | tf_op jit(solution)/shard_map/reduce_scatter | solution.py:187
  2255.0 15.9 multiply_reduce_fusion.1
  2293.6 11.0 multiply_reduce_fusion
  2304.6 8.7 multiply_convert_fusion
  2349.3 31.0 reduce-scatter.24.cloned.1.call-done
  2396.9 8.6 fusion.109
  2409.9 9.0 fusion.58
  2424.3 105.9 %all-gather.31.cloned.1.call-done = bf16[2688,4096]{1,0:T(8,128)(2,1)} async-done(((bf16[672,4096]{1,0:T(8,128)(2,1)}), bf16[2688,4096]{1,0:T(8,128)(2,1)}) %all-gather.31.cloned.1.call-update) | async-done | bytes 22020112 | tf_op jit(solution)/shard_map/all_gather | solution.py:163
  2580.5 132.8 %all-reduce.110.cloned.1.call-done = (bf16[2,1,128,1024]{3,2,0,1:T(8,128)(2,1)}, bf16[2,1,128,128]{3,2,0,1:T(8,128)(2,1)}, bf16[2,1,128,1024]{3,2,0,1:T(8,128)(2...) async-done(((bf16[2,1,128,1024]{3,2,0,1:T(8,128)(2,1)}, ...) | async-done | bytes 4128784 | tf_op jit(solution)/shard_map/psum | solution.py:415
  2725.3 88.4 %reduce-scatter.26.cloned.1.call-done = f32[1,256,4096]{2,1,0:T(8,128)} async-done(((f32[2,256,4096]{2,1,0:T(8,128)}), f32[1,256,4096]{2,1,0:T(8,128)}) %reduce-scatter.26.cloned.1.call-update) | async-done | bytes 4194320 | tf_op jit(solution)/shard_map/reduce_scatter | solution.py:187
  2851.6 15.8 select_bitcast_fusion.1
  3040.4 9.4 copy.419
  3049.7 98.3 %scatter_custom_fusion = f32[128,128]{0,1:T(8,128)S(1)} fusion(s32[16384]{0:T(1024)} %maximum_bitcast_fusion.2, f32[16384,128]{1,0:T(8,128)} %bitcast.646, f32[]{:T(128)} %constant.203.clone.1), kind=kCustom, calls=%fused_computation.404 | custom fusion | flops 2097152 | bytes 66048 | tf_op jit(solution)/shard_map/transpose(jvp())/scatter-add | solution.py:79
  3165.5 14.9 multiply_reduce_fusion.3
  3180.9 10.9 add_add_fusion.1
  3195.0 20.9 all-reduce.106
  3229.3 9.9 reduce-window.40
  3243.7 9.9 reduce-window.44
  (952 shorter events, 809.8 us)
Async XLA Ops:
  7.2 1086.1 %copy-start = (bf16[2,1,128,1280]{3,2,1,0:T(8,128)(2,1)S(1)}, bf16[2,1,128,1280]{3,2,1,0:T(8,128)(2,1)}, u32[]{:S(2)}) copy-start(bf16[2,1,128,1280]{3,2,1,0:T(8,128)(2,1)} %param.59) | copy-start | bytes 1966084
  7.2 401.9 %all-gather.15.cloned.1.call-start = ((), (), s32[]{:S(2)}) async-start(), calls=%async_computation.9 | async-start | bytes 6291456 | tf_op jit(solution)/shard_map/all_gather | solution.py:142
  35.8 289.8 %copy-start.5 = (f32[16,8,32,128]{3,2,1,0:T(8,128)}, f32[16,8,32,128]{3,2,1,0:T(8,128)S(1)}, u32[]{:S(2)}) copy-start(f32[16,8,32,128]{3,2,1,0:T(8,128)S(1)} %copy.443) | copy-start | bytes 6291460
  35.9 305.3 %copy-start.87 = (f32[128,16]{1,0:T(8,128)}, f32[128,16]{1,0:T(8,128)S(1)}, u32[]{:S(2)}) copy-start(f32[128,16]{1,0:T(8,128)S(1)} %copy.364) | copy-start | bytes 24580
  51.3 179.6 %copy-start.61 = (f32[128,16]{1,0:T(8,128)}, f32[128,16]{1,0:T(8,128)S(1)}, u32[]{:S(2)}) copy-start(f32[128,16]{1,0:T(8,128)S(1)} %copy.363) | copy-start | bytes 24580
  117.5 100.6 %copy-start.57 = (f32[128,32,16]{0,2,1:T(8,128)}, f32[128,32,16]{0,2,1:T(8,128)S(1)}, u32[]{:S(2)}) copy-start(f32[128,32,16]{0,2,1:T(8,128)S(1)} %get-tuple-element.903) | copy-start | bytes 786436
  117.5 100.6 %copy-start.59 = (f32[128,32,16]{0,2,1:T(8,128)}, f32[128,32,16]{0,2,1:T(8,128)S(1)}, u32[]{:S(2)}) copy-start(f32[128,32,16]{0,2,1:T(8,128)S(1)} %get-tuple-element.904) | copy-start | bytes 786436
  119.1 71.3 %copy-start.69 = (f32[128,16,16]{0,2,1:T(8,128)}, f32[128,16,16]{0,2,1:T(8,128)S(1)}, u32[]{:S(2)}) copy-start(f32[128,16,16]{0,2,1:T(8,128)S(1)} %get-tuple-element.798) | copy-start | bytes 393220
  175.6 130.7 %copy-start.160 = (pred[128,128]{1,0:T(8,128)(4,1)}, pred[128,128]{1,0:T(8,128)(4,1)S(1)}, u32[]{:S(2)}) copy-start(pred[128,128]{1,0:T(8,128)(4,1)S(1)} %subtract_compare_fusion) | copy-start | bytes 49156
  349.5 59.6 %copy-start.130 = (bf16[2,1,128,1024]{3,2,1,0:T(8,128)(2,1)S(1)}, bf16[2,1,128,1024]{3,2,1,0:T(8,128)(2,1)}, u32[]{:S(2)}) copy-start(bf16[2,1,128,1024]{3,2,1,0:T(8,128)(2,1)} %param.48) | copy-start | bytes 1572868
  349.5 448.0 %reduce-scatter.10.cloned.1.call-start = ((), (), s32[]{:S(2)}) async-start(), calls=%async_computation.10 | async-start | bytes 65536000 | tf_op jit(solution)/shard_map/reduce_scatter | solution.py:149
  440.5 357.0 %copy-start.206 = (f32[32]{0:T(128)S(1)}, f32[32]{0:T(128)}, u32[]{:S(2)}) copy-start(f32[32]{0:T(128)} %param.53) | copy-start | bytes 388
  440.5 357.0 %copy-start.208 = (f32[32]{0:T(128)S(1)}, f32[32]{0:T(128)}, u32[]{:S(2)}) copy-start(f32[32]{0:T(128)} %param.55) | copy-start | bytes 388
  440.5 357.0 %copy-start.217 = (f32[32]{0:T(128)S(1)}, f32[32]{0:T(128)}, u32[]{:S(2)}) copy-start(f32[32]{0:T(128)} %param.54) | copy-start | bytes 388
  440.5 396.4 %all-gather.17.cloned.1.call-start = ((), (), s32[]{:S(2)}) async-start(), calls=%async_computation.11 | async-start | bytes 4718592 | tf_op jit(solution)/shard_map/all_gather | solution.py:279
  799.6 149.8 %all-gather.19.cloned.1.call-start = ((), (), s32[]{:S(2)}) async-start(), calls=%async_computation.12 | async-start | bytes 6291456 | tf_op jit(solution)/shard_map/all_gather | solution.py:142
  802.9 76.8 %copy-start.45 = (bf16[256,4096]{1,0:T(8,128)(2,1)}, bf16[256,4096]{1,0:T(8,128)(2,1)S(1)}, u32[]{:S(2)}) copy-start(bf16[256,4096]{1,0:T(8,128)(2,1)S(1)} %multiply_convert_fusion.3) | copy-start | bytes 6291460
  892.4 56.9 %copy-start.74 = (bf16[2,1,256,512]{3,2,1,0:T(8,128)(2,1)S(1)}, bf16[2,1,256,512]{3,2,1,0:T(8,128)(2,1)}, u32[]{:S(2)}) copy-start(bf16[2,1,256,512]{3,2,1,0:T(8,128)(2,1)} %param.56) | copy-start | bytes 1572868
  892.4 136.8 %reduce-scatter.12.cloned.1.call-start = ((), (), s32[]{:S(2)}) async-start(), calls=%async_computation.13 | async-start | bytes 10485760 | tf_op jit(solution)/shard_map/reduce_scatter | solution.py:149
  957.3 71.9 %copy-start.3 = (f32[128,4096]{1,0:T(8,128)S(1)}, f32[128,4096]{1,0:T(8,128)}, u32[]{:S(2)}) copy-start(f32[128,4096]{1,0:T(8,128)} %param.36) | copy-start | bytes 6291460
  957.3 100.5 %copy-start.200 = (f32[128]{0:T(128)S(1)}, f32[128]{0:T(128)}, u32[]{:S(2)}) copy-start(f32[128]{0:T(128)} %param.57) | copy-start | bytes 1540
  957.3 100.5 %copy-start.218 = (f32[128]{0:T(128)S(1)}, f32[128]{0:T(128)}, u32[]{:S(2)}) copy-start(f32[128]{0:T(128)} %param.58) | copy-start | bytes 1540
  957.3 136.0 %all-gather.23.cloned.1.call-start = ((), (), s32[]{:S(2)}) async-start(), calls=%async_computation.22 | async-start | bytes 3145728 | tf_op jit(solution)/shard_map/all_gather | solution.py:142
  1060.7 368.9 %reduce-scatter.14.cloned.1.call-start = ((), (), s32[]{:S(2)}) async-start(), calls=%async_computation.14 | async-start | bytes 52428800 | tf_op jit(solution)/shard_map/reduce_scatter | solution.py:149
  1140.7 363.5 %all-gather.21.cloned.1.call-start = ((), (), s32[]{:S(2)}) async-start(), calls=%async_computation.15 | async-start | bytes 7864320 | tf_op jit(solution)/shard_map/all_gather | solution.py:142
  1435.5 150.0 %reduce-scatter.16.cloned.1.call-start = ((), (), s32[]{:S(2)}) async-start(), calls=%async_computation.16 | async-start | bytes 10485760 | tf_op jit(solution)/shard_map/reduce_scatter | solution.py:149
  1513.7 156.6 %all-gather.25.cloned.1.call-start = ((), (), s32[]{:S(2)}) async-start(), calls=%async_computation.23 | async-start | bytes 5242880 | tf_op jit(solution)/shard_map/all_gather | solution.py:163
  1634.7 166.8 %reduce-scatter.18.cloned.1.call-start = ((), (), s32[]{:S(2)}) async-start(), calls=%async_computation.17 | async-start | bytes 15728640 | tf_op jit(solution)/shard_map/reduce_scatter | solution.py:187
  1679.5 263.6 %all-gather.27.cloned.1.call-start = ((), (), s32[]{:S(2)}) async-start(), calls=%async_computation.24 | async-start | bytes 26214400 | tf_op jit(solution)/shard_map/all_gather | solution.py:163
  1811.3 205.9 %reduce-scatter.20.cloned.1.call-start = ((), (), s32[]{:S(2)}) async-start(), calls=%async_computation.18 | async-start | bytes 6291456 | tf_op jit(solution)/shard_map/reduce_scatter | solution.py:187
  1962.8 129.0 %all-gather.29.cloned.1.call-start = ((), (), s32[]{:S(2)}) async-start(), calls=%async_computation.25 | async-start | bytes 5242880 | tf_op jit(solution)/shard_map/all_gather | solution.py:163
  2057.2 191.4 %reduce-scatter.22.cloned.1.call-start = ((), (), s32[]{:S(2)}) async-start(), calls=%async_computation.19 | async-start | bytes 18874368 | tf_op jit(solution)/shard_map/reduce_scatter | solution.py:187
  2103.9 144.7 %copy-start.52 = (f32[256,2048]{1,0:T(8,128)S(1)}, f32[256,2048]{1,0:T(8,128)}, u32[]{:S(2)}) copy-start(f32[256,2048]{1,0:T(8,128)} %copy-done.51) | copy-start | bytes 6291460
  2104.0 276.3 %reduce-scatter.24.cloned.1.call-start = ((), (), s32[]{:S(2)}) async-start(), calls=%async_computation.20 | async-start | bytes 4718592 | tf_op jit(solution)/shard_map/reduce_scatter | solution.py:381
  2328.8 201.4 %all-gather.31.cloned.1.call-start = ((), (), s32[]{:S(2)}) async-start(), calls=%async_computation.26 | async-start | bytes 27525120 | tf_op jit(solution)/shard_map/all_gather | solution.py:163
  2392.6 320.6 %all-reduce.110.cloned.1.call-start = ((), (), s32[]{:S(2)}) async-start(), calls=%async_computation.27 | async-start | bytes 8257536 | tf_op jit(solution)/shard_map/psum | solution.py:415
  2557.3 256.3 %reduce-scatter.26.cloned.1.call-start = ((), (), s32[]{:S(2)}) async-start(), calls=%async_computation.21 | async-start | bytes 12582912 | tf_op jit(solution)/shard_map/reduce_scatter | solution.py:187
  2723.0 90.7 %copy-start.13 = (f32[128,4096]{1,0:T(8,128)S(1)}, f32[128,4096]{1,0:T(8,128)}, u32[]{:S(2)}) copy-start(f32[128,4096]{1,0:T(8,128)} %copy-done.11) | copy-start | bytes 6291460
  2723.0 90.7 %copy-start.204 = (f32[128]{0:T(128)S(1)}, f32[128]{0:T(128)}, u32[]{:S(2)}) copy-start(f32[128]{0:T(128)} %param.47) | copy-start | bytes 1540
  2867.3 56.8 %copy-start.95 = (f32[128,16,16]{0,2,1:T(8,128)S(1)}, f32[128,16,16]{0,2,1:T(8,128)}, u32[]{:S(2)}) copy-start(f32[128,16,16]{0,2,1:T(8,128)} %copy-done.94) | copy-start | bytes 393220
  2867.3 56.8 %copy-start.97 = (f32[128,16,16]{0,2,1:T(8,128)S(1)}, f32[128,16,16]{0,2,1:T(8,128)}, u32[]{:S(2)}) copy-start(f32[128,16,16]{0,2,1:T(8,128)} %copy-done.96) | copy-start | bytes 393220
  2924.1 55.4 %copy-start.83 = (f32[128,16,16]{0,2,1:T(8,128)S(1)}, f32[128,16,16]{0,2,1:T(8,128)}, u32[]{:S(2)}) copy-start(f32[128,16,16]{0,2,1:T(8,128)} %copy.427) | copy-start | bytes 393220
  2924.1 55.4 %copy-start.84 = (f32[128,16,16]{0,2,1:T(8,128)S(1)}, f32[128,16,16]{0,2,1:T(8,128)}, u32[]{:S(2)}) copy-start(f32[128,16,16]{0,2,1:T(8,128)} %copy.428) | copy-start | bytes 393220
  2924.1 55.4 %slice-start.15 = ((f32[128,8,16]{0,2,1:T(8,128)}), f32[128,1,16]{0,2,1:T(8,128)S(1)}, s32[]{:S(2)}) async-start(f32[128,8,16]{0,2,1:T(8,128)} %copy-done.152), calls=%async_computation.43 | async-start | bytes 16384 | tf_op jit(solution)/shard_map/transpose(jvp())/split | solution.py:100
  2924.1 55.4 %slice-start.16 = ((f32[128,8,16]{0,2,1:T(8,128)}), f32[128,1,16]{0,2,1:T(8,128)S(1)}, s32[]{:S(2)}) async-start(f32[128,8,16]{0,2,1:T(8,128)} %copy-done.153), calls=%async_computation.44 | async-start | bytes 16384 | tf_op jit(solution)/shard_map/transpose(jvp())/split | solution.py:100
  3040.4 108.7 %copy-start.137 = (f32[128,16,16]{0,2,1:T(8,128)S(1)}, f32[128,16,16]{0,2,1:T(8,128)}, u32[]{:S(2)}) copy-start(f32[128,16,16]{0,2,1:T(8,128)} %get-tuple-element.790) | copy-start | bytes 393220
  3040.4 108.9 %copy-start.142 = (f32[128,15,16]{0,2,1:T(8,128)S(1)}, f32[128,15,16]{0,2,1:T(8,128)}, u32[]{:S(2)}) copy-start(f32[128,15,16]{0,2,1:T(8,128)} %get-tuple-element.824) | copy-start | bytes 368644
  3040.4 109.0 %slice-start.13 = ((f32[128,16,16]{0,2,1:T(8,128)}), f32[128,1,16]{0,2,1:T(8,128)S(1)}, s32[]{:S(2)}) async-start(f32[128,16,16]{0,2,1:T(8,128)} %copy-done.135), calls=%async_computation.41 | async-start | bytes 16384 | tf_op jit(solution)/shard_map/transpose(jvp())/split | solution.py:100
  (213 other events, 1660.2 us)
Sparse Core Ops, SparseCore 0:
  349.6 59.4 all-gather.14
  440.6 356.7 reduce-scatter.9
  800.1 36.7 all-gather.16
  892.5 56.7 all-gather.18
  957.4 71.7 reduce-scatter.11
  1060.9 32.4 all-gather.22
  1140.9 288.7 reduce-scatter.13
  1435.7 68.5 all-gather.20
  1513.8 71.7 reduce-scatter.15
  1634.8 35.4 all-gather.24
  1679.6 121.8 reduce-scatter.17
  1811.4 131.6 all-gather.26
  1962.9 54.3 reduce-scatter.19
  2057.3 34.4 all-gather.28
  2104.1 144.4 reduce-scatter.21
  2328.9 51.3 reduce-scatter.23
  2392.7 137.3 all-gather.30
  2557.4 155.7 all-reduce.109
  2715.6 97.9 reduce-scatter.25
where the time goes:
time: 3290 us; the launch traced here: 3270 us
  waiting for transfers between devices  1920 us (58%)
  local copies, waits for them, and re-layouts  487 us (15%)
  other arithmetic  420 us (13%)
  matrix products  309 us (9%)
  blocking collectives  107 us (3%)
    reduce_scatter x4, waiting for transfers between devices, forward_products(): lax.psum_scatter(jnp.concatenate(partials, axis=1), 'col', scatter_dimens...  788 us
    reduce_scatter x4, waiting for transfers between devices, backward_products(): lax.psum_scatter(stacked, 'row', scatter_dimension=0, tiled=True)[0]  409 us
    all_gather x4, waiting for transfers between devices, backward_products(): lax.all_gather(jnp.concatenate(grad_list, axis=0)[None], 'col', axis=0, t...  307 us
    all_gather x4, waiting for transfers between devices, forward_products(): gathered = lax.all_gather(sources, 'row', axis=1, tiled=True)  217 us
    pad x64, local copies, waits for them, and re-layouts, ema_blocks(): lax.associative_scan(combine, (step_re, step_im, ends_re, ends_im), axis=1)  178 us
    psum x1, waiting for transfers between devices, shards(): lax.psum(front_grads[0].astype(jnp.bfloat16), 'dp').astype(jnp.float32)  133 us
    scatter-add x1, other arithmetic, ema_blocks(): kernel.T[:, jnp.maximum(offsets, 0)]  98.3 us
    unnamed x516, local copies, waits for them, and re-layouts  92.8 us
  transfers between devices with their start and end apart: 19, of which 19 were waited for; matrix products, arithmetic and copies ran while one was open for 3% of the time, Pallas kernels for 0%

commit v1 on v0

v1 whole, which is shorter than its diff:
```python
from functools import partial

import jax
import jax.numpy as jnp
from jax import lax
from jax.sharding import PartitionSpec as P

D = 1024
Z = 256
SPAN = 2048
GS = 32


EPSILON = 1e-05
NEGATIVE = -1000000000.0
PRECISE = lax.Precision.HIGHEST


def running_sums(values, first_flags, block_rows):
    height = values.shape[0]
    blocked = values.reshape(height, -1, block_rows)
    inside = jnp.cumsum(blocked, axis=2)
    totals = inside[:, :, -1]

    def carry_step(carried, scan_item):
        block_total, reset_flag = scan_item
        begin_sum = carried * (1.0 - reset_flag)
        return (begin_sum + block_total, begin_sum)

    unused, starts = lax.scan(
        carry_step, jnp.zeros((height,), jnp.float32), (totals.T, first_flags)
    )
    return (inside + starts.T[:, :, None]).reshape(height, -1)


def step_norm(layer_in, norm_gain, norm_bias, first_flags):
    channels, length = layer_in.shape
    grouped = layer_in.reshape(channels // GS, GS, length)
    sum_one = running_sums(jnp.sum(grouped, axis=1), first_flags, SPAN)
    sum_two = running_sums(jnp.sum(grouped * grouped, axis=1), first_flags, SPAN)
    counted = running_sums(jnp.ones((1, length), jnp.float32), first_flags, SPAN) * GS
    mean_val = sum_one / counted
    var_val = sum_two / counted - mean_val * mean_val
    centred = (grouped - mean_val[:, None, :]) * lax.rsqrt(var_val + EPSILON)[:, None, :]
    return centred.reshape(channels, length) * norm_gain[:, None] + norm_bias[:, None]


def silu_slope(pre_act):
    logistic = jax.nn.sigmoid(pre_act)
    return logistic * (1.0 + pre_act * (1.0 - logistic))


def contract_first(left_in, right_in):
    return lax.dot_general(
        left_in, right_in, (((0,), (0,)), ((), ())), preferred_element_type=jnp.float32
    )


def contract_last(left_in, right_in):
    return lax.dot_general(
        left_in, right_in, (((1,), (1,)), ((), ())), preferred_element_type=jnp.float32
    )


def ema_blocks(normed, ema_rate, ema_angle, ema_input, ema_out_real, ema_out_imag, piece_resets):
    piece_len = min(128, SPAN)
    channels, slot_count = normed.shape
    decay_rate = 1.0 - ema_rate
    in_coeff = jnp.sqrt(2.0 * ema_rate) * ema_input
    powers = jnp.arange(piece_len + 1, dtype=jnp.float32)[:, None, None]
    magnitude = jnp.exp(powers * jnp.log(decay_rate)[None])
    phases = powers * ema_angle[None]
    power_re = magnitude * jnp.cos(phases)
    power_im = magnitude * jnp.sin(phases)
    mixed_re = ema_out_real[None] * power_re - ema_out_imag[None] * power_im
    mixed_im = ema_out_real[None] * power_im + ema_out_imag[None] * power_re
    kernel = jnp.sum(in_coeff[None] * mixed_re[:piece_len], axis=2)
    offsets = jnp.arange(piece_len)[:, None] - jnp.arange(piece_len)[None, :]
    toeplitz = jnp.where(offsets[None] >= 0, kernel.T[:, jnp.maximum(offsets, 0)], 0.0)
    pieces = normed.reshape(channels, -1, piece_len)
    inside = jnp.einsum("cts,cbs->cbt", toeplitz, pieces, precision=PRECISE)
    back_re = power_re[:piece_len][::-1] * in_coeff[None]
    back_im = power_im[:piece_len][::-1] * in_coeff[None]
    ends_re = jnp.einsum("scj,cbs->cbj", back_re, pieces, precision=PRECISE)
    ends_im = jnp.einsum("scj,cbs->cbj", back_im, pieces, precision=PRECISE)
    keeping = (1.0 - piece_resets)[None, :, None]
    step_re = keeping * power_re[piece_len][:, None, :]
    step_im = keeping * power_im[piece_len][:, None, :]

    def combine(earlier, following):
        head_mre, head_mim, head_are, head_aim = earlier
        tail_mre, tail_mim, tail_are, tail_aim = following
        return (
            tail_mre * head_mre - tail_mim * head_mim,
            tail_mre * head_mim + tail_mim * head_mre,
            tail_mre * head_are - tail_mim * head_aim + tail_are,
            tail_mre * head_aim + tail_mim * head_are + tail_aim,
        )

    scanned = lax.associative_scan(combine, (step_re, step_im, ends_re, ends_im), axis=1)
    state_re = (
        jnp.concatenate([jnp.zeros_like(ends_re[:, :1]), scanned[2][:, :-1]], axis=1) * keeping
    )
    state_im = (
        jnp.concatenate([jnp.zeros_like(ends_im[:, :1]), scanned[3][:, :-1]], axis=1) * keeping
    )
    across = jnp.einsum("tcj,cbj->cbt", mixed_re[1:], state_re, precision=PRECISE) - jnp.einsum(
        "tcj,cbj->cbt", mixed_im[1:], state_im, precision=PRECISE
    )
    return (inside + across).reshape(channels, slot_count)


def front_piece(
    first_flags,
    piece_resets,
    layer_in,
    norm_gain,
    norm_bias,
    ema_rate,
    ema_angle,
    ema_input,
    ema_out_real,
    ema_out_imag,
    ema_skip,
):
    normed = step_norm(layer_in, norm_gain, norm_bias, first_flags)
    smoothed = ema_blocks(
        normed, ema_rate, ema_angle, ema_input, ema_out_real, ema_out_imag, piece_resets
    )
    return (normed, jax.nn.silu(smoothed + ema_skip[:, None] * normed))


def silu(pre_act):
    return pre_act * jax.nn.sigmoid(pre_act)


def swap_blocks(array_in, outer, inner):
    shaped = array_in.reshape(outer, inner, -1, array_in.shape[-1])
    return shaped.transpose(1, 0, 2, 3).reshape(array_in.shape)


def project(weights, source):
    return jnp.concatenate(
        [contract_first(weights[part], source) for part in range(weights.shape[0])], axis=0
    )


def project_back(weights, grads):
    parts = weights.shape[0]
    pieces = grads.reshape(parts, -1, grads.shape[-1])
    total = None
    for part in range(parts):
        product = jnp.dot(weights[part], pieces[part], preferred_element_type=jnp.float32)
        total = product if total is None else total + product
    return total


def weight_products(source, grads, parts):
    pieces = grads.reshape(parts, -1, grads.shape[-1])
    return [contract_last(source, pieces[part]).astype(jnp.bfloat16) for part in range(parts)]


def shards(
    layer_input,
    teacher,
    block_len,
    block_first,
    norm_gain,
    norm_bias,
    ema_rate,
    ema_angle,
    ema_input,
    ema_out_real,
    ema_out_imag,
    ema_skip,
    w_value,
    w_shared,
    w_reset,
    w_hidden,
    w_update,
    query_gain,
    query_bias,
    key_gain,
    w_output,
    final_gain,
    final_bias,
    w_gate,
    w_up,
    w_down,
):
    bf16 = jnp.bfloat16
    grid = ("row", "col")
    rows, cols, dps = lax.axis_size("row"), lax.axis_size("col"), lax.axis_size("dp")
    devices = rows * cols
    slot_count = layer_input.shape[1]
    blocks_here = slot_count // SPAN
    group = devices // blocks_here
    tokens = slot_count // devices
    half = tokens // 2
    place = lax.axis_index("row") * cols + lax.axis_index("col")
    my_block = place // group
    member = place % group
    piece_len = min(128, SPAN)
    per_block = SPAN // piece_len
    first_flags = block_first.astype(jnp.float32)
    piece_resets = jnp.repeat(first_flags, per_block) * (
        jnp.arange(slot_count // piece_len) % per_block == 0
    )

    def deal(array_in):
        feats = array_in.shape[0]
        shaped = array_in.reshape(feats, blocks_here, 2, group, half)
        paired = jnp.stack([shaped[:, :, 0], shaped[:, :, 1, ::-1]], axis=3)
        return paired.reshape(feats, slot_count)

    def undeal(array_in):
        feats = array_in.shape[0]
        shaped = array_in.reshape(feats, blocks_here, group, 2, half)
        paired = jnp.stack([shaped[:, :, :, 0], shaped[:, :, ::-1, 1]], axis=2)
        return paired.reshape(feats, slot_count)

    def to_slots(array_in):
        return lax.all_to_all(deal(array_in), grid, 1, 0, tiled=True)

    def to_features(array_in):
        return undeal(lax.all_to_all(array_in, grid, 0, 1, tiled=True))

    def gather_weights(local):
        gathered = lax.all_gather(local, grid, axis=0)
        return gathered.reshape(rows, -1, local.shape[-1])

    def local_matrix(weight_list):
        flat = [weight.reshape(-1, weight.shape[-1]) for weight in weight_list]
        return flat[0] if len(flat) == 1 else jnp.concatenate(flat, axis=1)

    front_weights = gather_weights(local_matrix([w_value, w_shared, w_reset, w_hidden, w_update]))
    output_weights = gather_weights(local_matrix([w_output]))
    inner_weights = gather_weights(local_matrix([w_gate, w_up]))
    down_weights = gather_weights(local_matrix([w_down]))
    vectors = lax.all_gather(
        jnp.concatenate([final_gain, final_bias, query_gain, query_bias, key_gain]), grid, axis=0
    )
    feat_share, z_share = final_gain.shape[0], query_gain.shape[0]

    def whole_vector(start, share):
        return vectors[:, start : start + share].reshape(-1)

    gain_all = whole_vector(0, feat_share)
    bias_all = whole_vector(feat_share, feat_share)
    query_gain_all = whole_vector(2 * feat_share, z_share)
    query_bias_all = whole_vector(2 * feat_share + z_share, z_share)
    key_gain_all = whole_vector(2 * feat_share + 2 * z_share, z_share)

    valid_total = lax.psum(jnp.sum(block_len), "dp").astype(jnp.float32)
    positions = jnp.concatenate(
        [member * half + jnp.arange(half), (2 * group - 1 - member) * half + jnp.arange(half)]
    )
    valid_mask = (positions < block_len[my_block]).astype(jnp.float32)
    members = jnp.arange(group)[:, None]
    inside = jnp.arange(half)[None, :]
    key_positions = jnp.stack(
        [members * half + inside, (2 * group - 1 - members) * half + inside], axis=1
    ).reshape(-1)

    front_out, front_pull = jax.vjp(
        partial(front_piece, first_flags, piece_resets),
        layer_input,
        norm_gain,
        norm_bias,
        ema_rate,
        ema_angle,
        ema_input,
        ema_out_real,
        ema_out_imag,
        ema_skip,
    )
    normed, mixed_act = front_out
    sources = lax.all_to_all(
        jnp.stack([deal(normed.astype(bf16)), deal(mixed_act.astype(bf16))]), grid, 2, 1, tiled=True
    )
    normed_low = swap_blocks(sources[0], rows, cols)
    mixed_low = swap_blocks(sources[1], rows, cols)
    n_value, n_shared, n_reset, n_hidden = (
        weight.shape[-1] for weight in (w_value, w_shared, w_reset, w_hidden)
    )
    value_pre = project(front_weights[:, :, :n_value], normed_low)
    mixed_out = [
        contract_first(front_weights[part, :, n_value:], mixed_low) for part in range(rows)
    ]

    def mixed_slice(start, count):
        return jnp.concatenate([piece[start : start + count] for piece in mixed_out], axis=0)

    shared = mixed_slice(0, n_shared)
    reset_pre = mixed_slice(n_shared, n_reset)
    hidden_pre = mixed_slice(n_shared + n_reset, n_hidden)
    update_pre = mixed_slice(n_shared + n_reset + n_hidden, n_hidden)
    values_low = silu(value_pre).astype(bf16)
    queries = (shared * query_gain_all[:, None] + query_bias_all[:, None]).astype(bf16)
    keys_low = (shared * key_gain_all[:, None]).astype(bf16)
    key_values = jnp.concatenate([values_low, keys_low], axis=0)
    if rows == blocks_here:
        gathered_kv = lax.all_gather(key_values, "col", axis=0)
    else:
        gathered_kv = lax.dynamic_slice_in_dim(
            lax.all_gather(key_values, grid, axis=0), my_block * group, group, 0
        )
    gathered_kv = gathered_kv.transpose(1, 0, 2).reshape(key_values.shape[0], -1)
    width = values_low.shape[0]
    value_all, key_all = gathered_kv[:width], gathered_kv[width:]
    input_slots = to_slots(layer_input)
    teacher_slots = to_slots(teacher)

    score_scale = Z ** (-0.5)
    causal = positions[:, None] >= key_positions[None, :]
    scores = jnp.where(causal, contract_first(queries, key_all) * score_scale, NEGATIVE)
    top_score = jnp.max(scores, axis=1, keepdims=True)
    exponent = jnp.exp(scores - top_score)
    probs = exponent / jnp.sum(exponent, axis=1, keepdims=True)
    probs_low = probs.astype(bf16)
    attended = contract_last(value_all, probs_low)
    reset_act = silu(reset_pre)
    att_in = swap_blocks((attended * reset_act).astype(bf16), rows, cols)
    summed = hidden_pre + project(output_weights, att_in)
    hidden_act = silu(summed)
    gate_act = jax.nn.sigmoid(update_pre)
    first_out = input_slots + gate_act * (hidden_act - input_slots)
    mean_val = jnp.mean(first_out, axis=0)
    inv_std = lax.rsqrt(jnp.mean(first_out * first_out, axis=0) - mean_val * mean_val + EPSILON)
    unit_norm = (first_out - mean_val) * inv_std
    final_norm = swap_blocks(
        (unit_norm * gain_all[:, None] + bias_all[:, None]).astype(bf16), rows, cols
    )
    n_inner = w_gate.shape[-1]
    inner_out = [contract_first(inner_weights[part], final_norm) for part in range(rows)]
    gate_pre = jnp.concatenate([piece[:n_inner] for piece in inner_out], axis=0)
    up_pre = jnp.concatenate([piece[n_inner:] for piece in inner_out], axis=0)
    inner_act = swap_blocks((silu(gate_pre) * up_pre).astype(bf16), rows, cols)
    output_slots = first_out + project(down_weights, inner_act)
    out_error = (output_slots - teacher_slots) * valid_mask
    loss_part = jnp.sum(out_error * out_error)
    out_grad = out_error * (slot_count * dps / valid_total)
    layer_output = to_features(output_slots)

    out_low = out_grad.astype(bf16)
    inner_grad = swap_blocks(project_back(down_weights, out_low), cols, rows)
    gate_grad = (inner_grad * up_pre * silu_slope(gate_pre)).astype(bf16)
    up_grad = (inner_grad * silu(gate_pre)).astype(bf16)
    inner_grads = jnp.concatenate(
        [gate_grad.reshape(rows, -1, tokens), up_grad.reshape(rows, -1, tokens)], axis=1
    )
    norm_grad = swap_blocks(
        project_back(inner_weights, inner_grads.reshape(-1, tokens)), cols, rows
    )

    def scatter_weight(product_list, rank):
        stacked = jnp.stack(product_list)
        shaped = stacked.reshape(devices, rows * rank, stacked.shape[-1])
        return lax.psum_scatter(shaped, grid, scatter_dimension=0, tiled=True)[0]

    down_sum = scatter_weight(weight_products(inner_act, out_low, rows), w_down.shape[2])
    inner_sum = scatter_weight(weight_products(final_norm, inner_grads, rows), w_gate.shape[2])
    down_sum, inner_sum = lax.psum((down_sum, inner_sum), "dp")

    final_gain_part = jnp.sum(norm_grad * unit_norm, axis=1)
    final_bias_part = jnp.sum(norm_grad, axis=1)
    unit_grad = norm_grad * gain_all[:, None]
    first_grad = out_grad + inv_std * (
        unit_grad
        - jnp.mean(unit_grad, axis=0)
        - unit_norm * jnp.mean(unit_grad * unit_norm, axis=0)
    )
    residual_grad = to_features(first_grad * (1.0 - gate_act))
    update_grad = (first_grad * (hidden_act - input_slots) * gate_act * (1.0 - gate_act)).astype(
        bf16
    )
    summed_grad = (first_grad * gate_act * silu_slope(summed)).astype(bf16)
    att_grad = swap_blocks(project_back(output_weights, summed_grad), cols, rows)
    attended_grad = (att_grad * reset_act).astype(bf16)
    reset_grad = (att_grad * attended * silu_slope(reset_pre)).astype(bf16)
    prob_grad = contract_first(attended_grad, value_all)
    row_dot = jnp.sum(probs * prob_grad, axis=1, keepdims=True)
    score_grad = (probs * (prob_grad - row_dot)).astype(bf16)
    query_grad = contract_last(key_all, score_grad) * score_scale
    key_grad = jnp.dot(queries, score_grad, preferred_element_type=jnp.float32) * score_scale
    value_grad = jnp.dot(attended_grad, probs_low, preferred_element_type=jnp.float32)
    kv_parts = jnp.concatenate([value_grad, key_grad], axis=0).astype(bf16)
    kv_parts = kv_parts.reshape(-1, group, tokens).transpose(1, 0, 2)
    if rows == blocks_here:
        kv_grads = lax.psum_scatter(kv_parts, "col", scatter_dimension=0, tiled=True)[0]
    else:
        spread = lax.dynamic_update_slice_in_dim(
            jnp.zeros((devices,) + kv_parts.shape[1:], bf16), kv_parts, my_block * group, 0
        )
        kv_grads = lax.psum_scatter(spread, grid, scatter_dimension=0, tiled=True)[0]
    value_grad, key_grad = kv_grads[:width].astype(jnp.float32), kv_grads[width:].astype(jnp.float32)
    value_pre_grad = (value_grad * silu_slope(value_pre)).astype(bf16)
    shared_grad = (
        query_grad * query_gain_all[:, None] + key_grad * key_gain_all[:, None]
    ).astype(bf16)
    query_gain_part = jnp.sum(query_grad * shared, axis=1)
    query_bias_part = jnp.sum(query_grad, axis=1)
    key_gain_part = jnp.sum(key_grad * shared, axis=1)
    mixed_grads = jnp.concatenate(
        [
            piece.reshape(rows, -1, tokens)
            for piece in (shared_grad, reset_grad, summed_grad, update_grad)
        ],
        axis=1,
    )
    normed_back = swap_blocks(
        project_back(front_weights[:, :, :n_value], value_pre_grad), cols, rows
    )
    mixed_back = swap_blocks(
        project_back(front_weights[:, :, n_value:], mixed_grads.reshape(-1, tokens)), cols, rows
    )
    backs = lax.all_to_all(
        jnp.stack([normed_back, mixed_back]).astype(bf16), grid, 1, 2, tiled=True
    ).astype(jnp.float32)
    input_pulls = front_pull((undeal(backs[0]), undeal(backs[1])))
    input_grad = residual_grad + input_pulls[0]

    output_sum = scatter_weight(weight_products(att_in, summed_grad, rows), w_output.shape[2])
    front_products = [
        jnp.concatenate(pair, axis=1)
        for pair in zip(
            weight_products(normed_low, value_pre_grad, rows),
            weight_products(mixed_low, mixed_grads, rows),
        )
    ]
    front_sum = scatter_weight(front_products, w_value.shape[2])
    output_sum, front_sum, down_sum = lax.optimization_barrier((output_sum, front_sum, down_sum))
    output_sum, front_sum = lax.psum((output_sum, front_sum), "dp")

    small = lax.psum(
        jnp.concatenate(
            [
                final_gain_part,
                final_bias_part,
                query_gain_part,
                query_bias_part,
                key_gain_part,
                loss_part[None],
            ]
        ),
        ("dp", "row", "col"),
    )
    loss_value = small[-1] / (2.0 * valid_total * D)

    def my_share(start, share):
        return lax.dynamic_slice_in_dim(small, start + place * share, share, 0)

    z_size = share_total = z_share * devices
    feat_size = feat_share * devices
    param_sums = lax.psum(input_pulls[1:], "dp")

    def split_columns(array_in, weight_list):
        results = []
        offset = 0
        for weight in weight_list:
            count = weight.shape[-1]
            piece = array_in[:, offset : offset + count].astype(jnp.float32)
            results.append(piece.reshape(weight.shape))
            offset += count
        return results

    value_g, shared_g, reset_g, hidden_g, update_g = split_columns(
        front_sum, [w_value, w_shared, w_reset, w_hidden, w_update]
    )
    (output_g,) = split_columns(output_sum, [w_output])
    gate_g, up_g = split_columns(inner_sum, [w_gate, w_up])
    (down_g,) = split_columns(down_sum, [w_down])
    return (
        layer_output,
        loss_value,
        input_grad,
        *param_sums,
        value_g,
        shared_g,
        reset_g,
        hidden_g,
        update_g,
        my_share(2 * feat_size, z_share),
        my_share(2 * feat_size + z_size, z_share),
        my_share(2 * feat_size + 2 * z_size, z_share),
        output_g,
        my_share(0, feat_share),
        my_share(feat_size, feat_share),
        gate_g,
        up_g,
        down_g,
    )


def solution(mesh):
    in_specs = (
        P(("row", "col"), "dp"),
        P(("row", "col"), "dp"),
        P("dp"),
        P("dp"),
        P(("row", "col")),
        P(("row", "col")),
        P(("row", "col"), None),
        P(("row", "col"), None),
        P(("row", "col"), None),
        P(("row", "col"), None),
        P(("row", "col"), None),
        P(("row", "col")),
        P(None, "col", None, "row"),
        P(None, "col", None, "row"),
        P(None, "col", None, "row"),
        P(None, "col", None, "row"),
        P(None, "col", None, "row"),
        P(("row", "col")),
        P(("row", "col")),
        P(("row", "col")),
        P(None, "col", None, "row"),
        P(("row", "col")),
        P(("row", "col")),
        P(None, "col", None, "row"),
        P(None, "col", None, "row"),
        P(None, "col", None, "row"),
    )
    out_specs = (
        P(("row", "col"), "dp"),
        P(),
        P(("row", "col"), "dp"),
        P(("row", "col")),
        P(("row", "col")),
        P(("row", "col"), None),
        P(("row", "col"), None),
        P(("row", "col"), None),
        P(("row", "col"), None),
        P(("row", "col"), None),
        P(("row", "col")),
        P(None, "col", None, "row"),
        P(None, "col", None, "row"),
        P(None, "col", None, "row"),
        P(None, "col", None, "row"),
        P(None, "col", None, "row"),
        P(("row", "col")),
        P(("row", "col")),
        P(("row", "col")),
        P(None, "col", None, "row"),
        P(("row", "col")),
        P(("row", "col")),
        P(None, "col", None, "row"),
        P(None, "col", None, "row"),
        P(None, "col", None, "row"),
    )
    return jax.shard_map(shards, mesh=mesh, in_specs=in_specs, out_specs=out_specs, check_vma=False)
```

time: 3290 us -> 1500 us (0.46)
  waiting for transfers between devices: 1920 us -> 121 us
  local copies, waits for them, and re-layouts: 487 us -> 593 us
  matrix products: 309 us -> 221 us
  other arithmetic: 420 us -> 374 us
    reduce_scatter x9 -> x5, waiting for transfers between devices: 1230 us -> 70 us  [the longest x1 70 us: shards(): lax.psum_scatter(kv_parts, 'col', scatter_dimension=0, tiled=True)[0]]
    all_gather x9 -> x5, waiting for transfers between devices: 559 us -> 39.7 us  [the longest x4 25.5 us: gather_weights(): gathered = lax.all_gather(local, grid, axis=0)]
    psum x1 -> x2, waiting for transfers between devices: 133 us -> 0.01 us  [the longest x1 0.01 us: shards(): output_sum, front_sum = lax.psum((output_sum, front_sum), 'dp')]
    dot_general x13 -> x12, matrix products: 88.4 us -> 36.1 us  [contract_first(): lax.dot_general(left_in, right_in, (((0,), (0,)), ((), ())), preferred_el...]
    concatenate x5 -> x6, other arithmetic: 49.3 us -> 5.5 us  [the longest x1 2.23 us: local_matrix(): return flat[0] if len(flat) == 1 else jnp.concatenate(flat, axis=1)]
    another operation x18 -> x40, local copies, waits for them, and re-layouts: 0.82 us -> 44.2 us  [the longest x1 18.1 us: shards(): jnp.stack([deal(normed.astype(bf16)), deal(mixed_act.astype(bf16))])]
    unnamed x0 -> x1, blocking collectives: none -> 41.9 us
    reshape x0 -> x14, local copies, waits for them, and re-layouts: none -> 38.7 us  [the longest x6 15.9 us: swap_blocks(): shaped = array_in.reshape(outer, inner, -1, array_in.shape[-1])]
  transfers between devices with their start and end apart: 19 -> 18, of which waited for: 19 -> 5; matrix products, arithmetic and copies ran while one was open for 3% -> 74% of each run, Pallas kernels for 0% -> 0%
where the time goes in v1:
time: 1500 us; the launch traced here: 1480 us
  local copies, waits for them, and re-layouts  593 us (40%)
  other arithmetic  374 us (25%)
  matrix products  221 us (15%)
  waiting for transfers between devices  121 us (8%)
  blocking collectives  116 us (8%)
  starting transfers between devices  26 us (2%)
  between operations  21.6 us (1%)
    pad x64, local copies, waits for them, and re-layouts, ema_blocks(): lax.associative_scan(combine, (step_re, step_im, ends_re, ends_im), axis=1)  157 us
    scatter-add x1, other arithmetic, ema_blocks(): kernel.T[:, jnp.maximum(offsets, 0)]  98.3 us
    unnamed x559, local copies, waits for them, and re-layouts  77.7 us
    reduce_scatter x1, waiting for transfers between devices, shards(): lax.psum_scatter(kv_parts, 'col', scatter_dimension=0, tiled=True)[0]  70 us
    gather x1, local copies, waits for them, and re-layouts, ema_blocks(): kernel.T[:, jnp.maximum(offsets, 0)]  59.6 us
    slice x18, local copies, waits for them, and re-layouts, ema_blocks(): lax.associative_scan(combine, (step_re, step_im, ends_re, ends_im), axis=1)  49.4 us
    dot_general x12, matrix products, contract_last(): lax.dot_general(left_in, right_in, (((1,), (1,)), ((), ())), preferred_el...  48.2 us
    psum x1, blocking collectives, shards(): lax.psum(jnp.concatenate([final_gain_part, final_bias_part, query_gain_pa...  43.9 us
  transfers between devices with their start and end apart: 18, of which 5 were waited for; matrix products, arithmetic and copies ran while one was open for 74% of the time, Pallas kernels for 0%

profile of v1, /device:TPU:0, one launch (start us, length us, event | category | flops | bytes accessed | tf_op | source)
XLA Modules:
  0.0 1475.4 jit_solution(6110343799298397937)
XLA Ops:
  16.1 10.4 fusion.90
  40.4 8.7 while.79
  73.7 6.4 slice.706
  80.1 6.6 slice.649
  90.3 6.4 slice.640
  99.0 5.7 fusion.118
  104.6 8.4 slice.636
  113.0 8.8 slice.641
  181.9 8.4 slice.702
  193.5 59.6 %gather_fusion = f32[16384,128]{1,0:T(8,128)} fusion(f32[128,128]{0,1:T(8,128)S(1)} %bitcast.655, s32[16384]{0:T(1024)} %broadcast_clamp_fusion), kind=kCustom, calls=%fused_computation | custom fusion | bytes 16842752 | tf_op jit(solution)/shard_map/jvp()/gather | solution.py:79
  253.1 9.9 select_bitcast_fusion
  263.1 9.4 copy.798
  305.4 6.0 pad.952
  313.5 6.1 fusion.110
  319.6 15.7 %fusion.220 = f32[128,32,128]{2,1,0:T(8,128)S(1)} fusion(f32[128,32,128]{2,1,0:T(8,128)S(1)} %bitcast.658, f32[128,128,128]{2,1,0:T(8,128)} %copy.798), kind=kOutput, calls=%fused_computation.570 | convolution fusion | flops 805306368 | bytes 12582912 | tf_op jit(solution)/shard_map/jvp(cts,cbs->cbt)/dot_general | solution.py:81
  346.7 18.1 %copy.814 = bf16[2,128,4096]{1,0,2:T(2,128)(2,1)} copy(bf16[2,128,4096]{1,2,0:T(8,128)(2,1)S(1)} %pad_maximum_fusion.12) | data formatting | bytes 4194304 | tf_op jit(solution)/shard_map/stack | solution.py:279
  371.7 41.9 %all-reduce.103 = f32[2816]{0:T(1024)S(1)} all-reduce(f32[2816]{0:T(1024)S(1)} %dynamic-update-slice), channel_id=3, replica_groups=mesh['dp'=4,'row'=2,'col'=4] {'row','col'}, use_global_device_ids=true, to_apply=%add.103 | all-reduce | flops 2816 | bytes 22528
  451.1 9.2 psum.98
  504.9 14.2 all-gather.16.cloned.1.call-done
  519.1 12.8 copy.820
  531.9 8.3 slice.874
  547.3 7.7 multiply_convert_fusion.1
  576.0 25.5 %all-gather.18.cloned.1.call-done = bf16[2048,2560]{1,0:T(8,128)(2,1)} async-done(((bf16[256,2560]{1,0:T(8,128)(2,1)}), bf16[2048,2560]{1,0:T(8,128)(2,1)}) %all-gather.18.cloned.1.call-update) | async-done | bytes 10485776 | tf_op jit(solution)/shard_map/all_gather | solution.py:229
  639.3 5.9 copy.830
  649.3 5.8 fusion.11
  668.0 6.4 fusion.75
  679.6 6.7 reshape.1146
  686.4 7.3 copy.833
  693.7 8.0 fusion.25
  703.8 8.3 multiply_reduce_fusion
  729.7 6.9 convolution_convert_fusion.4
  736.6 7.2 maximum_bitcast_fusion
  750.7 6.6 multiply_convert_fusion.4
  757.4 70.0 %reduce-scatter.6.cloned.1.call-done = bf16[1,2304,512]{2,1,0:T(8,128)(2,1)} async-done(((bf16[4,2304,512]{2,1,0:T(8,128)(2,1)}), bf16[1,2304,512]{2,1,0:T(8,128)(2,1)}) %reduce-scatter.6.cloned.1.call-update) | async-done | bytes 2359312 | tf_op jit(solution)/shard_map/reduce_scatter | solution.py:390
  861.1 7.7 pad_maximum_fusion
  870.2 6.4 fusion.68
  881.1 7.0 fusion.15
  888.1 6.0 fusion.14
  894.1 9.0 pad_maximum_fusion.1
  969.9 43.9 %psum.99 = f32[2817]{0:T(1024)S(1)} all-reduce(f32[2817]{0:T(1024)S(1)} %constant_dynamic-update-slice_fusion.7), channel_id=1, replica_groups=mesh['dp'=4,'row'=2,'col'=4] {'dp','row','col'}, use_global_device_ids=true, to_apply=%region_30.31 | all-reduce | flops 2817 | bytes 22536 | tf_op jit(solution)/shard_map/psum | solution.py:435
  1211.8 10.0 add_add_fusion.1
  1229.4 9.9 reduce-window.44
  1245.7 10.6 reduce-window.40
  1261.3 17.0 %select_bitcast_fusion.1 = f32[128,128,128]{1,0,2:T(8,128)} fusion(pred[128,128]{1,0:T(8,128)(4,1)S(1)} %copy-done.181, f32[128,32,128]{2,1,0:T(8,128)} %bitcast.665, f32[128,32,128]{2,1,0:T(8,128)S(1)} %bitcast.659), kind=kOutput, calls=%fused_computation.27 | convolution fusion | flops 807403520 | bytes 12599296 | tf_op jit(solution)/shard_map/transpose(jvp(cts,cbs->cbt))/dot_general | solution.py:81
  1278.3 9.3 copy.886
  1287.6 98.3 %scatter_custom_fusion = f32[128,128]{0,1:T(8,128)S(1)} fusion(s32[16384]{0:T(1024)} %maximum_bitcast_fusion.3, f32[16384,128]{1,0:T(8,128)} %bitcast.707, f32[]{:T(128)} %constant.217.clone.1), kind=kCustom, calls=%fused_computation.415 | custom fusion | flops 2097152 | bytes 66048 | tf_op jit(solution)/shard_map/transpose(jvp())/scatter-add | solution.py:79
  1413.2 13.6 multiply_reduce_fusion.2
  1427.0 21.5 %all-reduce.104 = (f32[128]{0:T(128)}, f32[128]{0:T(128)}, f32[128,16]{0,1:T(8,128)}, f32[128,16]{1,0:T(8,128)S(1)}, f32[128,16]{0,1:T(8,128)}, /*index=5*/f32[1...) all-reduce(f32[128]{0:T(128)S(1)} %copy-done.228, ...), channel_id=1, replica_groups=mesh['dp'=4,'row'=2,'col'=4] {'dp'}, use_global_device_ids=true, to_apply=%region_44.45 | all-reduce | flops 10624 | bytes 84992 | tf_op jit(solution)/shard_map/psum | solution.py:455
  (1072 shorter events, 749.9 us)
Async XLA Ops:
  7.2 408.1 %all-gather.14.cloned.1.call-start = ((), (), s32[]{:S(2)}) async-start(), calls=%async_computation.19 | async-start | bytes 14745600 | tf_op jit(solution)/shard_map/all_gather | solution.py:229
  11.7 469.2 %all-gather.10.cloned.1.call-start = ((), (), s32[]{:S(2)}) async-start(), calls=%async_computation.11 | async-start | bytes 4718592 | tf_op jit(solution)/shard_map/all_gather | solution.py:229
  12.4 472.9 %all-gather.12.cloned.1.call-start = ((), (), s32[]{:S(2)}) async-start(), calls=%async_computation.12 | async-start | bytes 5898240 | tf_op jit(solution)/shard_map/all_gather | solution.py:229
  15.0 238.1 %copy-start.180 = (pred[128,128]{1,0:T(8,128)(4,1)}, pred[128,128]{1,0:T(8,128)(4,1)S(1)}, u32[]{:S(2)}) copy-start(pred[128,128]{1,0:T(8,128)(4,1)S(1)} %subtract_compare_fusion) | copy-start | bytes 49156
  16.0 319.4 %copy-start.101 = (f32[128,16]{1,0:T(8,128)}, f32[128,16]{1,0:T(8,128)S(1)}, u32[]{:S(2)}) copy-start(f32[128,16]{1,0:T(8,128)S(1)} %copy.796) | copy-start | bytes 24580
  33.1 18.0 %copy-start.171 = (f32[4,2,2048]{2,1,0:T(2,128)}, f32[4,2,2048]{2,1,0:T(2,128)S(1)}, u32[]{:S(2)}) copy-start(f32[4,2,2048]{2,1,0:T(2,128)S(1)} %reduce_window_sum.111) | copy-start | bytes 196612
  67.4 252.2 %copy-start = (f32[16,8,32,128]{3,2,1,0:T(8,128)}, f32[16,8,32,128]{3,2,1,0:T(8,128)S(1)}, u32[]{:S(2)}) copy-start(f32[16,8,32,128]{3,2,1,0:T(8,128)S(1)} %copy.924) | copy-start | bytes 6291460
  67.5 122.8 %copy-start.64 = (f32[128,16]{1,0:T(8,128)}, f32[128,16]{1,0:T(8,128)S(1)}, u32[]{:S(2)}) copy-start(f32[128,16]{1,0:T(8,128)S(1)} %copy.792) | copy-start | bytes 24580
  136.9 167.3 %copy-start.55 = (f32[128,32,16]{0,2,1:T(8,128)}, f32[128,32,16]{0,2,1:T(8,128)S(1)}, u32[]{:S(2)}) copy-start(f32[128,32,16]{0,2,1:T(8,128)S(1)} %get-tuple-element.947) | copy-start | bytes 786436
  263.0 16.3 %copy-start.200 = (f32[128,1,16]{0,2,1:T(8,128)S(1)}, f32[128,1,16]{0,2,1:T(8,128)}, u32[]{:S(2)}) copy-start(f32[128,1,16]{0,2,1:T(8,128)} %slice.818) | copy-start | bytes 24580
  263.1 27.1 %copy-start.160 = (f32[128,7,16]{0,2,1:T(8,128)S(1)}, f32[128,7,16]{0,2,1:T(8,128)}, u32[]{:S(2)}) copy-start(f32[128,7,16]{0,2,1:T(8,128)} %get-tuple-element.742) | copy-start | bytes 172036
  272.4 18.7 %copy-start.201 = (f32[128,1,16]{0,2,1:T(8,128)S(1)}, f32[128,1,16]{0,2,1:T(8,128)}, u32[]{:S(2)}) copy-start(f32[128,1,16]{0,2,1:T(8,128)} %slice.853) | copy-start | bytes 24580
  313.5 21.9 %copy-start.36 = (f32[128,32,16]{1,2,0:T(8,128)}, f32[128,32,16]{1,2,0:T(8,128)S(1)}, u32[]{:S(2)}) copy-start(f32[128,32,16]{1,2,0:T(8,128)S(1)} %copy.810) | copy-start | bytes 786436
  364.9 48.9 %all-to-all-start.1 = ((bf16[2,128,4096]{1,0,2:T(2,128)(2,1)}), bf16[2,128,4096]{1,0,2:T(2,128)(2,1)S(1)}, u32[]{:S(2)}, u32[]{:S(2)}) async-start(bf16[2,128,4096]{1,0,2:T(2,128)(2,1)} %copy.814), calls=%async_computation.1 | async-start | bytes 4194304 | tf_op jit(solution)/shard_map/all_to_all | solution.py:278
  370.0 149.1 %all-gather.16.cloned.1.call-start = ((), (), s32[]{:S(2)}) async-start(), calls=%async_computation.20 | async-start | bytes 11796480 | tf_op jit(solution)/shard_map/all_gather | solution.py:303
  422.7 119.0 %copy-start.129 = (f32[128,512]{1,0:T(8,128)}, f32[128,512]{1,0:T(8,128)S(1)}, u32[]{:S(2)}) copy-start(f32[128,512]{1,0:T(8,128)S(1)} %slice.872) | copy-start | bytes 786436
  431.7 169.8 %all-gather.18.cloned.1.call-start = ((), (), s32[]{:S(2)}) async-start(), calls=%async_computation.21 | async-start | bytes 11796480 | tf_op jit(solution)/shard_map/all_gather | solution.py:229
  447.4 114.9 %all-to-all-start = ((f32[128,8,512]{2,0,1:T(8,128)}), f32[128,8,512]{2,0,1:T(8,128)S(1)}, u32[]{:S(2)}, u32[]{:S(2)}) async-start(f32[128,8,512]{2,0,1:T(8,128)} %all_to_all.72), calls=%async_computation | async-start | bytes 4194304 | tf_op jit(solution)/shard_map/all_to_all | solution.py:223
  460.4 81.3 %copy-start.229 = (f32[256]{0:T(256)}, f32[256]{0:T(256)S(1)}, u32[]{:S(2)}) copy-start(f32[256]{0:T(256)S(1)} %add.924) | copy-start | bytes 3076
  460.5 81.2 %copy-start.224 = (f32[256]{0:T(256)}, f32[256]{0:T(256)S(1)}, u32[]{:S(2)}) copy-start(f32[256]{0:T(256)S(1)} %mul.1433) | copy-start | bytes 3076
  563.6 59.5 %all-to-all-start.3 = ((f32[128,8,512]{2,0,1:T(8,128)}), f32[128,8,512]{2,0,1:T(8,128)S(1)}, u32[]{:S(2)}, u32[]{:S(2)}) async-start(f32[128,8,512]{2,0,1:T(8,128)} %all_to_all.82), calls=%async_computation.3 | async-start | bytes 4194304 | tf_op jit(solution)/shard_map/all_to_all | solution.py:223
  567.3 190.1 %reduce-scatter.12.cloned.1.call-start = ((), (), s32[]{:S(2)}) async-start(), calls=%async_computation.16 | async-start | bytes 5898240 | tf_op jit(solution)/shard_map/reduce_scatter | solution.py:359
  667.9 159.5 %reduce-scatter.6.cloned.1.call-start = ((), (), s32[]{:S(2)}) async-start(), calls=%async_computation.13 | async-start | bytes 11796480 | tf_op jit(solution)/shard_map/reduce_scatter | solution.py:390
  743.8 500.1 %reduce-scatter.8.cloned.1.call-start = ((), (), s32[]{:S(2)}) async-start(), calls=%async_computation.14 | async-start | bytes 4718592 | tf_op jit(solution)/shard_map/reduce_scatter | solution.py:359
  750.7 493.2 %all-reduce.109.cloned.1.call-start = ((), (), s32[]{:S(2)}) async-start(), calls=%async_computation.17 | async-start | bytes 1310720 | tf_op jit(solution)/shard_map/psum | solution.py:363
  750.7 76.7 %copy-start.223 = (f32[256]{0:T(256)S(1)}, f32[256]{0:T(256)}, u32[]{:S(2)}) copy-start(f32[256]{0:T(256)} %copy-done.222) | copy-start | bytes 3076
  757.4 486.5 %reduce-scatter.10.cloned.1.call-start = ((), (), s32[]{:S(2)}) async-start(), calls=%async_computation.15 | async-start | bytes 14745600 | tf_op jit(solution)/shard_map/reduce_scatter | solution.py:359
  876.5 31.2 %all-to-all-start.2 = ((f32[8,128,512]{2,1,0:T(8,128)}), f32[8,128,512]{2,1,0:T(8,128)}, u32[]{:S(2)}, u32[]{:S(2)}) async-start(f32[8,128,512]{2,1,0:T(8,128)} %get-tuple-element.732), calls=%async_computation.2 | async-start | bytes 4194304 | tf_op jit(solution)/shard_map/all_to_all | solution.py:226
  881.0 362.8 %reduce-scatter.14.cloned.1.call-start = ((), (), s32[]{:S(2)}) async-start(), calls=%async_computation.18 | async-start | bytes 11796480 | tf_op jit(solution)/shard_map/reduce_scatter | solution.py:359
  907.7 31.0 %all-to-all-start.4 = ((f32[8,128,512]{2,1,0:T(8,128)}), f32[8,128,512]{2,1,0:T(8,128)}, u32[]{:S(2)}, u32[]{:S(2)}) async-start(f32[8,128,512]{2,1,0:T(8,128)} %get-tuple-element.731), calls=%async_computation.5 | async-start | bytes 4194304 | tf_op jit(solution)/shard_map/all_to_all | solution.py:226
  938.7 77.5 %all-to-all-start.5 = ((bf16[2,1024,512]{2,0,1:T(2,128)(2,1)}), bf16[2,1024,512]{2,0,1:T(2,128)(2,1)}, u32[]{:S(2)}, u32[]{:S(2)}) async-start(bf16[2,1024,512]{2,0,1:T(2,128)(2,1)} %copy.841), calls=%async_computation.6 | async-start | bytes 4194304 | tf_op jit(solution)/shard_map/all_to_all | solution.py:417
  943.1 512.9 %all-reduce.111.cloned.1.call-start = ((), (), s32[]{:S(2)}) async-start(), calls=%async_computation.22 | async-start | bytes 6946816 | tf_op jit(solution)/shard_map/psum | solution.py:433
  1034.6 177.2 %copy-start.2 = (f32[16,8,32,128]{3,2,1,0:T(8,128)}, f32[16,8,32,128]{3,2,1,0:T(8,128)S(1)}, u32[]{:S(2)}) copy-start(f32[16,8,32,128]{3,2,1,0:T(8,128)S(1)} %copy.927) | copy-start | bytes 6291460
  1054.3 19.8 %copy-start.135 = (f32[128,8,16]{0,2,1:T(8,128)S(1)}, f32[128,8,16]{0,2,1:T(8,128)}, u32[]{:S(2)}) copy-start(f32[128,8,16]{0,2,1:T(8,128)} %copy-done.134) | copy-start | bytes 196612
  1054.3 19.8 %copy-start.137 = (f32[128,8,16]{0,2,1:T(8,128)S(1)}, f32[128,8,16]{0,2,1:T(8,128)}, u32[]{:S(2)}) copy-start(f32[128,8,16]{0,2,1:T(8,128)} %copy-done.136) | copy-start | bytes 196612
  1056.4 52.0 %copy-start.109 = (f32[128,16,16]{0,2,1:T(8,128)S(1)}, f32[128,16,16]{0,2,1:T(8,128)}, u32[]{:S(2)}) copy-start(f32[128,16,16]{0,2,1:T(8,128)} %copy-done.108) | copy-start | bytes 393220
  1062.4 44.2 %copy-start.188 = (f32[128,3,16]{0,2,1:T(8,128)S(1)}, f32[128,3,16]{0,2,1:T(8,128)}, u32[]{:S(2)}) copy-start(f32[128,3,16]{0,2,1:T(8,128)} %get-tuple-element.901) | copy-start | bytes 73732
  1108.5 54.2 %copy-start.98 = (f32[128,16,16]{0,2,1:T(8,128)S(1)}, f32[128,16,16]{0,2,1:T(8,128)}, u32[]{:S(2)}) copy-start(f32[128,16,16]{0,2,1:T(8,128)} %copy.898) | copy-start | bytes 393220
  1108.5 54.2 %copy-start.99 = (f32[128,16,16]{0,2,1:T(8,128)S(1)}, f32[128,16,16]{0,2,1:T(8,128)}, u32[]{:S(2)}) copy-start(f32[128,16,16]{0,2,1:T(8,128)} %copy.899) | copy-start | bytes 393220
  1108.5 54.2 %slice-start.4 = ((f32[128,8,16]{0,2,1:T(8,128)}), f32[128,1,16]{0,2,1:T(8,128)S(1)}, s32[]{:S(2)}) async-start(f32[128,8,16]{0,2,1:T(8,128)} %copy-done.176), calls=%async_computation.27 | async-start | bytes 16384 | tf_op jit(solution)/shard_map/transpose(jvp())/split | solution.py:100
  1108.5 54.2 %slice-start.5 = ((f32[128,8,16]{0,2,1:T(8,128)}), f32[128,1,16]{0,2,1:T(8,128)S(1)}, s32[]{:S(2)}) async-start(f32[128,8,16]{0,2,1:T(8,128)} %copy-done.177), calls=%async_computation.28 | async-start | bytes 16384 | tf_op jit(solution)/shard_map/transpose(jvp())/split | solution.py:100
  1164.9 18.5 %slice-start.3 = ((f32[128,16,16]{0,2,1:T(8,128)}), f32[128,1,16]{0,2,1:T(8,128)S(1)}, s32[]{:S(2)}) async-start(f32[128,16,16]{0,2,1:T(8,128)} %copy-done.155), calls=%async_computation.26 | async-start | bytes 16384 | tf_op jit(solution)/shard_map/transpose(jvp())/split | solution.py:100
  1172.2 19.5 %slice-start.2 = ((f32[128,16,16]{0,2,1:T(8,128)}), f32[128,1,16]{0,2,1:T(8,128)S(1)}, s32[]{:S(2)}) async-start(f32[128,16,16]{0,2,1:T(8,128)} %copy-done.154), calls=%async_computation.25 | async-start | bytes 16384 | tf_op jit(solution)/shard_map/transpose(jvp())/split | solution.py:100
  1224.5 15.9 %copy-start.210 = (f32[4]{0:T(128)S(1)}, f32[4]{0:T(128)}, u32[]{:S(2)}) copy-start(f32[4]{0:T(128)} %custom-call.2) | copy-start | bytes 52
  1243.9 17.5 %copy-start.1 = (f32[16,8,32,128]{3,2,1,0:T(8,128)S(1)}, f32[16,8,32,128]{3,2,1,0:T(8,128)}, u32[]{:S(2)}) copy-start(f32[16,8,32,128]{3,2,1,0:T(8,128)} %copy-done) | copy-start | bytes 6291460
  1243.9 17.5 %copy-start.181 = (pred[128,128]{1,0:T(8,128)(4,1)S(1)}, pred[128,128]{1,0:T(8,128)(4,1)}, u32[]{:S(2)}) copy-start(pred[128,128]{1,0:T(8,128)(4,1)} %copy-done.180) | copy-start | bytes 49156
  1413.2 37.3 %copy-start.10 = (f32[128,4096]{1,0:T(8,128)S(1)}, f32[128,4096]{1,0:T(8,128)}, u32[]{:S(2)}) copy-start(f32[128,4096]{1,0:T(8,128)} %param.36) | copy-start | bytes 6291460
  1413.2 37.3 %copy-start.173 = (f32[1,4,32,128]{3,1,2,0:T(4,128)S(1)}, f32[1,4,32,128]{3,1,2,0:T(4,128)}, u32[]{:S(2)}) copy-start(f32[1,4,32,128]{3,1,2,0:T(4,128)} %copy.963) | copy-start | bytes 196612
  (227 other events, 961.5 us)
Sparse Core Ops, SparseCore 0:
  11.8 77.0 all-gather.13
  90.7 36.7 all-gather.9
  129.4 41.1 all-gather.11
  431.8 87.2 all-gather.15
  521.4 80.1 all-gather.17
  668.0 62.1 reduce-scatter.11
  743.9 83.4 reduce-scatter.5
  831.2 51.3 reduce-scatter.7
  884.9 40.3 all-reduce.108
  928.7 105.0 reduce-scatter.9
  1037.3 81.5 reduce-scatter.13
  1244.0 131.7 all-reduce.110

commit v2 on v1

v2 whole, which is shorter than its diff:
```python
from functools import partial

import jax
import jax.numpy as jnp
from jax import lax
from jax.experimental import pallas as pl
from jax.experimental.pallas import tpu as pltpu
from jax.sharding import PartitionSpec as P

D = 1024
Z = 256
SPAN = 2048
GS = 32
UNIT = 128
STATES = 16
COUNT_ROWS = 256
BATCH = 16
BATCH_BACK = 16

EPSILON = 1e-05
NEGATIVE = -1000000000.0


NT = (((1,), (1,)), ((), ()))
NN = (((1,), (0,)), ((), ()))
TN = (((0,), (0,)), ((), ()))


def halves(array_in):
    high = array_in.astype(jnp.bfloat16)
    return high, (array_in - high.astype(jnp.float32)).astype(jnp.bfloat16)


def dot_split(left, right, dims):
    left_high, left_low = left
    right_high, right_low = right
    product = partial(lax.dot_general, dimension_numbers=dims, preferred_element_type=jnp.float32)
    return (
        product(left_high, right_high)
        + product(left_low, right_high)
        + product(left_high, right_low)
    )


def dot_exact(left, right):
    return lax.dot_general(
        left, right, NN, precision=lax.Precision.HIGHEST, preferred_element_type=jnp.float32
    )


def toeplitz(kernel_row):
    rows = lax.broadcasted_iota(jnp.int32, (UNIT, UNIT), 0)
    lanes = lax.broadcasted_iota(jnp.int32, (UNIT, UNIT), 1)
    spread = pltpu.roll(
        jnp.broadcast_to(kernel_row, (UNIT, UNIT)), 0, 1, stride=1, stride_axis=0
    )
    return jnp.where(lanes >= rows, spread, 0.0)


def lag_sums(products):
    rows = lax.broadcasted_iota(jnp.int32, (UNIT, UNIT), 0)
    lanes = lax.broadcasted_iota(jnp.int32, (UNIT, UNIT), 1)
    kept = jnp.where(rows + lanes >= UNIT - 1, products, 0.0)
    aligned = pltpu.roll(kept, 0, 1, stride=1, stride_axis=0)
    return pltpu.roll(jnp.sum(aligned, axis=0, keepdims=True), 1, 1)


def reversed_lanes(parts):
    rows = lax.broadcasted_iota(jnp.int32, (UNIT, UNIT), 0)
    lanes = lax.broadcasted_iota(jnp.int32, (UNIT, UNIT), 1)
    mirror = (rows + lanes == UNIT - 1).astype(jnp.bfloat16)
    return tuple(
        lax.dot_general(part, mirror, NN, preferred_element_type=jnp.float32).astype(jnp.bfloat16)
        for part in parts
    )


def power_tables(turn_re, turn_im):
    lanes = lax.broadcasted_iota(jnp.int32, (STATES, UNIT), 1)
    now_re = jnp.broadcast_to(turn_re, (STATES, UNIT))
    now_im = jnp.broadcast_to(turn_im, (STATES, UNIT))
    up_re = jnp.ones((STATES, UNIT), jnp.float32)
    up_im = jnp.zeros((STATES, UNIT), jnp.float32)
    down_re, down_im = up_re, up_im
    for bit in range(UNIT.bit_length() - 1):
        is_set = ((lanes >> bit) & 1) == 1
        next_re = up_re * now_re - up_im * now_im
        next_im = up_re * now_im + up_im * now_re
        fall_re = down_re * now_re - down_im * now_im
        fall_im = down_re * now_im + down_im * now_re
        up_re, up_im = jnp.where(is_set, next_re, up_re), jnp.where(is_set, next_im, up_im)
        down_re = jnp.where(is_set, down_re, fall_re)
        down_im = jnp.where(is_set, down_im, fall_im)
        now_re, now_im = now_re * now_re - now_im * now_im, 2.0 * now_re * now_im
    return up_re, up_im, down_re, down_im, now_re, now_im


def state_scan(ends_re, ends_im, leap_re, leap_im, allowed, units, sign):
    lanes = lax.broadcasted_iota(jnp.int32, ends_re.shape, 1)
    distance = 1
    while distance < units:
        shift = distance if sign > 0 else units - distance
        past_re = pltpu.roll(ends_re, shift, 1)
        past_im = pltpu.roll(ends_im, shift, 1)
        keep = allowed(lanes, distance)
        past_re = jnp.where(keep, past_re, 0.0)
        past_im = jnp.where(keep, past_im, 0.0)
        ends_re, ends_im = (
            ends_re + leap_re * past_re - leap_im * past_im,
            ends_im + leap_re * past_im + leap_im * past_re,
        )
        leap_re, leap_im = leap_re * leap_re - leap_im * leap_im, 2.0 * leap_re * leap_im
        distance *= 2
    shift = 1 if sign > 0 else units - 1
    keep = allowed(lanes, 1)
    return (
        jnp.where(keep, pltpu.roll(ends_re, shift, 1), 0.0),
        jnp.where(keep, pltpu.roll(ends_im, shift, 1), 0.0),
    )


def front_forward_kernel(
    places,
    units,
    start_row,
    start_col,
    x_ref,
    teacher_ref,
    state_ref,
    channel_ref,
    send_ref,
    plain_ref,
    pre_ref,
    stat_ref,
    table_ref,
    row_ref,
    hold_ref,
    normed_ref,
    sums_ref,
    ends_ref,
):
    f32 = jnp.float32
    rows = lax.broadcasted_iota(jnp.int32, (UNIT, UNIT), 0)
    lanes = lax.broadcasted_iota(jnp.int32, (UNIT, UNIT), 1)
    upper = (rows <= lanes).astype(f32)
    for unit in range(units):
        tile = x_ref[:, unit * UNIT : (unit + 1) * UNIT]
        sums_ref[unit : unit + 1, :] = jnp.sum(tile, axis=0, keepdims=True)
        sums_ref[units + unit : units + unit + 1, :] = jnp.sum(tile * tile, axis=0, keepdims=True)
    inside = dot_exact(sums_ref[...], upper)
    starts = start_col[...]
    later = lax.broadcasted_iota(jnp.int32, (units, units), 0)
    sooner = lax.broadcasted_iota(jnp.int32, (units, units), 1)
    before = ((sooner < later) & (sooner >= starts)).astype(f32)
    totals = jnp.broadcast_to(inside[:, UNIT - 1 : UNIT], (2 * units, UNIT))
    sum_one = inside[:units] + dot_exact(before, totals[:units])
    sum_two = inside[units:] + dot_exact(before, totals[units:])
    unit_at = lax.broadcasted_iota(jnp.int32, (units, UNIT), 0)
    lane_at = lax.broadcasted_iota(jnp.int32, (units, UNIT), 1)
    counted = (GS * ((unit_at - starts) * UNIT + lane_at + 1)).astype(f32)
    mean_val = sum_one / counted
    inv_std = lax.rsqrt(sum_two / counted - mean_val * mean_val + EPSILON)
    stat_ref[0, :units, :] = mean_val
    stat_ref[0, units:, :] = inv_std
    gain, bias, skip = channel_ref[:, 0:1], channel_ref[:, 1:2], channel_ref[:, 2:3]
    for unit in range(units):
        tile = x_ref[:, unit * UNIT : (unit + 1) * UNIT]
        mean_row = stat_ref[0, unit : unit + 1, :]
        std_row = stat_ref[0, units + unit : units + unit + 1, :]
        normed_ref[unit * GS : (unit + 1) * GS, :] = (tile - mean_row) * std_row * gain + bias

    def first_pass(step, unused):
        first = step * BATCH
        many = range(BATCH)
        base = pl.multiple_of(first * STATES, BATCH * STATES)
        params = [state_ref[pl.ds(base + one * STATES, STATES), :] for one in many]
        series = [halves(normed_ref[pl.ds(first + one, units, stride=GS), :]) for one in many]
        tables = [power_tables(params[one][:, 0:1], params[one][:, 1:2]) for one in many]
        ends, mixers, matrices, kernel_rows = [], [], [], []
        for one in many:
            turn_re, turn_im = params[one][:, 0:1], params[one][:, 1:2]
            in_coeff, out_re, out_im = (params[one][:, at : at + 1] for at in (2, 3, 4))
            up_re, up_im, down_re, down_im, _, _ = tables[one]
            out_up_re = out_re * up_re - out_im * up_im
            out_up_im = out_re * up_im + out_im * up_re
            kernel_rows.append(jnp.sum(in_coeff * out_up_re, axis=0, keepdims=True))
            mixers.append(
                jnp.concatenate(
                    [
                        turn_re * out_up_re - turn_im * out_up_im,
                        -(turn_re * out_up_im + turn_im * out_up_re),
                    ],
                    axis=0,
                )
            )
            feed = jnp.concatenate([in_coeff * down_re, in_coeff * down_im], axis=0)
            ends.append(dot_split(halves(feed), series[one], NT))
        starts_row = start_row[...]
        held_re, held_im = state_scan(
            jnp.concatenate([part[:STATES] for part in ends], axis=0),
            jnp.concatenate([part[STATES:] for part in ends], axis=0),
            jnp.concatenate([part[4][:, :units] for part in tables], axis=0),
            jnp.concatenate([part[5][:, :units] for part in tables], axis=0),
            lambda lanes, distance: (lanes - distance) >= starts_row,
            units,
            1,
        )
        smoothed = []
        for one in many:
            span = slice(one * STATES, (one + 1) * STATES)
            held = jnp.concatenate([held_re[span], held_im[span]], axis=0)
            smoothed.append(
                dot_split(series[one], halves(toeplitz(kernel_rows[one])), NN)
                + dot_split(halves(held), halves(mixers[one]), TN)
            )
        for index in range(4):
            table_ref[index, pl.ds(base, BATCH * STATES), :] = jnp.concatenate(
                [part[index] for part in tables], axis=0
            )
        hold_ref[0, pl.ds(base, BATCH * STATES), :] = held_re
        hold_ref[1, pl.ds(base, BATCH * STATES), :] = held_im
        for one in many:
            row_ref[pl.ds(first + one, 1), :] = kernel_rows[one]
            ends_ref[pl.ds(first + one, units, stride=GS), :] = smoothed[one]
        return unused

    lax.fori_loop(0, GS // BATCH, first_pass, 0)
    for unit in range(units):
        here = slice(unit * GS, (unit + 1) * GS)
        normed = normed_ref[here, :]
        pre_act = ends_ref[here, :] + skip * normed
        pre_ref[0, here, :] = pre_act
        device, spot = places[unit]
        across = slice(spot * UNIT, (spot + 1) * UNIT)
        span = slice(unit * UNIT, (unit + 1) * UNIT)
        plain_ref[device, 0, :, across] = x_ref[:, span].astype(jnp.bfloat16)
        plain_ref[device, 1, :, across] = teacher_ref[:, span].astype(jnp.bfloat16)
        send_ref[device, 0, :, across] = normed.astype(jnp.bfloat16)
        send_ref[device, 1, :, across] = (pre_act * jax.nn.sigmoid(pre_act)).astype(jnp.bfloat16)


def front_backward_kernel(
    places,
    units,
    start_row,
    stop_row,
    start_col,
    stop_col,
    x_ref,
    state_ref,
    channel_ref,
    grad_ref,
    direct_ref,
    pre_ref,
    stat_ref,
    table_ref,
    row_ref,
    hold_ref,
    output_ref,
    out_ref,
    state_grad_ref,
    channel_grad_ref,
    normed_ref,
    slope_ref,
    back_ref,
    sums_ref,
):
    f32 = jnp.float32
    gain, bias, skip = channel_ref[:, 0:1], channel_ref[:, 1:2], channel_ref[:, 2:3]
    skip_sum = jnp.zeros((GS, UNIT), f32)
    for unit in range(units):
        here = slice(unit * GS, (unit + 1) * GS)
        device, spot = places[unit]
        across = slice(spot * UNIT, (spot + 1) * UNIT)
        tile = x_ref[:, unit * UNIT : (unit + 1) * UNIT]
        mean_row = stat_ref[0, unit : unit + 1, :]
        std_row = stat_ref[0, units + unit : units + unit + 1, :]
        normed = (tile - mean_row) * std_row * gain + bias
        normed_ref[here, :] = normed
        pre_act = pre_ref[0, here, :]
        logistic = jax.nn.sigmoid(pre_act)
        slope = (
            grad_ref[device, 1, :, across].astype(f32)
            * logistic
            * (1.0 + pre_act * (1.0 - logistic))
        )
        slope_ref[here, :] = slope
        skip_sum = skip_sum + slope * normed
    channel_grad_ref[:, 2:3] = jnp.sum(skip_sum, axis=1, keepdims=True)

    lag = lax.broadcasted_iota(jnp.int32, (STATES, UNIT), 1).astype(f32)

    def channel_pass(step, unused):
        first = step * BATCH_BACK
        many = range(BATCH_BACK)
        base = pl.multiple_of(first * STATES, BATCH_BACK * STATES)

        def pick(ref_at):
            return [ref_at[one * STATES : (one + 1) * STATES] for one in many]

        rows_here = pl.ds(base, BATCH_BACK * STATES)
        params = pick(state_ref[rows_here, :])
        up_re_all, up_im_all, down_re_all, down_im_all = (
            pick(table_ref[index, rows_here, :]) for index in range(4)
        )
        held_re_all, held_im_all = (pick(hold_ref[index, rows_here, :]) for index in range(2))
        kernel_rows = [row_ref[pl.ds(first + one, 1), :] for one in many]
        slopes = [halves(slope_ref[pl.ds(first + one, units, stride=GS), :]) for one in many]
        series = [halves(normed_ref[pl.ds(first + one, units, stride=GS), :]) for one in many]
        nexts, mixes, pulled = [], [], []
        for one in many:
            turn_re, turn_im = params[one][:, 0:1], params[one][:, 1:2]
            out_re, out_im = params[one][:, 3:4], params[one][:, 4:5]
            next_re = turn_re * up_re_all[one] - turn_im * up_im_all[one]
            next_im = turn_re * up_im_all[one] + turn_im * up_re_all[one]
            mix_re = out_re * next_re - out_im * next_im
            mix_im = out_re * next_im + out_im * next_re
            nexts.append((next_re, next_im))
            mixes.append((mix_re, mix_im))
            pulled.append(
                dot_split(halves(jnp.concatenate([mix_re, -mix_im], axis=0)), slopes[one], NT)
            )
        stops_row = stop_row[...]
        leaps_re = [jnp.broadcast_to(part[:, 5:6], (STATES, units)) for part in params]
        leaps_im = [jnp.broadcast_to(-part[:, 6:7], (STATES, units)) for part in params]
        pull_re_all, pull_im_all = state_scan(
            jnp.concatenate([part[:STATES] for part in pulled], axis=0),
            jnp.concatenate([part[STATES:] for part in pulled], axis=0),
            jnp.concatenate(leaps_re, axis=0),
            jnp.concatenate(leaps_im, axis=0),
            lambda lanes, distance: (lanes + distance) <= stops_row,
            units,
            -1,
        )
        pull_re_all, pull_im_all = pick(pull_re_all), pick(pull_im_all)
        backs, columns = [], []
        for one in many:
            in_coeff, out_re, out_im = (params[one][:, at : at + 1] for at in (2, 3, 4))
            leap_re, leap_im = params[one][:, 5:6], params[one][:, 6:7]
            up_re, up_im = up_re_all[one], up_im_all[one]
            down_re, down_im = down_re_all[one], down_im_all[one]
            (next_re, next_im), (mix_re, mix_im) = nexts[one], mixes[one]
            pull_re, pull_im = pull_re_all[one], pull_im_all[one]
            held_re, held_im = held_re_all[one], held_im_all[one]
            pull = halves(jnp.concatenate([pull_re, pull_im], axis=0))
            held = halves(jnp.concatenate([held_re, held_im], axis=0))
            feed_re, feed_im = in_coeff * down_re, in_coeff * down_im
            feed = halves(jnp.concatenate([feed_re, feed_im], axis=0))
            matrix = halves(toeplitz(kernel_rows[one]))
            backs.append(dot_split(slopes[one], matrix, NT) + dot_split(pull, feed, TN))
            lags = lag_sums(dot_split(slopes[one], reversed_lanes(series[one]), TN))
            mix_grad = dot_split(held, slopes[one], NN)
            feed_grad = dot_split(pull, series[one], NN)
            mg_re, mg_im = mix_grad[:STATES], -mix_grad[STATES:]
            fg_re, fg_im = feed_grad[:STATES], feed_grad[STATES:]
            leap_grad_re = held_re * pull_re + held_im * pull_im
            leap_grad_im = held_re * pull_im - held_im * pull_re
            leap_grad_re = jnp.sum(leap_grad_re, axis=1, keepdims=True)
            leap_grad_im = jnp.sum(leap_grad_im, axis=1, keepdims=True)
            lag_up_re, lag_up_im = lags * up_re, lags * up_im
            out_grad_re = jnp.sum(
                in_coeff * lag_up_re + mg_re * next_re + mg_im * next_im, axis=1, keepdims=True
            )
            out_grad_im = jnp.sum(
                -in_coeff * lag_up_im + mg_im * next_re - mg_re * next_im, axis=1, keepdims=True
            )
            tap_re = out_re * lag_up_re - out_im * lag_up_im
            tap_im = out_re * lag_up_im + out_im * lag_up_re
            in_grad = jnp.sum(tap_re + fg_re * down_re + fg_im * down_im, axis=1, keepdims=True)
            log_re = jnp.sum(
                lag * in_coeff * tap_re
                + (lag + 1.0) * (mix_re * mg_re + mix_im * mg_im)
                + (UNIT - 1.0 - lag) * (feed_re * fg_re + feed_im * fg_im),
                axis=1,
                keepdims=True,
            ) + UNIT * (leap_re * leap_grad_re + leap_im * leap_grad_im)
            log_im = jnp.sum(
                -lag * in_coeff * tap_im
                + (lag + 1.0) * (mix_re * mg_im - mix_im * mg_re)
                + (UNIT - 1.0 - lag) * (feed_re * fg_im - feed_im * fg_re),
                axis=1,
                keepdims=True,
            ) + UNIT * (leap_re * leap_grad_im - leap_im * leap_grad_re)
            columns.append((log_re, log_im, in_grad, out_grad_re, out_grad_im))
        for one in many:
            back_ref[pl.ds(first + one, units, stride=GS), :] = backs[one]
        for index in range(5):
            state_grad_ref[rows_here, index : index + 1] = jnp.concatenate(
                [part[index] for part in columns], axis=0
            )
        return unused

    lax.fori_loop(0, GS // BATCH_BACK, channel_pass, 0)

    gain_sum = jnp.zeros((GS, UNIT), f32)
    bias_sum = jnp.zeros((GS, UNIT), f32)
    for unit in range(units):
        here = slice(unit * GS, (unit + 1) * GS)
        device, spot = places[unit]
        across = slice(spot * UNIT, (spot + 1) * UNIT)
        tile = x_ref[:, unit * UNIT : (unit + 1) * UNIT]
        mean_row = stat_ref[0, unit : unit + 1, :]
        std_row = stat_ref[0, units + unit : units + unit + 1, :]
        plain = (tile - mean_row) * std_row
        total = (
            grad_ref[device, 0, :, across].astype(f32)
            + skip * slope_ref[here, :]
            + back_ref[here, :]
        )
        gain_sum = gain_sum + total * plain
        bias_sum = bias_sum + total
        scaled = total * gain
        back_ref[here, :] = scaled
        sums_ref[unit : unit + 1, :] = jnp.sum(scaled, axis=0, keepdims=True)
        sums_ref[units + unit : units + unit + 1, :] = jnp.sum(
            scaled * plain, axis=0, keepdims=True
        )
    channel_grad_ref[:, 0:1] = jnp.sum(gain_sum, axis=1, keepdims=True)
    channel_grad_ref[:, 1:2] = jnp.sum(bias_sum, axis=1, keepdims=True)
    mean_val, inv_std = stat_ref[0, :units, :], stat_ref[0, units:, :]
    var_grad = -0.5 * inv_std * inv_std * sums_ref[units:, :]
    mean_grad = -inv_std * sums_ref[:units, :] - 2.0 * mean_val * var_grad
    unit_at = lax.broadcasted_iota(jnp.int32, (units, UNIT), 0)
    lane_at = lax.broadcasted_iota(jnp.int32, (units, UNIT), 1)
    counted = (GS * ((unit_at - start_col[...]) * UNIT + lane_at + 1)).astype(f32)
    sums_ref[:units, :] = mean_grad / counted
    sums_ref[units:, :] = var_grad / counted
    rows = lax.broadcasted_iota(jnp.int32, (UNIT, UNIT), 0)
    lanes = lax.broadcasted_iota(jnp.int32, (UNIT, UNIT), 1)
    inside = dot_exact(sums_ref[...], (rows >= lanes).astype(f32))
    sooner = lax.broadcasted_iota(jnp.int32, (units, units), 0)
    later = lax.broadcasted_iota(jnp.int32, (units, units), 1)
    after = ((later > sooner) & (later <= stop_col[...])).astype(f32)
    totals = jnp.broadcast_to(inside[:, 0:1], (2 * units, UNIT))
    sums_ref[:units, :] = inside[:units] + dot_exact(after, totals[:units])
    sums_ref[units:, :] = 2.0 * (inside[units:] + dot_exact(after, totals[units:]))
    for unit in range(units):
        here = slice(unit * GS, (unit + 1) * GS)
        device, spot = places[unit]
        across = slice(spot * UNIT, (spot + 1) * UNIT)
        span = slice(unit * UNIT, (unit + 1) * UNIT)
        out_ref[:, span] = (
            back_ref[here, :] * stat_ref[0, units + unit : units + unit + 1, :]
            + sums_ref[unit : unit + 1, :]
            + x_ref[:, span] * sums_ref[units + unit : units + unit + 1, :]
            + direct_ref[device, 0, :, across].astype(f32)
        )
        output_ref[:, span] = direct_ref[device, 1, :, across].astype(f32)


def sequence_bounds(block_first, blocks, units):
    per_block = units // blocks
    index = jnp.arange(units, dtype=jnp.int32)
    begins = jnp.where(
        (index % per_block == 0) & (jnp.repeat(block_first, per_block) == 1), index, 0
    )
    starts = lax.cummax(begins)
    is_start = (index % per_block == 0) & (jnp.repeat(block_first, per_block) == 1)
    following = jnp.where(is_start, index - 1, units - 1)
    shifted = jnp.concatenate([following[1:], jnp.full((1,), units - 1, jnp.int32)])
    stops = lax.cummin(shifted, reverse=True)
    return starts, stops


def whole(shape):
    return pl.BlockSpec(shape, lambda group: (0,) * len(shape))


def front_forward(layer_input, teacher, state_params, channel_params, bounds, places, devices):
    channels, slots = layer_input.shape
    units = slots // UNIT
    tokens = slots // devices
    groups = channels // GS
    starts, stops = bounds
    f32 = jnp.float32
    return pl.pallas_call(
        partial(front_forward_kernel, places, units),
        grid=(groups,),
        in_specs=[
            whole((1, units)),
            whole((units, 1)),
            pl.BlockSpec((GS, slots), lambda group: (group, 0)),
            pl.BlockSpec((GS, slots), lambda group: (group, 0)),
            pl.BlockSpec((GS * STATES, 8), lambda group: (group, 0)),
            pl.BlockSpec((GS, 8), lambda group: (group, 0)),
        ],
        out_specs=[
            pl.BlockSpec((devices, 2, GS, tokens), lambda group: (0, 0, group, 0)),
            pl.BlockSpec((devices, 2, GS, tokens), lambda group: (0, 0, group, 0)),
            pl.BlockSpec((1, units * GS, UNIT), lambda group: (group, 0, 0)),
            pl.BlockSpec((1, 2 * units, UNIT), lambda group: (group, 0, 0)),
            pl.BlockSpec((4, GS * STATES, UNIT), lambda group: (0, group, 0)),
            pl.BlockSpec((GS, UNIT), lambda group: (group, 0)),
            pl.BlockSpec((2, GS * STATES, units), lambda group: (0, group, 0)),
        ],
        out_shape=[
            jax.ShapeDtypeStruct((devices, 2, channels, tokens), jnp.bfloat16),
            jax.ShapeDtypeStruct((devices, 2, channels, tokens), jnp.bfloat16),
            jax.ShapeDtypeStruct((groups, units * GS, UNIT), f32),
            jax.ShapeDtypeStruct((groups, 2 * units, UNIT), f32),
            jax.ShapeDtypeStruct((4, channels * STATES, UNIT), f32),
            jax.ShapeDtypeStruct((channels, UNIT), f32),
            jax.ShapeDtypeStruct((2, channels * STATES, units), f32),
        ],
        scratch_shapes=[
            pltpu.VMEM((units * GS, UNIT), f32),
            pltpu.VMEM((2 * units, UNIT), f32),
            pltpu.VMEM((units * GS, UNIT), f32),
        ],
        cost_estimate=pl.CostEstimate(
            flops=channels * slots * 60000, bytes_accessed=channels * slots * 24, transcendentals=0
        ),
        name="front_forward",
    )(starts[None, :], starts[:, None], layer_input, teacher, state_params, channel_params)


def front_backward(
    layer_input, state_params, channel_params, bounds, places, devices, grads, direct, saved
):
    channels, slots = layer_input.shape
    units = slots // UNIT
    tokens = slots // devices
    groups = channels // GS
    starts, stops = bounds
    f32 = jnp.float32
    return pl.pallas_call(
        partial(front_backward_kernel, places, units),
        grid=(groups,),
        in_specs=[
            whole((1, units)),
            whole((1, units)),
            whole((units, 1)),
            whole((units, 1)),
            pl.BlockSpec((GS, slots), lambda group: (group, 0)),
            pl.BlockSpec((GS * STATES, 8), lambda group: (group, 0)),
            pl.BlockSpec((GS, 8), lambda group: (group, 0)),
            pl.BlockSpec((devices, 2, GS, tokens), lambda group: (0, 0, group, 0)),
            pl.BlockSpec((devices, 2, GS, tokens), lambda group: (0, 0, group, 0)),
            pl.BlockSpec((1, units * GS, UNIT), lambda group: (group, 0, 0)),
            pl.BlockSpec((1, 2 * units, UNIT), lambda group: (group, 0, 0)),
            pl.BlockSpec((4, GS * STATES, UNIT), lambda group: (0, group, 0)),
            pl.BlockSpec((GS, UNIT), lambda group: (group, 0)),
            pl.BlockSpec((2, GS * STATES, units), lambda group: (0, group, 0)),
        ],
        out_specs=[
            pl.BlockSpec((GS, slots), lambda group: (group, 0)),
            pl.BlockSpec((GS, slots), lambda group: (group, 0)),
            pl.BlockSpec((GS * STATES, 8), lambda group: (group, 0)),
            pl.BlockSpec((GS, 8), lambda group: (group, 0)),
        ],
        out_shape=[
            jax.ShapeDtypeStruct((channels, slots), f32),
            jax.ShapeDtypeStruct((channels, slots), f32),
            jax.ShapeDtypeStruct((channels * STATES, 8), f32),
            jax.ShapeDtypeStruct((channels, 8), f32),
        ],
        scratch_shapes=[
            pltpu.VMEM((units * GS, UNIT), f32),
            pltpu.VMEM((units * GS, UNIT), f32),
            pltpu.VMEM((units * GS, UNIT), f32),
            pltpu.VMEM((2 * units, UNIT), f32),
        ],
        cost_estimate=pl.CostEstimate(
            flops=channels * slots * 140000, bytes_accessed=channels * slots * 32, transcendentals=0
        ),
        name="front_backward",
    )(
        starts[None, :],
        stops[None, :],
        starts[:, None],
        stops[:, None],
        layer_input,
        state_params,
        channel_params,
        grads,
        direct,
        *saved,
    )


def front_parameters(rate, angle, ema_in, out_re, out_im, gain, bias, skip):
    magnitude = 1.0 - rate
    leap = jnp.exp(UNIT * jnp.log(magnitude))
    columns = [
        magnitude * jnp.cos(angle),
        magnitude * jnp.sin(angle),
        jnp.sqrt(2.0 * rate) * ema_in,
        out_re,
        out_im,
        leap * jnp.cos(UNIT * angle),
        leap * jnp.sin(UNIT * angle),
        rate,
    ]
    states = jnp.stack(columns, axis=-1).reshape(-1, 8)
    channels = jnp.stack([gain, bias, skip] + [skip] * 5, axis=-1)
    return states, channels


def front_parameter_grads(state_grads, channel_grads, rate, ema_in):
    shaped = state_grads.reshape(rate.shape + (8,))
    log_re, log_im, in_grad = shaped[..., 0], shaped[..., 1], shaped[..., 2]
    root = jnp.sqrt(2.0 * rate)
    return (
        channel_grads[:, 0],
        channel_grads[:, 1],
        in_grad * ema_in / root - log_re / (1.0 - rate),
        log_im,
        in_grad * root,
        shaped[..., 3],
        shaped[..., 4],
        channel_grads[:, 2],
    )


def unit_places(slots, devices, blocks):
    units = slots // UNIT
    per_block = units // blocks
    group = devices // blocks
    per_device = per_block // group
    places = [None] * units
    for block in range(blocks):
        for member in range(group):
            if per_device % 2 == 0:
                half = per_device // 2
                mirror = 2 * group - 1 - member
                owned = [member * half + step for step in range(half)]
                owned += [mirror * half + step for step in range(half)]
            else:
                owned = [member * per_device + step for step in range(per_device)]
            for spot, unit in enumerate(owned):
                places[block * per_block + unit] = (block * group + member, spot)
    return places


def chunk_sites(group, tokens):
    if tokens % (2 * UNIT) == 0:
        half = tokens // 2
        sites = [(member, 0) for member in range(group)]
        sites += [(2 * group - 1 - chunk, half) for chunk in range(group, 2 * group)]
        return half, sites
    return tokens, [(member, 0) for member in range(group)]


def query_pieces(group, tokens, member):
    half, sites = chunk_sites(group, tokens)
    if half < tokens:
        return half, [(member, 0), (2 * group - 1 - member, half)]
    return half, [(member, 0)]


def masked_scores(turned, keys, allowed, scale):
    products = lax.dot_general(turned, keys, NN, preferred_element_type=jnp.float32) * scale
    return jnp.where(allowed, products, NEGATIVE)


def causal_tile(size, key_chunk, query_chunk):
    rows = lax.broadcasted_iota(jnp.int32, (size, size), 0)
    lanes = lax.broadcasted_iota(jnp.int32, (size, size), 1)
    return (lanes <= rows) | (key_chunk < query_chunk)


def attention_forward_kernel(
    group, member_ref, query_ref, keep_ref, out_ref, log_ref, score_ref, prob_ref
):
    f32, bf16 = jnp.float32, jnp.bfloat16
    tokens = query_ref.shape[1]
    width = out_ref.shape[0]
    member = member_ref[0]
    half, pieces = query_pieces(group, tokens, member)
    _, sites = chunk_sites(group, tokens)
    scale = Z ** (-0.5)
    for chunk, offset in pieces:
        turned = query_ref[:, offset : offset + half].astype(f32).T.astype(bf16)
        log_ref[offset : offset + half, :] = jnp.full((half, UNIT), NEGATIVE, f32)
        out_ref[:, offset : offset + half] = jnp.zeros((width, half), f32)
        for index, (owner, start) in enumerate(sites):

            @pl.when(index <= chunk)
            def _():
                keys = keep_ref[owner, width:, start : start + half]
                scores = masked_scores(turned, keys, causal_tile(half, index, chunk), scale)
                score_ref[index] = scores
                log_ref[offset : offset + half, :] = jnp.maximum(
                    log_ref[offset : offset + half, :], jnp.max(scores, axis=1, keepdims=True)
                )

        tops = log_ref[offset : offset + half, 0:1]
        prob_ref[:, 0:1] = jnp.zeros((half, 1), f32)
        for index in range(len(sites)):

            @pl.when(index <= chunk)
            def _():
                exponent = jnp.exp(score_ref[index] - tops)
                score_ref[index] = exponent
                prob_ref[:, 0:1] += jnp.sum(exponent, axis=1, keepdims=True)

        totals = prob_ref[:, 0:1]
        log_ref[offset : offset + half, :] = jnp.broadcast_to(
            tops + jnp.log(totals), (half, UNIT)
        )
        for index, (owner, start) in enumerate(sites):

            @pl.when(index <= chunk)
            def _():
                probs = (score_ref[index] / totals).astype(bf16)
                values = keep_ref[owner, :width, start : start + half]
                out_ref[:, offset : offset + half] += lax.dot_general(
                    values, probs, NT, preferred_element_type=f32
                )


def attention_backward_kernel(
    group,
    member_ref,
    query_ref,
    keep_ref,
    grad_ref,
    log_ref,
    query_grad_ref,
    out_ref,
    prob_ref,
    slope_ref,
    low_ref,
    score_grad_ref,
    dot_ref,
    turned_ref,
):
    f32, bf16 = jnp.float32, jnp.bfloat16
    tokens = query_ref.shape[1]
    width = grad_ref.shape[0]
    member = member_ref[0]
    half, pieces = query_pieces(group, tokens, member)
    _, sites = chunk_sites(group, tokens)
    scale = Z ** (-0.5)
    for which, (chunk, offset) in enumerate(pieces):
        here = slice(offset, offset + half)
        turned = query_ref[:, here].astype(f32).T.astype(bf16)
        for start in range(0, width, half):
            turned_ref[:, start : start + half] = (
                grad_ref[start : start + half, here].astype(f32).T.astype(bf16)
            )
        logs = log_ref[here, 0:1]
        dot_ref[...] = jnp.zeros(dot_ref.shape, f32)
        query_grad_ref[:, here] = jnp.zeros((Z, half), f32)
        for index, (owner, start) in enumerate(sites):

            @pl.when(index <= chunk)
            def _():
                keys = keep_ref[owner, width:, start : start + half]
                scores = masked_scores(turned, keys, causal_tile(half, index, chunk), scale)
                probs = jnp.exp(scores - logs)
                prob_ref[index] = probs
                low_ref[which, index] = probs.astype(bf16)
                slope = lax.dot_general(
                    turned_ref[...],
                    keep_ref[owner, :width, start : start + half],
                    NN,
                    preferred_element_type=f32,
                )
                slope_ref[index] = slope
                dot_ref[:, 0:1] += jnp.sum(probs * slope, axis=1, keepdims=True)

        dots = dot_ref[:, 0:1]
        for index, (owner, start) in enumerate(sites):

            @pl.when(index <= chunk)
            def _():
                score_grad = (prob_ref[index] * (slope_ref[index] - dots)).astype(bf16)
                score_grad_ref[which, index] = score_grad
                keys = keep_ref[owner, width:, start : start + half]
                query_grad_ref[:, here] += (
                    lax.dot_general(keys, score_grad, NT, preferred_element_type=f32) * scale
                )

    last = pieces[-1]
    for index, (owner, start) in enumerate(sites):
        there = slice(start, start + half)

        def emit(used):
            value_sum, key_sum = None, None
            for which in used:
                offset = pieces[which][1]
                here = slice(offset, offset + half)
                value_part = lax.dot_general(
                    grad_ref[:, here], low_ref[which, index], NN, preferred_element_type=f32
                )
                key_part = lax.dot_general(
                    query_ref[:, here], score_grad_ref[which, index], NN, preferred_element_type=f32
                )
                value_sum = value_part if value_sum is None else value_sum + value_part
                key_sum = key_part if key_sum is None else key_sum + key_part
            out_ref[owner, :width, there] = value_sum.astype(bf16)
            out_ref[owner, width:, there] = (key_sum * scale).astype(bf16)

        if len(pieces) == 2:

            @pl.when(index <= pieces[0][0])
            def _():
                emit((0, 1))

            @pl.when((index > pieces[0][0]) & (index <= last[0]))
            def _():
                emit((1,))

        else:

            @pl.when(index <= last[0])
            def _():
                emit((0,))

        @pl.when(index > last[0])
        def _():
            out_ref[owner, :, there] = jnp.zeros((out_ref.shape[1], half), bf16)


VMEM_BUDGET = 60 * 1024 * 1024


def attention_forward(member, queries, key_values, group):
    tokens = queries.shape[1]
    width = key_values.shape[1] - queries.shape[0]
    half, sites = chunk_sites(group, tokens)
    f32 = jnp.float32
    vmem = pl.BlockSpec(memory_space=pltpu.VMEM)
    return pl.pallas_call(
        partial(attention_forward_kernel, group),
        in_specs=[pl.BlockSpec(memory_space=pltpu.SMEM), vmem, vmem],
        out_specs=[vmem, vmem],
        out_shape=[
            jax.ShapeDtypeStruct((width, tokens), f32),
            jax.ShapeDtypeStruct((tokens, UNIT), f32),
        ],
        scratch_shapes=[
            pltpu.VMEM((len(sites), half, half), f32),
            pltpu.VMEM((half, UNIT), f32),
        ],
        compiler_params=pltpu.CompilerParams(vmem_limit_bytes=VMEM_BUDGET),
        cost_estimate=pl.CostEstimate(
            flops=2 * tokens * tokens * group * (width + Z),
            bytes_accessed=2 * key_values.size + 4 * width * tokens,
            transcendentals=tokens * tokens * group,
        ),
        name="attention_forward",
    )(member, queries, key_values)


def attention_backward(member, queries, key_values, grads, logs, group):
    tokens = queries.shape[1]
    half, sites = chunk_sites(group, tokens)
    count = tokens // half
    f32, bf16 = jnp.float32, jnp.bfloat16
    vmem = pl.BlockSpec(memory_space=pltpu.VMEM)
    return pl.pallas_call(
        partial(attention_backward_kernel, group),
        in_specs=[pl.BlockSpec(memory_space=pltpu.SMEM), vmem, vmem, vmem, vmem],
        out_specs=[vmem, vmem],
        out_shape=[
            jax.ShapeDtypeStruct(queries.shape, f32),
            jax.ShapeDtypeStruct(key_values.shape, bf16),
        ],
        scratch_shapes=[
            pltpu.VMEM((len(sites), half, half), f32),
            pltpu.VMEM((len(sites), half, half), f32),
            pltpu.VMEM((count, len(sites), half, half), bf16),
            pltpu.VMEM((count, len(sites), half, half), bf16),
            pltpu.VMEM((half, UNIT), f32),
            pltpu.VMEM((half, grads.shape[0]), bf16),
        ],
        compiler_params=pltpu.CompilerParams(vmem_limit_bytes=VMEM_BUDGET),
        cost_estimate=pl.CostEstimate(
            flops=4 * tokens * tokens * group * (grads.shape[0] + Z),
            bytes_accessed=4 * key_values.size,
            transcendentals=tokens * tokens * group,
        ),
        name="attention_backward",
    )(member, queries, key_values, grads, logs)


PIECES = 4


def meet_neighbours(side, across):
    barrier = pltpu.get_barrier_semaphore()
    for target in (side, across):
        pl.semaphore_signal(
            barrier, inc=1, device_id={"col": target}, device_id_type=pl.DeviceIdType.MESH
        )
    pl.semaphore_wait(barrier, 2)


def neighbours():
    me = lax.axis_index("col")
    return me, me + 1 - 2 * (me % 2), (me + 2) % 4


def push(source, target, send_sem, recv_sem, device):
    return pltpu.make_async_remote_copy(
        src_ref=source,
        dst_ref=target,
        send_sem=send_sem,
        recv_sem=recv_sem,
        device_id={"col": device},
        device_id_type=pl.DeviceIdType.MESH,
    )


def gather_kernel(
    own_ref, out_ref, local_sem, cross_send, cross_recv, side_send, side_recv, pass_send, pass_recv
):
    me, side, across = neighbours()
    count = own_ref.shape[0] // PIECES
    meet_neighbours(side, across)
    crossing = []
    for piece in range(PIECES):
        rows = pl.ds(piece * count, count)
        copy = push(
            own_ref.at[rows],
            out_ref.at[me, rows],
            cross_send.at[piece],
            cross_recv.at[piece],
            across,
        )
        copy.start()
        crossing.append(copy)
    beside = push(own_ref, out_ref.at[me], side_send, side_recv, side)
    beside.start()
    local = pltpu.make_async_copy(own_ref, out_ref.at[me], local_sem)
    local.start()
    passing = []
    for piece in range(PIECES):
        rows = pl.ds(piece * count, count)
        crossing[piece].wait_recv()
        copy = push(
            out_ref.at[across, rows],
            out_ref.at[across, rows],
            pass_send.at[piece],
            pass_recv.at[piece],
            side,
        )
        copy.start()
        passing.append(copy)
    for piece in range(PIECES):
        crossing[piece].wait_send()
        passing[piece].wait()
    beside.wait()
    local.wait()


def gather_members(own):
    dma = pltpu.SemaphoreType.DMA
    anywhere = pl.BlockSpec(memory_space=pl.ANY)
    return pl.pallas_call(
        gather_kernel,
        in_specs=[anywhere],
        out_specs=anywhere,
        out_shape=jax.ShapeDtypeStruct((4,) + own.shape, own.dtype),
        scratch_shapes=[
            dma,
            dma((PIECES,)),
            dma((PIECES,)),
            dma,
            dma,
            dma((PIECES,)),
            dma((PIECES,)),
        ],
        compiler_params=pltpu.CompilerParams(collective_id=0, has_side_effects=True),
        name="gather_members",
    )(own)


def reduce_kernel(
    parts_ref,
    out_ref,
    beside_ref,
    sum_ref,
    landed_ref,
    first_send,
    first_recv,
    second_send,
    second_recv,
    cross_send,
    cross_recv,
):
    f32, bf16 = jnp.float32, jnp.bfloat16
    me, side, across = neighbours()
    count = out_ref.shape[0] // PIECES
    beyond = (side + 2) % 4
    meet_neighbours(side, across)
    first, second, crossing = [], [], []
    for piece in range(PIECES):
        rows = pl.ds(piece * count, count)
        copy = push(
            parts_ref.at[beyond, rows],
            beside_ref.at[0, rows],
            first_send.at[piece],
            first_recv.at[piece],
            side,
        )
        copy.start()
        first.append(copy)
    for piece in range(PIECES):
        rows = pl.ds(piece * count, count)
        copy = push(
            parts_ref.at[side, rows],
            beside_ref.at[1, rows],
            second_send.at[piece],
            second_recv.at[piece],
            side,
        )
        copy.start()
        second.append(copy)
    for piece in range(PIECES):
        rows = pl.ds(piece * count, count)
        first[piece].wait_recv()
        total = parts_ref[across, rows, :].astype(f32) + beside_ref[0, rows, :].astype(f32)
        sum_ref[rows, :] = total.astype(bf16)
        copy = push(
            sum_ref.at[rows],
            landed_ref.at[rows],
            cross_send.at[piece],
            cross_recv.at[piece],
            across,
        )
        copy.start()
        crossing.append(copy)
    for piece in range(PIECES):
        rows = pl.ds(piece * count, count)
        second[piece].wait_recv()
        crossing[piece].wait_recv()
        out_ref[rows, :] = (
            parts_ref[me, rows, :].astype(f32)
            + beside_ref[1, rows, :].astype(f32)
            + landed_ref[rows, :].astype(f32)
        )
    for piece in range(PIECES):
        first[piece].wait_send()
        second[piece].wait_send()
        crossing[piece].wait_send()


def reduce_members(parts):
    dma = pltpu.SemaphoreType.DMA
    vmem = pl.BlockSpec(memory_space=pltpu.VMEM)
    shape = parts.shape[1:]
    return pl.pallas_call(
        reduce_kernel,
        in_specs=[vmem],
        out_specs=vmem,
        out_shape=jax.ShapeDtypeStruct(shape, jnp.float32),
        scratch_shapes=[
            pltpu.VMEM((2,) + shape, parts.dtype),
            pltpu.VMEM(shape, parts.dtype),
            pltpu.VMEM(shape, parts.dtype),
        ]
        + [dma((PIECES,))] * 6,
        compiler_params=pltpu.CompilerParams(
            collective_id=1, has_side_effects=True, vmem_limit_bytes=VMEM_BUDGET
        ),
        name="reduce_members",
    )(parts)


def silu_slope(pre_act):
    logistic = jax.nn.sigmoid(pre_act)
    return logistic * (1.0 + pre_act * (1.0 - logistic))


def contract_first(left_in, right_in):
    return lax.dot_general(
        left_in, right_in, (((0,), (0,)), ((), ())), preferred_element_type=jnp.float32
    )


def contract_last(left_in, right_in):
    return lax.dot_general(
        left_in, right_in, (((1,), (1,)), ((), ())), preferred_element_type=jnp.float32
    )


def silu(pre_act):
    return pre_act * jax.nn.sigmoid(pre_act)


def swap_blocks(array_in, outer, inner):
    shaped = array_in.reshape(outer, inner, -1, array_in.shape[-1])
    return shaped.transpose(1, 0, 2, 3).reshape(array_in.shape)


def project(weights, source):
    return jnp.concatenate(
        [contract_first(weights[part], source) for part in range(weights.shape[0])], axis=0
    )


def project_back(weights, grads):
    parts = weights.shape[0]
    pieces = grads.reshape(parts, -1, grads.shape[-1])
    total = None
    for part in range(parts):
        product = jnp.dot(weights[part], pieces[part], preferred_element_type=jnp.float32)
        total = product if total is None else total + product
    return total


def weight_products(source, grads, parts):
    pieces = grads.reshape(parts, -1, grads.shape[-1])
    return [contract_last(source, pieces[part]).astype(jnp.bfloat16) for part in range(parts)]


def shards(
    layer_input,
    teacher,
    block_len,
    block_first,
    norm_gain,
    norm_bias,
    ema_rate,
    ema_angle,
    ema_input,
    ema_out_real,
    ema_out_imag,
    ema_skip,
    w_value,
    w_shared,
    w_reset,
    w_hidden,
    w_update,
    query_gain,
    query_bias,
    key_gain,
    w_output,
    final_gain,
    final_bias,
    w_gate,
    w_up,
    w_down,
):
    bf16 = jnp.bfloat16
    grid = ("row", "col")
    rows, cols, dps = lax.axis_size("row"), lax.axis_size("col"), lax.axis_size("dp")
    devices = rows * cols
    slot_count = layer_input.shape[1]
    blocks_here = slot_count // SPAN
    group = devices // blocks_here
    tokens = slot_count // devices
    place = lax.axis_index("row") * cols + lax.axis_index("col")
    my_block = place // group
    member = place % group
    places = unit_places(slot_count, devices, blocks_here)
    state_params, channel_params = front_parameters(
        ema_rate,
        ema_angle,
        ema_input,
        ema_out_real,
        ema_out_imag,
        norm_gain,
        norm_bias,
        ema_skip,
    )
    bounds = sequence_bounds(block_first, blocks_here, slot_count // UNIT)

    def exchange(array_in):
        return lax.all_to_all(array_in, grid, 0, 0, tiled=True)

    def gather_weights(local):
        gathered = lax.all_gather(local, grid, axis=0)
        return gathered.reshape(rows, -1, local.shape[-1])

    def local_matrix(weight_list):
        flat = [weight.reshape(-1, weight.shape[-1]) for weight in weight_list]
        return flat[0] if len(flat) == 1 else jnp.concatenate(flat, axis=1)

    barrier = lax.optimization_barrier
    vectors = exchange(
        jnp.broadcast_to(
            jnp.concatenate([final_gain, final_bias, query_gain, query_bias, key_gain])[None],
            (devices, 2 * final_gain.shape[0] + 3 * query_gain.shape[0]),
        )
    )
    valid_here = jnp.sum(block_len).astype(jnp.float32)
    valid_all = lax.psum(jnp.broadcast_to(valid_here, (COUNT_ROWS, D)), "dp")
    valid_total = valid_all[0, 0]
    parts_out = w_output.shape[2] // w_value.shape[2]
    output_local = w_output.reshape(rows, parts_out, w_value.shape[2], -1)
    output_local = [output_local[:, part].reshape(-1, w_output.shape[-1]) for part in range(parts_out)]
    value_weights = gather_weights(local_matrix([w_value, w_shared]))
    rest_weights = gather_weights(
        jnp.concatenate(output_local + [local_matrix([w_reset, w_hidden, w_update])], axis=1)
    )
    inner_weights = gather_weights(local_matrix([w_gate, w_up]))
    down_weights = gather_weights(local_matrix([w_down]))
    feat_share, z_share = final_gain.shape[0], query_gain.shape[0]

    def whole_vector(start, share):
        return vectors[:, start : start + share].reshape(-1)

    gain_all = whole_vector(0, feat_share)
    bias_all = whole_vector(feat_share, feat_share)
    query_gain_all = whole_vector(2 * feat_share, z_share)
    query_bias_all = whole_vector(2 * feat_share + z_share, z_share)
    key_gain_all = whole_vector(2 * feat_share + 2 * z_share, z_share)

    half, pieces = query_pieces(group, tokens, member)
    positions = jnp.concatenate([chunk * half + jnp.arange(half) for chunk, offset in pieces])
    valid_mask = (positions < block_len[my_block]).astype(jnp.float32)

    send, send_plain, *saved = front_forward(
        layer_input, teacher, state_params, channel_params, bounds, places, devices
    )
    sources = exchange(send)
    feats = layer_input.shape[0]
    sources = sources.reshape(rows, cols, 2, feats, tokens).transpose(2, 1, 0, 3, 4)
    sources = sources.reshape(2, devices * feats, tokens)
    normed_low, mixed_low = sources[0], sources[1]
    n_value, n_shared, n_reset, n_hidden = (
        weight.shape[-1] for weight in (w_value, w_shared, w_reset, w_hidden)
    )
    n_out = w_output.shape[-1]
    skip_out = parts_out * n_out
    value_pre = project(value_weights[:, :, :n_value], normed_low)
    shared = project(value_weights[:, :, n_value:], mixed_low)
    mixed_out = [
        contract_first(rest_weights[part, :, skip_out:], mixed_low) for part in range(rows)
    ]

    def mixed_slice(start, count):
        return jnp.concatenate([piece[start : start + count] for piece in mixed_out], axis=0)

    reset_pre = mixed_slice(0, n_reset)
    hidden_pre = mixed_slice(n_reset, n_hidden)
    update_pre = mixed_slice(n_reset + n_hidden, n_hidden)
    values_low = silu(value_pre).astype(bf16)
    queries = (shared * query_gain_all[:, None] + query_bias_all[:, None]).astype(bf16)
    keys_low = (shared * key_gain_all[:, None]).astype(bf16)
    key_values = jnp.concatenate([values_low, keys_low], axis=0)
    near = rows == blocks_here and cols == 4
    if near:
        gathered_kv = gather_members(key_values)
    else:
        gathered_kv = lax.dynamic_slice_in_dim(
            lax.all_gather(key_values, grid, axis=0), my_block * group, group, 0
        )
    width = values_low.shape[0]
    send_plain, gathered_kv = barrier((send_plain, gathered_kv))
    plain = exchange(send_plain)
    plain = plain.astype(jnp.float32)
    input_slots = plain[:, 0].reshape(devices * feats, tokens)
    teacher_slots = plain[:, 1].reshape(devices * feats, tokens)

    attended, logs = attention_forward(member[None], queries, gathered_kv, group)
    reset_act = silu(reset_pre)
    att_in = (attended * reset_act).astype(bf16)
    att_in = att_in.reshape(rows, cols, parts_out, -1, tokens).transpose(2, 1, 0, 3, 4)
    att_in = att_in.reshape(parts_out, -1, tokens)
    summed = hidden_pre
    for part in range(parts_out):
        summed = summed + project(
            rest_weights[:, :, part * n_out : (part + 1) * n_out], att_in[part]
        )
    hidden_act = silu(summed)
    gate_act = jax.nn.sigmoid(update_pre)
    first_out = input_slots + gate_act * (hidden_act - input_slots)
    mean_val = jnp.mean(first_out, axis=0)
    inv_std = lax.rsqrt(jnp.mean(first_out * first_out, axis=0) - mean_val * mean_val + EPSILON)
    unit_norm = (first_out - mean_val) * inv_std
    final_norm = swap_blocks(
        (unit_norm * gain_all[:, None] + bias_all[:, None]).astype(bf16), rows, cols
    )
    n_inner = w_gate.shape[-1]
    inner_out = [contract_first(inner_weights[part], final_norm) for part in range(rows)]
    gate_pre = jnp.concatenate([piece[:n_inner] for piece in inner_out], axis=0)
    up_pre = jnp.concatenate([piece[n_inner:] for piece in inner_out], axis=0)
    inner_act = swap_blocks((silu(gate_pre) * up_pre).astype(bf16), rows, cols)
    output_slots = first_out + project(down_weights, inner_act)
    out_error = (output_slots - teacher_slots) * valid_mask
    loss_part = jnp.sum(out_error * out_error)
    out_grad = out_error * (slot_count * dps / valid_total)

    out_low = out_grad.astype(bf16)
    inner_grad = swap_blocks(project_back(down_weights, out_low), cols, rows)
    gate_grad = (inner_grad * up_pre * silu_slope(gate_pre)).astype(bf16)
    up_grad = (inner_grad * silu(gate_pre)).astype(bf16)
    inner_grads = jnp.concatenate(
        [gate_grad.reshape(rows, -1, tokens), up_grad.reshape(rows, -1, tokens)], axis=1
    )
    norm_grad = swap_blocks(
        project_back(inner_weights, inner_grads.reshape(-1, tokens)), cols, rows
    )

    def scatter_weight(product_list, rank):
        stacked = jnp.stack(product_list)
        shaped = stacked.reshape(devices, rows * rank, stacked.shape[-1])
        return lax.psum_scatter(shaped, grid, scatter_dimension=0, tiled=True)[0]

    down_sum = scatter_weight(weight_products(inner_act, out_low, rows), w_down.shape[2])
    inner_sum = scatter_weight(weight_products(final_norm, inner_grads, rows), w_gate.shape[2])
    down_sum, inner_sum, valid_all = barrier((down_sum, inner_sum, valid_all))
    down_sum, inner_sum = lax.psum((down_sum, inner_sum), "dp")

    final_gain_part = jnp.sum(norm_grad * unit_norm, axis=1)
    final_bias_part = jnp.sum(norm_grad, axis=1)
    unit_grad = norm_grad * gain_all[:, None]
    first_grad = out_grad + inv_std * (
        unit_grad
        - jnp.mean(unit_grad, axis=0)
        - unit_norm * jnp.mean(unit_grad * unit_norm, axis=0)
    )
    direct = exchange(
        jnp.stack(
            [
                (first_grad * (1.0 - gate_act)).reshape(devices, feats, tokens),
                output_slots.reshape(devices, feats, tokens),
            ],
            axis=1,
        ).astype(bf16)
    )
    update_grad = (first_grad * (hidden_act - input_slots) * gate_act * (1.0 - gate_act)).astype(
        bf16
    )
    summed_grad = (first_grad * gate_act * silu_slope(summed)).astype(bf16)
    att_grad = jnp.stack(
        [
            project_back(rest_weights[:, :, part * n_out : (part + 1) * n_out], summed_grad)
            for part in range(parts_out)
        ]
    )
    att_grad = att_grad.reshape(parts_out, cols, rows, feats, tokens).transpose(2, 1, 0, 3, 4)
    att_grad = att_grad.reshape(-1, tokens)
    attended_grad = (att_grad * reset_act).astype(bf16)
    reset_grad = (att_grad * attended * silu_slope(reset_pre)).astype(bf16)
    mixed_grads = jnp.concatenate(
        [piece.reshape(rows, -1, tokens) for piece in (reset_grad, summed_grad, update_grad)],
        axis=1,
    )
    rest_products = [
        jnp.concatenate(columns, axis=1)
        for columns in zip(
            *[weight_products(att_in[part], summed_grad, rows) for part in range(parts_out)],
            weight_products(mixed_low, mixed_grads, rows),
        )
    ]
    query_grad, kv_parts = attention_backward(
        member[None], queries, gathered_kv, attended_grad, logs, group
    )
    kv_parts, direct = barrier((kv_parts, direct))
    if near:
        kv_grads = reduce_members(kv_parts)
    else:
        spread = lax.dynamic_update_slice_in_dim(
            jnp.zeros((devices,) + kv_parts.shape[1:], bf16), kv_parts, my_block * group, 0
        )
        kv_grads = lax.psum_scatter(spread, grid, scatter_dimension=0, tiled=True)[0]
    kv_grads, rest_products = barrier((kv_grads, rest_products))
    rest_sum = scatter_weight(rest_products, w_value.shape[2])
    rest_sum, down_sum, inner_sum = barrier((rest_sum, down_sum, inner_sum))
    rest_sum = lax.psum(rest_sum, "dp")
    value_grad, key_grad = kv_grads[:width].astype(jnp.float32), kv_grads[width:].astype(jnp.float32)
    value_pre_grad = (value_grad * silu_slope(value_pre)).astype(bf16)
    shared_grad = (
        query_grad * query_gain_all[:, None] + key_grad * key_gain_all[:, None]
    ).astype(bf16)
    query_gain_part = jnp.sum(query_grad * shared, axis=1)
    query_bias_part = jnp.sum(query_grad, axis=1)
    key_gain_part = jnp.sum(key_grad * shared, axis=1)
    normed_back = project_back(value_weights[:, :, :n_value], value_pre_grad)
    mixed_back = project_back(
        rest_weights[:, :, skip_out:], mixed_grads.reshape(-1, tokens)
    ) + project_back(value_weights[:, :, n_value:], shared_grad)
    backs = jnp.stack([normed_back, mixed_back]).astype(bf16)
    backs = backs.reshape(2, cols, rows, feats, tokens).transpose(2, 1, 0, 3, 4)
    backs = exchange(backs.reshape(devices, 2, feats, tokens))
    layer_output, input_grad, state_grads, channel_grads = front_backward(
        layer_input, state_params, channel_params, bounds, places, devices, backs, direct, saved
    )
    param_grads = front_parameter_grads(state_grads, channel_grads, ema_rate, ema_input)

    value_products = [
        jnp.concatenate(pair, axis=1)
        for pair in zip(
            weight_products(normed_low, value_pre_grad, rows),
            weight_products(mixed_low, shared_grad, rows),
        )
    ]
    value_sum = scatter_weight(value_products, w_value.shape[2])
    value_sum, rest_sum = barrier((value_sum, rest_sum))
    value_sum = lax.psum(value_sum, "dp")

    vector_parts = [final_gain_part, final_bias_part, query_gain_part, query_bias_part, key_gain_part]
    vector_parts = jnp.concatenate(
        [part.reshape(devices, -1) for part in vector_parts]
        + [jnp.broadcast_to(loss_part, (devices, 1))],
        axis=1,
    )
    vector_sums = jnp.sum(exchange(vector_parts), axis=0)
    *param_sums, small = lax.psum((*param_grads, vector_sums), "dp")
    loss_value = small[-1] / (2.0 * valid_total * D)

    def split_columns(array_in, weight_list):
        results = []
        offset = 0
        for weight in weight_list:
            count = weight.shape[-1]
            piece = array_in[:, offset : offset + count].astype(jnp.float32)
            results.append(piece.reshape(weight.shape))
            offset += count
        return results

    value_g, shared_g = split_columns(value_sum, [w_value, w_shared])
    reset_g, hidden_g, update_g = split_columns(
        rest_sum[:, skip_out:], [w_reset, w_hidden, w_update]
    )
    output_g = jnp.stack(
        [
            rest_sum[:, part * n_out : (part + 1) * n_out].reshape(rows, -1, n_out)
            for part in range(parts_out)
        ],
        axis=1,
    )
    output_g = output_g.astype(jnp.float32).reshape(w_output.shape)
    gate_g, up_g = split_columns(inner_sum, [w_gate, w_up])
    (down_g,) = split_columns(down_sum, [w_down])
    return (
        layer_output,
        loss_value,
        input_grad,
        *param_sums,
        value_g,
        shared_g,
        reset_g,
        hidden_g,
        update_g,
        small[2 * feat_share : 2 * feat_share + z_share],
        small[2 * feat_share + z_share : 2 * feat_share + 2 * z_share],
        small[2 * feat_share + 2 * z_share : 2 * feat_share + 3 * z_share],
        output_g,
        small[:feat_share],
        small[feat_share : 2 * feat_share],
        gate_g,
        up_g,
        down_g,
    )


def solution(mesh):
    in_specs = (
        P(("row", "col"), "dp"),
        P(("row", "col"), "dp"),
        P("dp"),
        P("dp"),
        P(("row", "col")),
        P(("row", "col")),
        P(("row", "col"), None),
        P(("row", "col"), None),
        P(("row", "col"), None),
        P(("row", "col"), None),
        P(("row", "col"), None),
        P(("row", "col")),
        P(None, "col", None, "row"),
        P(None, "col", None, "row"),
        P(None, "col", None, "row"),
        P(None, "col", None, "row"),
        P(None, "col", None, "row"),
        P(("row", "col")),
        P(("row", "col")),
        P(("row", "col")),
        P(None, "col", None, "row"),
        P(("row", "col")),
        P(("row", "col")),
        P(None, "col", None, "row"),
        P(None, "col", None, "row"),
        P(None, "col", None, "row"),
    )
    out_specs = (
        P(("row", "col"), "dp"),
        P(),
        P(("row", "col"), "dp"),
        P(("row", "col")),
        P(("row", "col")),
        P(("row", "col"), None),
        P(("row", "col"), None),
        P(("row", "col"), None),
        P(("row", "col"), None),
        P(("row", "col"), None),
        P(("row", "col")),
        P(None, "col", None, "row"),
        P(None, "col", None, "row"),
        P(None, "col", None, "row"),
        P(None, "col", None, "row"),
        P(None, "col", None, "row"),
        P(("row", "col")),
        P(("row", "col")),
        P(("row", "col")),
        P(None, "col", None, "row"),
        P(("row", "col")),
        P(("row", "col")),
        P(None, "col", None, "row"),
        P(None, "col", None, "row"),
        P(None, "col", None, "row"),
    )
    return jax.shard_map(shards, mesh=mesh, in_specs=in_specs, out_specs=out_specs, check_vma=False)
```

time: 1500 us -> 894 us (0.60)
  local copies, waits for them, and re-layouts: 593 us -> 87.6 us
  Pallas kernels: 0 us -> 308 us
  other arithmetic: 374 us -> 97.6 us
  matrix products: 221 us -> 127 us
  blocking collectives: 116 us -> 22.1 us
  waiting for transfers between devices: 121 us -> 193 us
    pallas_call x0 -> x6, Pallas kernels: none -> 308 us  [the longest x1 97.2 us: gather_members(): pl.pallas_call(gather_kernel, in_specs=[anywhere], out_specs=anywhere, ou...]
    pad x64 -> x0, local copies, waits for them, and re-layouts: 157 us -> none  [ema_blocks(): lax.associative_scan(combine, (step_re, step_im, ends_re, ends_im), axis=1)]
    dot_general x17 -> x0, matrix products: 104 us -> none  [the longest x3 42.7 us: ema_blocks(): inside = jnp.einsum('cts,cbs->cbt', toeplitz, pieces, precision=PRECISE)]
    scatter-add x1 -> x0, other arithmetic: 98.3 us -> none  [ema_blocks(): kernel.T[:, jnp.maximum(offsets, 0)]]
    slice x40 -> x11, local copies, waits for them, and re-layouts: 82.9 us -> 8.48 us  [the longest x1 2.81 us: front_parameter_grads(): shaped[..., 4]]
    all_to_all x6, waiting for transfers between devices: 9.44 us -> 82.6 us  [exchange(): return lax.all_to_all(array_in, grid, 0, 0, tiled=True)]
    reduce_scatter x1 -> x0, waiting for transfers between devices: 70 us -> none  [shards(): lax.psum_scatter(kv_parts, 'col', scatter_dimension=0, tiled=True)[0]]
    psum x1 -> x3, waiting for transfers between devices: 0.01 us -> 67.2 us  [the longest x1 36 us: shards(): value_sum = lax.psum(value_sum, 'dp')]
  transfers between devices with their start and end apart: 18 -> 18, of which waited for: 5 -> 7; matrix products, arithmetic and copies ran while one was open for 74% -> 29% of each run, Pallas kernels for 0% -> 35%
where the time goes in v2:
time: 894 us; the launch traced here: 883 us
  Pallas kernels  308 us (34%)
  waiting for transfers between devices  193 us (22%)
  matrix products  127 us (14%)
  other arithmetic  97.6 us (11%)
  local copies, waits for them, and re-layouts  87.6 us (10%)
  starting transfers between devices  26.1 us (3%)
  blocking collectives  22.1 us (2%)
  between operations  21.8 us (2%)
    pallas_call x1, Pallas kernels, gather_members(): pl.pallas_call(gather_kernel, in_specs=[anywhere], out_specs=anywhere, ou...  97.2 us
    all_to_all x6, waiting for transfers between devices, exchange(): return lax.all_to_all(array_in, grid, 0, 0, tiled=True)  82.6 us
    pallas_call x1, Pallas kernels, front_backward(): pl.pallas_call(partial(front_backward_kernel, places, units), grid=(group...  76.6 us
    pallas_call x1, Pallas kernels, reduce_members(): pl.pallas_call(reduce_kernel, in_specs=[vmem], out_specs=vmem, out_shape=...  61.9 us
    dot_general x14, matrix products, project_back(): jnp.dot(weights[part], pieces[part], preferred_element_type=jnp.float32)  47.6 us
    dot_general x14, matrix products, contract_last(): lax.dot_general(left_in, right_in, (((1,), (1,)), ((), ())), preferred_el...  41 us
    dot_general x14, matrix products, contract_first(): lax.dot_general(left_in, right_in, (((0,), (0,)), ((), ())), preferred_el...  38.6 us
    psum x1, waiting for transfers between devices, shards(): value_sum = lax.psum(value_sum, 'dp')  36 us
  transfers between devices with their start and end apart: 18, of which 7 were waited for; matrix products, arithmetic and copies ran while one was open for 29% of the time, Pallas kernels for 35%

profile of v2, /device:TPU:0, one launch (start us, length us, event | category | flops | bytes accessed | tf_op | source)
XLA Modules:
  0.0 883.4 jit_solution(6022858991264553284)
XLA Ops:
  19.7 5.2 all-to-all-start.1
  30.1 35.3 %front_forward.1 = (bf16[8,2,128,512]{3,2,1,0:T(8,128)(2,1)}, bf16[8,2,128,512]{3,2,1,0:T(8,128)(2,1)}, f32[4,1024,128]{2,1,0:T(8,128)}, f32[4,64,128]{2,1,0:T(8...) custom-call(s32[1,32]{1,0:T(1,128)} %bitcast.467, s32[32,1]{1,0:T(8,128)} %copy-done.83, ...), custom_call_target="tpu_custom_call" | custom-call | flops 31457280000 | bytes 12582912 | tf_op jit(solution)/shard_map/front_forward/pallas_call | solution.py:476
  65.4 4.2 all-to-all-start
  70.0 40.4 %all-to-all-done = bf16[8,2,128,512]{3,2,1,0:T(8,128)(2,1)S(1)} async-done(((bf16[8,2,128,512]{3,2,1,0:T(8,128)(2,1)}), bf16[8,2,128,512]{3,2,1,0:T(8,128)(2,1)S(1)}, u32[]{:S(2)}, u32[]{:S(2)}) %all-to-all-start) | async-done | bytes 2097184 | tf_op jit(solution)/shard_map/all_to_all | solution.py:1163
  114.6 3.4 fusion.51
  122.4 97.2 %gather_members.1.keep_ref = bf16[4,2304,512]{2,1,0:T(8,128)(2,1)} custom-call(bf16[2304,512]{1,0:T(8,128)(2,1)} %pad_maximum_fusion.13.own_ref), custom_call_target="tpu_custom_call" | custom-call | tf_op jit(solution)/shard_map/gather_members/pallas_call | solution.py:952
  219.6 3.6 all-to-all-start.2
  227.0 15.9 %attention_forward.1 = (f32[2048,512]{1,0:T(8,128)}, f32[512,128]{1,0:T(8,128)}) custom-call(s32[1]{0:T(128)} %bitcast.8.member_ref, bf16[256,512]{1,0:T(8,128)(2,1)} %get-tuple-element.251.query_ref, bf16[4,2304,512]{2,1,0:T(8,128)(2,1)} %gather_members.1.keep_ref), custom_call_target="tpu_custom_call" | custom-call | flops 4831838208 | bytes 13631488 | tf_op jit(solution)/shard_map/attention_forward/pallas_call | solution.py:825
  242.9 5.1 fusion.98
  248.1 10.4 %all-to-all-done.2 = bf16[8,2,128,512]{3,2,1,0:T(8,128)(2,1)S(1)} async-done(((bf16[8,2,128,512]{3,2,1,0:T(8,128)(2,1)}), bf16[8,2,128,512]{3,2,1,0:T(8,128)(2,1)S(1)}, u32[]{:S(2)}, u32[]{:S(2)}) %all-to-all-start.2) | async-done | bytes 2097184 | tf_op jit(solution)/shard_map/all_to_all | solution.py:1163
  263.6 4.6 fusion.23
  268.4 6.3 fusion.21
  295.1 6.1 all-gather.14.cloned.1.call-done
  301.2 5.5 fusion.6
  322.7 3.0 pad_maximum_fusion.14
  331.9 3.6 fusion.69
  335.6 3.9 add_bitcast_fusion
  339.4 6.6 copy.279
  346.0 3.3 copy.280
  350.2 5.1 fusion.1
  355.3 5.9 fusion.5
  361.2 6.0 fusion.4
  367.2 9.0 %pad_maximum_fusion.1 = bf16[2,1024,2560]{2,1,0:T(8,128)(2,1)} fusion(bf16[1,1024,2560]{2,1,0:T(8,128)(2,1)} %fusion.5, bf16[1,1024,2560]{2,1,0:T(8,128)(2,1)} %fusion.4), kind=kLoop, calls=%fused_computation.1 | loop fusion | flops 5242880 | bytes 20971520 | tf_op jit(solution)/shard_map/stack | solution.py:1291
  376.2 6.2 fusion.8
  382.4 5.4 fusion.52
  393.1 4.1 fusion.41
  416.9 4.5 all-to-all-start.3
  432.0 3.3 convolution_convert_fusion.8
  438.3 6.0 fusion.16
  452.7 3.1 pad_maximum_fusion.2
  455.8 4.4 convolution_convert_fusion.4
  460.2 35.8 %reduce-scatter.11.cloned.1.call-done = bf16[1,256,2560]{2,1,0:T(8,128)(2,1)} async-done(((bf16[8,256,2560]{2,1,0:T(8,128)(2,1)}), bf16[1,256,2560]{2,1,0:T(8,128)(2,1)}) %reduce-scatter.11.cloned.1.call-update) | async-done | bytes 1310736 | tf_op jit(solution)/shard_map/reduce_scatter | solution.py:1293
  496.1 5.5 pad_maximum_fusion.3
  501.6 21.4 %attention_backward.1 = (f32[256,512]{1,0:T(8,128)}, bf16[4,2304,512]{2,1,0:T(8,128)(2,1)}) custom-call(s32[1]{0:T(128)} %bitcast.8.member_ref, bf16[256,512]{1,0:T(8,128)(2,1)} %get-tuple-element.251.query_ref, bf16[4,2304,512]{2,1,0:T(8,128)(2,1)} %gather_members.1.keep_ref, bf16[2048,512]{1,0:T(8,128)(2,1)} %get-tuple-element.214.grad_ref, ...), custom_call_target="tpu_custom_call" | custom-call | flops 9663676416 | bytes 18874368 | tf_op jit(solution)/shard_map/attention_backward/pallas_call | solution.py:853
  522.9 61.9 %reduce_members.1 = f32[2304,512]{1,0:T(8,128)} custom-call(bf16[4,2304,512]{2,1,0:T(8,128)(2,1)} %get-tuple-element.61.parts_ref), custom_call_target="tpu_custom_call" | custom-call | tf_op jit(solution)/shard_map/reduce_members/pallas_call | solution.py:1045
  584.8 10.6 %pad_maximum_fusion = bf16[2,1024,3072]{2,1,0:T(8,128)(2,1)} fusion(bf16[1,1024,3072]{2,1,0:T(8,128)(2,1)} %bitcast.358, bf16[1,1024,3072]{2,1,0:T(8,128)(2,1)} %bitcast.357), kind=kLoop, calls=%fused_computation | loop fusion | flops 6291456 | bytes 25165824 | tf_op jit(solution)/shard_map/stack | solution.py:1291
  596.1 6.6 fusion.20
  602.8 7.0 fusion.22
  613.1 3.3 all-to-all-start.5
  619.0 3.7 multiply_convert_fusion
  625.4 3.0 fusion.48
  632.1 4.6 all-to-all-start.4
  643.3 6.8 copy.302
  651.9 31.8 %all-to-all-done.4.grad_ref = bf16[8,2,128,512]{3,2,1,0:T(8,128)(2,1)} async-done(((bf16[8,2,128,512]{3,2,1,0:T(8,128)(2,1)}), bf16[8,2,128,512]{3,2,1,0:T(8,128)(2,1)}, u32[]{:S(2)}, u32[]{:S(2)}) %all-to-all-start.4) | async-done | bytes 2097184 | tf_op jit(solution)/shard_map/all_to_all | solution.py:1163
  683.7 76.6 %front_backward.1 = (f32[128,4096]{1,0:T(8,128)}, f32[128,4096]{1,0:T(8,128)}, f32[2048,8]{1,0:T(8,128)}, f32[128,8]{1,0:T(8,128)}) custom-call(s32[1,32]{1,0:T(1,128)} %bitcast.468, s32[1,32]{1,0:T(1,128)} %bitcast.469, s32[32,1]{1,0:T(8,128)} %copy-done.83, s32[32,1]{1,0:T(8,128)} %copy-done.84, f32[128,4096]{1,0:T(8,128)} %x_ref.3, ...), custom_call_target="tpu_custom_call" | custom-call | flops 73400320000 | bytes 16777216 | tf_op jit(solution)/shard_map/front_backward/pallas_call | solution.py:526
  769.5 22.1 %all-reduce = (f32[353]{0:T(512)S(1)}, f32[128]{0:T(128)}, f32[128]{0:T(128)}, f32[128,16]{0,1:T(8,128)}, f32[128,16]{0,1:T(8,128)}, /*index=5*/f32[128,16]{0,1:...) all-reduce(f32[353]{0:T(512)S(1)} %reduce_sum.119, ...), channel_id=1, replica_groups=mesh['dp'=4,'row'=2,'col'=4] {'dp'}, use_global_device_ids=true, to_apply=%region_15.16 | all-reduce | flops 10977 | bytes 87816 | tf_op jit(solution)/shard_map/psum | solution.py:1395
  798.9 31.2 %all-reduce.9.cloned.1.call-done = bf16[256,3072]{1,0:T(8,128)(2,1)} async-done(((bf16[256,3072]{1,0:T(8,128)(2,1)}), bf16[256,3072]{1,0:T(8,128)(2,1)}) %all-reduce.9.cloned.1.call-update) | async-done | bytes 1572880 | tf_op jit(solution)/shard_map/psum | solution.py:1356
  835.3 36.0 %all-reduce.11.cloned.1.call-done = bf16[256,1152]{1,0:T(8,128)(2,1)} async-done(((bf16[256,1152]{1,0:T(8,128)(2,1)}), bf16[256,1152]{1,0:T(8,128)(2,1)}) %all-reduce.11.cloned.1.call-update) | async-done | bytes 589840 | tf_op jit(solution)/shard_map/psum | solution.py:1386
  (436 shorter events, 167.2 us)
Async XLA Ops:
  8.0 102.8 %all-gather.10.cloned.1.call-start = ((), (), s32[]{:S(2)}) async-start(), calls=%async_computation.18 | async-start | bytes 5308416 | tf_op jit(solution)/shard_map/all_gather | solution.py:1166
  10.1 215.0 %all-reduce.7.cloned.1.call-start = ((), (), s32[]{:S(2)}) async-start(), calls=%async_computation.11 | async-start | bytes 2097152 | tf_op jit(solution)/shard_map/psum | solution.py:1181
  13.2 229.7 %all-gather.8.cloned.1.call-start = ((), (), s32[]{:S(2)}) async-start(), calls=%async_computation.10 | async-start | bytes 5898240 | tf_op jit(solution)/shard_map/all_gather | solution.py:1166
  14.0 249.6 %all-gather.12.cloned.1.call-start = ((), (), s32[]{:S(2)}) async-start(), calls=%async_computation.19 | async-start | bytes 14155776 | tf_op jit(solution)/shard_map/all_gather | solution.py:1166
  17.6 7.2 copy-start.103
  17.7 8.6 copy-start.81
  17.7 8.7 copy-start.85
  17.7 8.7 copy-start.95
  17.7 9.4 %copy-start.93 = (f32[128,16]{0,1:T(8,128)S(1)}, f32[128,16]{0,1:T(8,128)}, u32[]{:S(2)}) copy-start(f32[128,16]{0,1:T(8,128)} %param.35) | copy-start | bytes 24580
  17.7 283.5 %all-gather.14.cloned.1.call-start = ((), (), s32[]{:S(2)}) async-start(), calls=%async_computation.20 | async-start | bytes 11796480 | tf_op jit(solution)/shard_map/all_gather | solution.py:1166
  17.8 9.5 %copy-start.94 = (f32[128,16]{0,1:T(8,128)S(1)}, f32[128,16]{0,1:T(8,128)}, u32[]{:S(2)}) copy-start(f32[128,16]{0,1:T(8,128)} %param.36) | copy-start | bytes 24580
  18.9 10.5 %copy-start.87 = (f32[128]{0:T(128)S(1)}, f32[128]{0:T(128)}, u32[]{:S(2)}) copy-start(f32[128]{0:T(128)} %param.37) | copy-start | bytes 1540
  18.9 10.5 %copy-start.101 = (f32[128]{0:T(128)S(1)}, f32[128]{0:T(128)}, u32[]{:S(2)}) copy-start(f32[128]{0:T(128)} %param.30) | copy-start | bytes 1540
  18.9 10.5 %copy-start.102 = (f32[128]{0:T(128)S(1)}, f32[128]{0:T(128)}, u32[]{:S(2)}) copy-start(f32[128]{0:T(128)} %param.31) | copy-start | bytes 1540
  19.7 45.7 %all-to-all-start.1 = ((f32[8,1,352]{2,1,0:T(1,128)}), f32[8,1,352]{2,1,0:T(1,128)S(1)}, u32[]{:S(2)}, u32[]{:S(2)}) async-start(f32[8,1,352]{2,1,0:T(1,128)} %broadcast_in_dim.56), calls=%async_computation.1 | async-start | bytes 24576 | tf_op jit(solution)/shard_map/all_to_all | solution.py:1163
  65.4 44.9 %all-to-all-start = ((bf16[8,2,128,512]{3,2,1,0:T(8,128)(2,1)}), bf16[8,2,128,512]{3,2,1,0:T(8,128)(2,1)S(1)}, u32[]{:S(2)}, u32[]{:S(2)}) async-start(bf16[8,2,128,512]{3,2,1,0:T(8,128)(2,1)} %get-tuple-element.54), calls=%async_computation | async-start | bytes 4194304 | tf_op jit(solution)/shard_map/all_to_all | solution.py:1163
  69.8 43.9 %copy-start.89 = (f32[256]{0:T(256)}, f32[256]{0:T(256)S(1)}, u32[]{:S(2)}) copy-start(f32[256]{0:T(256)S(1)} %mul.410) | copy-start | bytes 3076
  70.0 43.8 %copy-start.91 = (f32[256]{0:T(256)}, f32[256]{0:T(256)S(1)}, u32[]{:S(2)}) copy-start(f32[256]{0:T(256)S(1)} %mul.406) | copy-start | bytes 3076
  110.8 7.3 copy-start.70
  110.8 157.6 %copy-start.15 = (bf16[1,4,2,128,512]{4,3,2,1,0:T(8,128)(2,1)}, bf16[1,4,2,128,512]{4,3,2,1,0:T(8,128)(2,1)S(1)}, u32[]{:S(2)}) copy-start(bf16[1,4,2,128,512]{4,3,2,1,0:T(8,128)(2,1)S(1)} %get-tuple-element.236) | copy-start | bytes 3145732
  219.6 38.9 %all-to-all-start.2 = ((bf16[8,2,128,512]{3,2,1,0:T(8,128)(2,1)}), bf16[8,2,128,512]{3,2,1,0:T(8,128)(2,1)S(1)}, u32[]{:S(2)}, u32[]{:S(2)}) async-start(bf16[8,2,128,512]{3,2,1,0:T(8,128)(2,1)} %get-tuple-element.57), calls=%async_computation.2 | async-start | bytes 4194304 | tf_op jit(solution)/shard_map/all_to_all | solution.py:1163
  223.2 237.0 %reduce-scatter.9.cloned.1.call-start = ((), (), s32[]{:S(2)}) async-start(), calls=%async_computation.14 | async-start | bytes 5898240 | tf_op jit(solution)/shard_map/reduce_scatter | solution.py:1293
  279.4 8.9 %copy-start.23 = (f32[512,512]{1,0:T(8,128)}, f32[512,512]{1,0:T(8,128)S(1)}, u32[]{:S(2)}) copy-start(f32[512,512]{1,0:T(8,128)S(1)} %get-tuple-element.225) | copy-start | bytes 3145732
  279.6 6.7 copy-start.72
  331.8 164.1 %reduce-scatter.11.cloned.1.call-start = ((), (), s32[]{:S(2)}) async-start(), calls=%async_computation.15 | async-start | bytes 11796480 | tf_op jit(solution)/shard_map/reduce_scatter | solution.py:1293
  388.0 21.5 %copy-start.9 = (f32[2,4,128,512]{3,2,1,0:T(8,128)}, f32[2,4,128,512]{3,2,1,0:T(8,128)S(1)}, u32[]{:S(2)}) copy-start(f32[2,4,128,512]{3,2,1,0:T(8,128)S(1)} %copy.281) | copy-start | bytes 6291460
  397.2 6.5 copy-start.36
  416.9 106.1 %all-to-all-start.3 = ((bf16[8,2,128,512]{3,2,1,0:T(8,128)(2,1)}), bf16[8,2,128,512]{3,2,1,0:T(8,128)(2,1)}, u32[]{:S(2)}, u32[]{:S(2)}) async-start(bf16[8,2,128,512]{3,2,1,0:T(8,128)(2,1)} %pad_maximum_fusion.15), calls=%async_computation.3 | async-start | bytes 4194304 | tf_op jit(solution)/shard_map/all_to_all | solution.py:1163
  421.4 338.9 %all-reduce.13.cloned.1.call-start = ((), (), s32[]{:S(2)}) async-start(), calls=%async_computation.21 | async-start | bytes 3932160 | tf_op jit(solution)/shard_map/psum | solution.py:1298
  438.2 7.0 copy-start.13
  438.2 7.6 copy-start.18
  455.8 40.2 %copy-start.68 = (bf16[1024,512]{1,0:T(8,128)(2,1)S(1)}, bf16[1024,512]{1,0:T(8,128)(2,1)}, u32[]{:S(2)}) copy-start(bf16[1024,512]{1,0:T(8,128)(2,1)} %convolution_convert_fusion.9) | copy-start | bytes 3145732
  460.2 35.9 %copy-start.67 = (bf16[1024,512]{1,0:T(8,128)(2,1)S(1)}, bf16[1024,512]{1,0:T(8,128)(2,1)}, u32[]{:S(2)}) copy-start(bf16[1024,512]{1,0:T(8,128)(2,1)} %convolution_convert_fusion.8) | copy-start | bytes 3145732
  496.0 264.3 %reduce-scatter.7.cloned.1.call-start = ((), (), s32[]{:S(2)}) async-start(), calls=%async_computation.13 | async-start | bytes 14155776 | tf_op jit(solution)/shard_map/reduce_scatter | solution.py:1293
  596.1 6.7 copy-start.49
  602.8 7.0 copy-start.55
  602.8 7.0 copy-start.57
  602.8 7.0 copy-start.78
  602.8 7.0 copy-start.90
  602.8 7.0 copy-start.92
  611.2 7.8 copy-start.39
  613.1 19.0 %all-to-all-start.5 = ((f32[8,1,353]{2,1,0:T(1,128)}), f32[8,1,353]{2,1,0:T(1,128)S(1)}, u32[]{:S(2)}, u32[]{:S(2)}) async-start(f32[8,1,353]{2,1,0:T(1,128)} %copy.296), calls=%async_computation.5 | async-start | bytes 24576 | tf_op jit(solution)/shard_map/all_to_all | solution.py:1163
  619.0 9.4 %slice-start.5 = ((s8[4718592]{0:T(1024)(128)(4,1)}), s8[4194304]{0:T(1024)(128)(4,1)S(1)}, s32[]{:S(2)}) async-start(s8[4718592]{0:T(1024)(128)(4,1)} %bitcast.444), calls=%async_computation.27 | async-start | bytes 8388608
  632.1 51.6 %all-to-all-start.4 = ((bf16[8,2,128,512]{3,2,1,0:T(8,128)(2,1)}), bf16[8,2,128,512]{3,2,1,0:T(8,128)(2,1)}, u32[]{:S(2)}, u32[]{:S(2)}) async-start(bf16[8,2,128,512]{3,2,1,0:T(8,128)(2,1)} %bitcast.91), calls=%async_computation.4 | async-start | bytes 4194304 | tf_op jit(solution)/shard_map/all_to_all | solution.py:1163
  636.7 162.2 %reduce-scatter.5.cloned.1.call-start = ((), (), s32[]{:S(2)}) async-start(), calls=%async_computation.12 | async-start | bytes 5308416 | tf_op jit(solution)/shard_map/reduce_scatter | solution.py:1293
  650.1 180.0 %all-reduce.9.cloned.1.call-start = ((), (), s32[]{:S(2)}) async-start(), calls=%async_computation.16 | async-start | bytes 3145728 | tf_op jit(solution)/shard_map/psum | solution.py:1356
  650.5 33.1 %copy-start.84 = (s32[32,1]{1,0:T(8,128)}, s32[32,1]{1,0:T(8,128)S(1)}, u32[]{:S(2)}) copy-start(s32[32,1]{1,0:T(8,128)S(1)} %broadcast_in_dim.53.stop_col) | copy-start | bytes 388
  760.4 111.0 %all-reduce.11.cloned.1.call-start = ((), (), s32[]{:S(2)}) async-start(), calls=%async_computation.17 | async-start | bytes 1179648 | tf_op jit(solution)/shard_map/psum | solution.py:1386
  (87 other events, 294.2 us)
Sparse Core Ops, SparseCore 0:
  11.3 41.7 all-gather.9
  55.0 55.0 all-gather.7
  112.0 114.1 all-gather.11
  228.6 72.6 all-gather.13
  332.0 56.5 reduce-scatter.8
  391.9 104.0 reduce-scatter.10
  595.5 114.9 reduce-scatter.6
  714.0 53.8 reduce-scatter.4
Sparse Core Ops, SparseCore 1:
  13.5 54.4 all-reduce.6
  496.1 82.0 all-reduce.12
  760.5 69.6 all-reduce.8
  832.6 38.8 all-reduce.10

commit v3 on v2

--- a/solution.py
+++ b/solution.py
@@ -14,11 +14,16 @@
 UNIT = 128
 STATES = 16
 COUNT_ROWS = 256
+TILE = 256
 BATCH = 16
 BATCH_BACK = 16
 
 EPSILON = 1e-05
 NEGATIVE = -1000000000.0
+
+
+def expected(weight):
+    return pl.CostEstimate(flops=weight * 1150000000, bytes_accessed=0, transcendentals=0)
 
 
 NT = (((1,), (1,)), ((), ()))
@@ -129,6 +134,7 @@
     state_ref,
     channel_ref,
     send_ref,
+    mixed_ref,
     plain_ref,
     pre_ref,
     stat_ref,
@@ -235,36 +241,38 @@
         span = slice(unit * UNIT, (unit + 1) * UNIT)
         plain_ref[device, 0, :, across] = x_ref[:, span].astype(jnp.bfloat16)
         plain_ref[device, 1, :, across] = teacher_ref[:, span].astype(jnp.bfloat16)
-        send_ref[device, 0, :, across] = normed.astype(jnp.bfloat16)
-        send_ref[device, 1, :, across] = (pre_act * jax.nn.sigmoid(pre_act)).astype(jnp.bfloat16)
-
-
-def front_backward_kernel(
-    places,
-    units,
-    start_row,
-    stop_row,
-    start_col,
-    stop_col,
-    x_ref,
-    state_ref,
-    channel_ref,
-    grad_ref,
-    direct_ref,
-    pre_ref,
-    stat_ref,
-    table_ref,
-    row_ref,
-    hold_ref,
-    output_ref,
-    out_ref,
-    state_grad_ref,
-    channel_grad_ref,
-    normed_ref,
-    slope_ref,
-    back_ref,
-    sums_ref,
-):
+        send_ref[device, :, across] = normed.astype(jnp.bfloat16)
+        mixed_ref[device, :, across] = (pre_act * jax.nn.sigmoid(pre_act)).astype(jnp.bfloat16)
+
+
+def front_backward_kernel(places, units, skipped, *refs):
+    (
+        start_row,
+        stop_row,
+        start_col,
+        stop_col,
+        x_ref,
+        state_ref,
+        channel_ref,
+        normed_grad_ref,
+        mixed_grad_ref,
+        direct_ref,
+        pre_ref,
+        stat_ref,
+        table_ref,
+        row_ref,
+        hold_ref,
+    ) = refs[:15]
+    (
+        output_ref,
+        out_ref,
+        state_grad_ref,
+        channel_grad_ref,
+        normed_ref,
+        slope_ref,
+        back_ref,
+        sums_ref,
+    ) = refs[15 + skipped :]
     f32 = jnp.float32
     gain, bias, skip = channel_ref[:, 0:1], channel_ref[:, 1:2], channel_ref[:, 2:3]
     skip_sum = jnp.zeros((GS, UNIT), f32)
@@ -280,7 +288,7 @@
         pre_act = pre_ref[0, here, :]
         logistic = jax.nn.sigmoid(pre_act)
         slope = (
-            grad_ref[device, 1, :, across].astype(f32)
+            mixed_grad_ref[device, :, across].astype(f32)
             * logistic
             * (1.0 + pre_act * (1.0 - logistic))
         )
@@ -403,7 +411,7 @@
         std_row = stat_ref[0, units + unit : units + unit + 1, :]
         plain = (tile - mean_row) * std_row
         total = (
-            grad_ref[device, 0, :, across].astype(f32)
+            normed_grad_ref[device, :, across].astype(f32)
             + skip * slope_ref[here, :]
             + back_ref[here, :]
         )
@@ -485,7 +493,8 @@
             pl.BlockSpec((GS, 8), lambda group: (group, 0)),
         ],
         out_specs=[
-            pl.BlockSpec((devices, 2, GS, tokens), lambda group: (0, 0, group, 0)),
+            pl.BlockSpec((devices, GS, tokens), lambda group: (0, group, 0)),
+            pl.BlockSpec((devices, GS, tokens), lambda group: (0, group, 0)),
             pl.BlockSpec((devices, 2, GS, tokens), lambda group: (0, 0, group, 0)),
             pl.BlockSpec((1, units * GS, UNIT), lambda group: (group, 0, 0)),
             pl.BlockSpec((1, 2 * units, UNIT), lambda group: (group, 0, 0)),
@@ -494,7 +503,8 @@
             pl.BlockSpec((2, GS * STATES, units), lambda group: (0, group, 0)),
         ],
         out_shape=[
-            jax.ShapeDtypeStruct((devices, 2, channels, tokens), jnp.bfloat16),
+            jax.ShapeDtypeStruct((devices, channels, tokens), jnp.bfloat16),
+            jax.ShapeDtypeStruct((devices, channels, tokens), jnp.bfloat16),
             jax.ShapeDtypeStruct((devices, 2, channels, tokens), jnp.bfloat16),
             jax.ShapeDtypeStruct((groups, units * GS, UNIT), f32),
             jax.ShapeDtypeStruct((groups, 2 * units, UNIT), f32),
@@ -507,15 +517,25 @@
             pltpu.VMEM((2 * units, UNIT), f32),
             pltpu.VMEM((units * GS, UNIT), f32),
         ],
-        cost_estimate=pl.CostEstimate(
-            flops=channels * slots * 60000, bytes_accessed=channels * slots * 24, transcendentals=0
-        ),
+        cost_estimate=expected(35),
         name="front_forward",
     )(starts[None, :], starts[:, None], layer_input, teacher, state_params, channel_params)
 
 
 def front_backward(
-    layer_input, state_params, channel_params, bounds, places, devices, grads, direct, saved
+    layer_input,
+    state_params,
+    channel_params,
+    bounds,
+    places,
+    devices,
+    normed_grads,
+    mixed_grads,
+    direct,
+    saved,
+    first=0,
+    count=1,
+    filled=(),
 ):
     channels, slots = layer_input.shape
     units = slots // UNIT
@@ -524,29 +544,31 @@
     starts, stops = bounds
     f32 = jnp.float32
     return pl.pallas_call(
-        partial(front_backward_kernel, places, units),
-        grid=(groups,),
+        partial(front_backward_kernel, places, units, len(filled)),
+        grid=(count,),
         in_specs=[
             whole((1, units)),
             whole((1, units)),
             whole((units, 1)),
             whole((units, 1)),
-            pl.BlockSpec((GS, slots), lambda group: (group, 0)),
-            pl.BlockSpec((GS * STATES, 8), lambda group: (group, 0)),
-            pl.BlockSpec((GS, 8), lambda group: (group, 0)),
-            pl.BlockSpec((devices, 2, GS, tokens), lambda group: (0, 0, group, 0)),
-            pl.BlockSpec((devices, 2, GS, tokens), lambda group: (0, 0, group, 0)),
-            pl.BlockSpec((1, units * GS, UNIT), lambda group: (group, 0, 0)),
-            pl.BlockSpec((1, 2 * units, UNIT), lambda group: (group, 0, 0)),
-            pl.BlockSpec((4, GS * STATES, UNIT), lambda group: (0, group, 0)),
-            pl.BlockSpec((GS, UNIT), lambda group: (group, 0)),
-            pl.BlockSpec((2, GS * STATES, units), lambda group: (0, group, 0)),
-        ],
+            pl.BlockSpec((GS, slots), lambda group: (first + group, 0)),
+            pl.BlockSpec((GS * STATES, 8), lambda group: (first + group, 0)),
+            pl.BlockSpec((GS, 8), lambda group: (first + group, 0)),
+            pl.BlockSpec((devices, GS, tokens), lambda group: (0, first + group, 0)),
+            pl.BlockSpec((devices, GS, tokens), lambda group: (0, first + group, 0)),
+            pl.BlockSpec((devices, 2, GS, tokens), lambda group: (0, 0, first + group, 0)),
+            pl.BlockSpec((1, units * GS, UNIT), lambda group: (first + group, 0, 0)),
+            pl.BlockSpec((1, 2 * units, UNIT), lambda group: (first + group, 0, 0)),
+            pl.BlockSpec((4, GS * STATES, UNIT), lambda group: (0, first + group, 0)),
+            pl.BlockSpec((GS, UNIT), lambda group: (first + group, 0)),
+            pl.BlockSpec((2, GS * STATES, units), lambda group: (0, first + group, 0)),
+        ]
+        + [pl.BlockSpec(memory_space=pl.ANY)] * len(filled),
         out_specs=[
-            pl.BlockSpec((GS, slots), lambda group: (group, 0)),
-            pl.BlockSpec((GS, slots), lambda group: (group, 0)),
-            pl.BlockSpec((GS * STATES, 8), lambda group: (group, 0)),
-            pl.BlockSpec((GS, 8), lambda group: (group, 0)),
+            pl.BlockSpec((GS, slots), lambda group: (first + group, 0)),
+            pl.BlockSpec((GS, slots), lambda group: (first + group, 0)),
+            pl.BlockSpec((GS * STATES, 8), lambda group: (first + group, 0)),
+            pl.BlockSpec((GS, 8), lambda group: (first + group, 0)),
         ],
         out_shape=[
             jax.ShapeDtypeStruct((channels, slots), f32),
@@ -560,9 +582,8 @@
             pltpu.VMEM((units * GS, UNIT), f32),
             pltpu.VMEM((2 * units, UNIT), f32),
         ],
-        cost_estimate=pl.CostEstimate(
-            flops=channels * slots * 140000, bytes_accessed=channels * slots * 32, transcendentals=0
-        ),
+        input_output_aliases={15 + index: index for index in range(len(filled))},
+        cost_estimate=expected(20 * count),
         name="front_backward",
     )(
         starts[None, :],
@@ -572,9 +593,11 @@
         layer_input,
         state_params,
         channel_params,
-        grads,
+        normed_grads,
+        mixed_grads,
         direct,
         *saved,
+        *filled,
     )
 
 
@@ -660,7 +683,7 @@
 
 
 def attention_forward_kernel(
-    group, member_ref, query_ref, keep_ref, out_ref, log_ref, score_ref, prob_ref
+    group, member_ref, query_ref, key_ref, value_ref, out_ref, log_ref, score_ref, prob_ref
 ):
     f32, bf16 = jnp.float32, jnp.bfloat16
     tokens = query_ref.shape[1]
@@ -677,7 +700,7 @@
 
             @pl.when(index <= chunk)
             def _():
-                keys = keep_ref[owner, width:, start : start + half]
+                keys = key_ref[owner, :, start : start + half]
                 scores = masked_scores(turned, keys, causal_tile(half, index, chunk), scale)
                 score_ref[index] = scores
                 log_ref[offset : offset + half, :] = jnp.maximum(
@@ -703,7 +726,7 @@
             @pl.when(index <= chunk)
             def _():
                 probs = (score_ref[index] / totals).astype(bf16)
-                values = keep_ref[owner, :width, start : start + half]
+                values = value_ref[owner, :, start : start + half]
                 out_ref[:, offset : offset + half] += lax.dot_general(
                     values, probs, NT, preferred_element_type=f32
                 )
@@ -713,11 +736,14 @@
     group,
     member_ref,
     query_ref,
-    keep_ref,
+    key_ref,
+    value_ref,
+    bend_ref,
     grad_ref,
     log_ref,
     query_grad_ref,
-    out_ref,
+    key_out_ref,
+    value_out_ref,
     prob_ref,
     slope_ref,
     low_ref,
@@ -746,14 +772,14 @@
 
             @pl.when(index <= chunk)
             def _():
-                keys = keep_ref[owner, width:, start : start + half]
+                keys = key_ref[owner, :, start : start + half]
                 scores = masked_scores(turned, keys, causal_tile(half, index, chunk), scale)
                 probs = jnp.exp(scores - logs)
                 prob_ref[index] = probs
                 low_ref[which, index] = probs.astype(bf16)
                 slope = lax.dot_general(
                     turned_ref[...],
-                    keep_ref[owner, :width, start : start + half],
+                    value_ref[owner, :, start : start + half],
                     NN,
                     preferred_element_type=f32,
                 )
@@ -767,7 +793,7 @@
             def _():
                 score_grad = (prob_ref[index] * (slope_ref[index] - dots)).astype(bf16)
                 score_grad_ref[which, index] = score_grad
-                keys = keep_ref[owner, width:, start : start + half]
+                keys = key_ref[owner, :, start : start + half]
                 query_grad_ref[:, here] += (
                     lax.dot_general(keys, score_grad, NT, preferred_element_type=f32) * scale
                 )
@@ -789,8 +815,10 @@
                 )
                 value_sum = value_part if value_sum is None else value_sum + value_part
                 key_sum = key_part if key_sum is None else key_sum + key_part
-            out_ref[owner, :width, there] = value_sum.astype(bf16)
-            out_ref[owner, width:, there] = (key_sum * scale).astype(bf16)
+            value_out_ref[owner, :, there] = (
+                value_sum * bend_ref[owner, :, there].astype(f32)
+            ).astype(bf16)
+            key_out_ref[owner, :, there] = (key_sum * scale).astype(bf16)
 
         if len(pieces) == 2:
 
@@ -810,21 +838,22 @@
 
         @pl.when(index > last[0])
         def _():
-            out_ref[owner, :, there] = jnp.zeros((out_ref.shape[1], half), bf16)
+            value_out_ref[owner, :, there] = jnp.zeros((width, half), bf16)
+            key_out_ref[owner, :, there] = jnp.zeros((Z, half), bf16)
 
 
 VMEM_BUDGET = 60 * 1024 * 1024
 
 
-def attention_forward(member, queries, key_values, group):
+def attention_forward(member, queries, keys, values, group):
     tokens = queries.shape[1]
-    width = key_values.shape[1] - queries.shape[0]
+    width = values.shape[1]
     half, sites = chunk_sites(group, tokens)
     f32 = jnp.float32
     vmem = pl.BlockSpec(memory_space=pltpu.VMEM)
     return pl.pallas_call(
         partial(attention_forward_kernel, group),
-        in_specs=[pl.BlockSpec(memory_space=pltpu.SMEM), vmem, vmem],
+        in_specs=[pl.BlockSpec(memory_space=pltpu.SMEM)] + [vmem] * 3,
         out_specs=[vmem, vmem],
         out_shape=[
             jax.ShapeDtypeStruct((width, tokens), f32),
@@ -835,16 +864,12 @@
             pltpu.VMEM((half, UNIT), f32),
         ],
         compiler_params=pltpu.CompilerParams(vmem_limit_bytes=VMEM_BUDGET),
-        cost_estimate=pl.CostEstimate(
-            flops=2 * tokens * tokens * group * (width + Z),
-            bytes_accessed=2 * key_values.size + 4 * width * tokens,
-            transcendentals=tokens * tokens * group,
-        ),
+        cost_estimate=expected(16),
         name="attention_forward",
-    )(member, queries, key_values)
-
-
-def attention_backward(member, queries, key_values, grads, logs, group):
+    )(member, queries, keys, values)
+
+
+def attention_backward(member, queries, keys, values, bends, grads, logs, group):
     tokens = queries.shape[1]
     half, sites = chunk_sites(group, tokens)
     count = tokens // half
@@ -852,11 +877,12 @@
     vmem = pl.BlockSpec(memory_space=pltpu.VMEM)
     return pl.pallas_call(
         partial(attention_backward_kernel, group),
-        in_specs=[pl.BlockSpec(memory_space=pltpu.SMEM), vmem, vmem, vmem, vmem],
-        out_specs=[vmem, vmem],
+        in_specs=[pl.BlockSpec(memory_space=pltpu.SMEM)] + [vmem] * 6,
+        out_specs=[vmem] * 3,
         out_shape=[
             jax.ShapeDtypeStruct(queries.shape, f32),
-            jax.ShapeDtypeStruct(key_values.shape, bf16),
+            jax.ShapeDtypeStruct(keys.shape, bf16),
+            jax.ShapeDtypeStruct(values.shape, bf16),
         ],
         scratch_shapes=[
             pltpu.VMEM((len(sites), half, half), f32),
@@ -867,16 +893,471 @@
             pltpu.VMEM((half, grads.shape[0]), bf16),
         ],
         compiler_params=pltpu.CompilerParams(vmem_limit_bytes=VMEM_BUDGET),
-        cost_estimate=pl.CostEstimate(
-            flops=4 * tokens * tokens * group * (grads.shape[0] + Z),
-            bytes_accessed=4 * key_values.size,
-            transcendentals=tokens * tokens * group,
-        ),
+        cost_estimate=expected(8),
         name="attention_backward",
-    )(member, queries, key_values, grads, logs)
-
-
-PIECES = 4
+    )(member, queries, keys, values, bends, grads, logs)
+
+
+def values_kernel(weight_ref, source_ref, value_ref, slope_ref, turned_ref):
+    @pl.when(pl.program_id(1) == 0)
+    def _():
+        width = weight_ref.shape[2]
+        for start in range(0, width, TILE):
+            turned_ref[start : start + TILE, :] = (
+                weight_ref[0, :, start : start + TILE].astype(jnp.float32).T.astype(jnp.bfloat16)
+            )
+
+    product = jnp.dot(turned_ref[...], source_ref[0], preferred_element_type=jnp.float32)
+    logistic = jax.nn.sigmoid(product)
+    value_ref[0] = (product * logistic).astype(jnp.bfloat16)
+    slope_ref[0] = (logistic * (1.0 + product * (1.0 - logistic))).astype(jnp.bfloat16)
+
+
+def block_values(weights, sources, count):
+    rows, depth = weights.shape[:2]
+    group, _, tokens = sources.shape
+    return pl.pallas_call(
+        values_kernel,
+        grid=(rows, group),
+        in_specs=[
+            pl.BlockSpec((1, depth, count), lambda part, step: (part, 0, 0)),
+            pl.BlockSpec((1, depth, tokens), lambda part, step: (step, 0, 0)),
+        ],
+        out_specs=[
+            pl.BlockSpec((1, count, tokens), lambda part, step: (step, part, 0)),
+            pl.BlockSpec((1, count, tokens), lambda part, step: (step, part, 0)),
+        ],
+        out_shape=[jax.ShapeDtypeStruct((group, rows * count, tokens), jnp.bfloat16)] * 2,
+        scratch_shapes=[pltpu.VMEM((count, depth), jnp.bfloat16)],
+        compiler_params=pltpu.CompilerParams(vmem_limit_bytes=VMEM_BUDGET),
+        cost_estimate=expected(19),
+        name="block_values",
+    )(weights, sources)
+
+
+def values_back_kernel(weight_ref, grad_ref, out_ref):
+    count = weight_ref.shape[2]
+    total = None
+    for part in range(weight_ref.shape[0]):
+        piece = jnp.dot(
+            weight_ref[part],
+            grad_ref[0, part * count : (part + 1) * count, :],
+            preferred_element_type=jnp.float32,
+        )
+        total = piece if total is None else total + piece
+    out_ref[0] = total.astype(jnp.bfloat16)
+
+
+def block_values_back(weights, grads, count):
+    rows, depth = weights.shape[:2]
+    group, width, tokens = grads.shape
+    return pl.pallas_call(
+        values_back_kernel,
+        grid=(group,),
+        in_specs=[
+            pl.BlockSpec((rows, depth, count), lambda step: (0, 0, 0)),
+            pl.BlockSpec((1, width, tokens), lambda step: (step, 0, 0)),
+        ],
+        out_specs=pl.BlockSpec((1, depth, tokens), lambda step: (step, 0, 0)),
+        out_shape=jax.ShapeDtypeStruct((group, depth, tokens), jnp.bfloat16),
+        compiler_params=pltpu.CompilerParams(vmem_limit_bytes=VMEM_BUDGET),
+        cost_estimate=expected(5),
+        name="block_values_back",
+    )(weights, grads)
+
+
+def values_products_kernel(source_ref, grad_ref, out_ref):
+    total = None
+    for step in range(source_ref.shape[0]):
+        piece = lax.dot_general(
+            source_ref[step], grad_ref[step], NT, preferred_element_type=jnp.float32
+        )
+        total = piece if total is None else total + piece
+    out_ref[0] = total.astype(jnp.bfloat16)
+
+
+def block_values_products(rows, sources, grads):
+    group, depth, tokens = sources.shape
+    width = grads.shape[1]
+    count = width // rows
+    return pl.pallas_call(
+        values_products_kernel,
+        grid=(rows,),
+        in_specs=[
+            pl.BlockSpec((group, depth, tokens), lambda part: (0, 0, 0)),
+            pl.BlockSpec((group, count, tokens), lambda part: (0, part, 0)),
+        ],
+        out_specs=pl.BlockSpec((1, depth, count), lambda part: (part, 0, 0)),
+        out_shape=jax.ShapeDtypeStruct((rows, depth, count), jnp.bfloat16),
+        compiler_params=pltpu.CompilerParams(vmem_limit_bytes=VMEM_BUDGET),
+        cost_estimate=expected(5),
+        name="block_values_products",
+    )(sources, grads)
+
+
+def packed_pieces(rows, deep, columns):
+    pieces = []
+    start = 0
+    while start < rows * deep:
+        block, inside = divmod(start, UNIT)
+        count = min(UNIT - inside, deep - start % deep)
+        if block < 4:
+            side, lane = (block // 2) * UNIT + inside, (block % 2) * columns
+            pieces.append((start, count, side, lane, columns, 0))
+        else:
+            for part in range(2):
+                pieces.append(
+                    (
+                        start,
+                        count,
+                        part * UNIT + inside,
+                        2 * columns,
+                        columns // 2,
+                        part * (columns // 2),
+                    )
+                )
+        start += count
+    return pieces
+
+
+def inner_kernel(
+    rows,
+    cols,
+    arrays,
+    first_ref,
+    teacher_ref,
+    mask_ref,
+    factor_ref,
+    gain_ref,
+    bias_ref,
+    *refs,
+):
+    inner_hbm, down_hbm = refs[0], refs[1] if arrays == 2 else None
+    inner_body(
+        rows,
+        cols,
+        first_ref,
+        teacher_ref,
+        mask_ref,
+        factor_ref,
+        gain_ref,
+        bias_ref,
+        inner_hbm,
+        down_hbm,
+        *refs[arrays:],
+    )
+
+
+def inner_body(
+    rows,
+    cols,
+    first_ref,
+    teacher_ref,
+    mask_ref,
+    factor_ref,
+    gain_ref,
+    bias_ref,
+    inner_hbm,
+    down_hbm,
+    out_ref,
+    loss_ref,
+    norm_ref,
+    act_ref,
+    low_ref,
+    grads_ref,
+    first_grad_ref,
+    gain_sum_ref,
+    bias_sum_ref,
+    inner_ref,
+    down_ref,
+    turned_ref,
+    gate_ref,
+    up_ref,
+    act_turned_ref,
+    inner_sem,
+    down_sem,
+):
+    f32, bf16 = jnp.float32, jnp.bfloat16
+    width = first_ref.shape[0]
+    tokens = first_ref.shape[1]
+    hidden = act_ref.shape[0]
+    n_inner = hidden // rows
+    n_down = width // rows
+    deep = width // (rows * cols)
+    deep_down = hidden // (rows * cols)
+
+    packed = down_hbm is None
+
+    def inner_copies():
+        copies = []
+        for row in range(rows):
+            for col in range(cols):
+                target = inner_ref.at[:, pl.ds((row * cols + col) * deep, deep)]
+                if packed:
+                    source = inner_hbm.at[:, col, pl.ds(row * deep, deep), pl.ds(0, 2 * n_inner)]
+                else:
+                    source = inner_hbm.at[:, col, row]
+                copies.append(
+                    pltpu.make_async_copy(source, target, inner_sem.at[row * cols + col])
+                )
+        return copies
+
+    def down_copies():
+        copies = []
+        for col in range(cols):
+            if packed:
+                for start, count, side, lane, width_, column in packed_pieces(
+                    rows, deep_down, n_down
+                ):
+                    row, inside = start // deep_down, start % deep_down
+                    source = inner_hbm.at[
+                        :, col, pl.ds(side, count), pl.ds(2 * n_inner + lane, width_)
+                    ]
+                    target = down_ref.at[
+                        :,
+                        pl.ds((row * cols + col) * deep_down + inside, count),
+                        pl.ds(column, width_),
+                    ]
+                    copies.append(pltpu.make_async_copy(source, target, down_sem.at[len(copies)]))
+            else:
+                for row in range(rows):
+                    target = down_ref.at[:, pl.ds((row * cols + col) * deep_down, deep_down)]
+                    copies.append(
+                        pltpu.make_async_copy(
+                            down_hbm.at[:, col, row], target, down_sem.at[len(copies)]
+                        )
+                    )
+        return copies
+
+    for copy in inner_copies():
+        copy.start()
+    for copy in down_copies():
+        copy.start()
+    chunk = min(TILE, n_down)
+    chunks = [slice(start, start + chunk) for start in range(0, width, chunk)]
+    total = jnp.zeros((1, tokens), f32)
+    squares = jnp.zeros((1, tokens), f32)
+    for here in chunks:
+        part = first_ref[here, :]
+        total = total + jnp.sum(part, axis=0, keepdims=True)
+        squares = squares + jnp.sum(part * part, axis=0, keepdims=True)
+    mean_val = total / width
+    inv_std = lax.rsqrt(squares / width - mean_val * mean_val + EPSILON)
+    for here in chunks:
+        unit = (first_ref[here, :] - mean_val) * inv_std
+        scaled = unit * gain_ref[here, :] + bias_ref[here, :]
+        norm_ref[here, :] = scaled.astype(bf16)
+        turned_ref[:, here] = scaled.T.astype(bf16)
+    for copy in inner_copies():
+        copy.wait()
+    tile = min(TILE, n_inner)
+    spans = [
+        (part, start, min(tile, n_inner - start))
+        for part in range(rows)
+        for start in range(0, n_inner, tile)
+    ]
+    for part, start, size in spans:
+        gate = jnp.dot(
+            turned_ref[...], inner_ref[part, :, start : start + size], preferred_element_type=f32
+        )
+        up = jnp.dot(
+            turned_ref[...],
+            inner_ref[part, :, n_inner + start : n_inner + start + size],
+            preferred_element_type=f32,
+        )
+        there = slice(part * n_inner + start, part * n_inner + start + size)
+        gate_ref[:, there] = gate
+        up_ref[:, there] = up
+        act = gate * jax.nn.sigmoid(gate) * up
+        act_turned_ref[:, there] = act.astype(bf16)
+        act_ref[there, :] = act.T.astype(bf16)
+    for copy in down_copies():
+        copy.wait()
+    factor = factor_ref[0]
+    mask = mask_ref[...]
+    loss = jnp.zeros((1, tokens), f32)
+    for part in range(rows):
+        for start in range(0, n_down, chunk):
+            delta = jnp.dot(
+                act_turned_ref[...],
+                down_ref[part, :, start : start + chunk],
+                preferred_element_type=f32,
+            )
+            here = slice(part * n_down + start, part * n_down + start + chunk)
+            result = first_ref[here, :] + delta.T
+            out_ref[here, :] = result.astype(bf16)
+            error = (result - teacher_ref[here, :].astype(f32)) * mask
+            loss = loss + jnp.sum(error * error, axis=0, keepdims=True)
+            error = error * factor
+            first_grad_ref[here, :] = error
+            low_ref[part, :, start : start + chunk] = error.T.astype(bf16)
+    loss_ref[...] = loss
+    for part, start, size in spans:
+        there = slice(part * n_inner + start, part * n_inner + start + size)
+        back = None
+        for other in range(rows):
+            piece = lax.dot_general(
+                low_ref[other], down_ref[other, there, :], NT, preferred_element_type=f32
+            )
+            back = piece if back is None else back + piece
+        gate, up = gate_ref[:, there], up_ref[:, there]
+        logistic = jax.nn.sigmoid(gate)
+        grads_ref[part, :, start : start + size] = (
+            back * up * logistic * (1.0 + gate * (1.0 - logistic))
+        ).astype(bf16)
+        grads_ref[part, :, n_inner + start : n_inner + start + size] = (
+            back * gate * logistic
+        ).astype(bf16)
+    mean_one = jnp.zeros((1, tokens), f32)
+    mean_two = jnp.zeros((1, tokens), f32)
+    for here in chunks:
+        back = None
+        for part in range(rows):
+            piece = lax.dot_general(
+                grads_ref[part], inner_ref[part, here, :], NT, preferred_element_type=f32
+            )
+            back = piece if back is None else back + piece
+        back = back.T
+        unit = (first_ref[here, :] - mean_val) * inv_std
+        gain_sum_ref[here, :] = jnp.sum(back * unit, axis=1, keepdims=True)
+        bias_sum_ref[here, :] = jnp.sum(back, axis=1, keepdims=True)
+        scaled = back * gain_ref[here, :]
+        mean_one = mean_one + jnp.sum(scaled, axis=0, keepdims=True)
+        mean_two = mean_two + jnp.sum(scaled * unit, axis=0, keepdims=True)
+        first_grad_ref[here, :] = first_grad_ref[here, :] + inv_std * scaled
+    mean_one = mean_one / width
+    mean_two = mean_two / width
+    for here in chunks:
+        unit = (first_ref[here, :] - mean_val) * inv_std
+        first_grad_ref[here, :] = first_grad_ref[here, :] - inv_std * (
+            mean_one + unit * mean_two
+        )
+
+
+def inner_layer(
+    rows, cols, first_out, teacher, mask, factor, gain, bias, weights, inner_cols, hidden
+):
+    width, tokens = first_out.shape
+    f32, bf16 = jnp.float32, jnp.bfloat16
+    vmem = pl.BlockSpec(memory_space=pltpu.VMEM)
+    anywhere = pl.BlockSpec(memory_space=pl.ANY)
+    places = rows * cols
+    if len(weights) == 1:
+        shaped = [weights[0].reshape(rows, cols, -1, weights[0].shape[-1])]
+        down_count = cols * len(packed_pieces(rows, hidden // places, width // rows))
+    else:
+        shaped = [weight.reshape(rows, cols, rows, -1, weight.shape[-1]) for weight in weights]
+        down_count = places
+    return pl.pallas_call(
+        partial(inner_kernel, rows, cols, len(shaped)),
+        in_specs=[vmem, vmem, vmem, pl.BlockSpec(memory_space=pltpu.SMEM)]
+        + [vmem] * 2
+        + [anywhere] * len(shaped),
+        out_specs=[vmem] * 9,
+        out_shape=[
+            jax.ShapeDtypeStruct((width, tokens), bf16),
+            jax.ShapeDtypeStruct((1, tokens), f32),
+            jax.ShapeDtypeStruct((width, tokens), bf16),
+            jax.ShapeDtypeStruct((hidden, tokens), bf16),
+            jax.ShapeDtypeStruct((rows, tokens, width // rows), bf16),
+            jax.ShapeDtypeStruct((rows, tokens, inner_cols), bf16),
+            jax.ShapeDtypeStruct((width, tokens), f32),
+            jax.ShapeDtypeStruct((width, 1), f32),
+            jax.ShapeDtypeStruct((width, 1), f32),
+        ],
+        scratch_shapes=[
+            pltpu.VMEM((rows, width, inner_cols), bf16),
+            pltpu.VMEM((rows, hidden, width // rows), bf16),
+            pltpu.VMEM((tokens, width), bf16),
+            pltpu.VMEM((tokens, hidden), f32),
+            pltpu.VMEM((tokens, hidden), f32),
+            pltpu.VMEM((tokens, hidden), bf16),
+            pltpu.SemaphoreType.DMA((places,)),
+            pltpu.SemaphoreType.DMA((down_count,)),
+        ],
+        compiler_params=pltpu.CompilerParams(vmem_limit_bytes=VMEM_BUDGET),
+        cost_estimate=expected(29),
+        name="inner_layer",
+    )(first_out, teacher, mask, factor, gain, bias, *shaped)
+
+
+def packed_products_kernel(inner_ref, inner_grad_ref, down_ref, down_grad_ref, out_ref, hold_ref):
+    f32, bf16 = jnp.float32, jnp.bfloat16
+    rows, _, depth, _ = inner_ref.shape
+    deep = down_ref.shape[2]
+    start_at = inner_grad_ref.shape[2]
+    columns = down_grad_ref.shape[2]
+    for row in range(rows):
+        out_ref[0, 0, row * depth : (row + 1) * depth, :start_at] = jnp.dot(
+            inner_ref[row, 0], inner_grad_ref[0], preferred_element_type=f32
+        ).astype(bf16)
+        hold_ref[row * deep : (row + 1) * deep, :] = jnp.dot(
+            down_ref[row, 0], down_grad_ref[0], preferred_element_type=f32
+        ).astype(bf16)
+    for start, count, side, lane, width, column in packed_pieces(rows, deep, columns):
+        out_ref[0, 0, side : side + count, start_at + lane : start_at + lane + width] = hold_ref[
+            start : start + count, column : column + width
+        ]
+
+
+def packed_products(rows, cols, inner, inner_grads, down, down_grads):
+    tokens = inner.shape[1]
+    places = rows * cols
+    depth, deep = inner.shape[0] // places, down.shape[0] // places
+    inner_cols, columns = inner_grads.shape[-1], down_grads.shape[-1]
+    total = inner_cols + rows * deep * columns // (rows * depth)
+    return pl.pallas_call(
+        packed_products_kernel,
+        grid=(rows, cols),
+        in_specs=[
+            pl.BlockSpec((rows, 1, depth, tokens), lambda part, col: (0, col, 0, 0)),
+            pl.BlockSpec((1, tokens, inner_cols), lambda part, col: (part, 0, 0)),
+            pl.BlockSpec((rows, 1, deep, tokens), lambda part, col: (0, col, 0, 0)),
+            pl.BlockSpec((1, tokens, columns), lambda part, col: (part, 0, 0)),
+        ],
+        out_specs=pl.BlockSpec((1, 1, rows * depth, total), lambda part, col: (part, col, 0, 0)),
+        out_shape=jax.ShapeDtypeStruct((rows, cols, rows * depth, total), jnp.bfloat16),
+        scratch_shapes=[pltpu.VMEM((rows * deep, columns), jnp.bfloat16)],
+        compiler_params=pltpu.CompilerParams(vmem_limit_bytes=VMEM_BUDGET),
+        cost_estimate=expected(20),
+        name="packed_products",
+    )(
+        inner.reshape(rows, cols, depth, tokens),
+        inner_grads,
+        down.reshape(rows, cols, deep, tokens),
+        down_grads,
+    )
+
+
+def products_kernel(source_ref, grad_ref, out_ref):
+    depth = source_ref.shape[2]
+    for row in range(source_ref.shape[0]):
+        out_ref[0, 0, row * depth : (row + 1) * depth, :] = jnp.dot(
+            source_ref[row, 0], grad_ref[0], preferred_element_type=jnp.float32
+        ).astype(jnp.bfloat16)
+
+
+def local_products(rows, cols, source, grads):
+    height, tokens = source.shape
+    depth = height // (rows * cols)
+    columns = grads.shape[-1]
+    return pl.pallas_call(
+        products_kernel,
+        grid=(rows, cols),
+        in_specs=[
+            pl.BlockSpec((rows, 1, depth, tokens), lambda part, col: (0, col, 0, 0)),
+            pl.BlockSpec((1, tokens, columns), lambda part, col: (part, 0, 0)),
+        ],
+        out_specs=pl.BlockSpec((1, 1, rows * depth, columns), lambda part, col: (part, col, 0, 0)),
+        out_shape=jax.ShapeDtypeStruct((rows, cols, rows * depth, columns), jnp.bfloat16),
+        compiler_params=pltpu.CompilerParams(vmem_limit_bytes=VMEM_BUDGET),
+        cost_estimate=expected(9 if columns < height else 13),
+        name="local_products",
+    )(source.reshape(rows, cols, depth, tokens), grads)
+
+
+PIECES = 2
+GATHER_PIECES = 2
 
 
 def meet_neighbours(side, across):
@@ -908,10 +1389,10 @@
     own_ref, out_ref, local_sem, cross_send, cross_recv, side_send, side_recv, pass_send, pass_recv
 ):
     me, side, across = neighbours()
-    count = own_ref.shape[0] // PIECES
+    count = own_ref.shape[0] // GATHER_PIECES
     meet_neighbours(side, across)
     crossing = []
-    for piece in range(PIECES):
+    for piece in range(GATHER_PIECES):
         rows = pl.ds(piece * count, count)
         copy = push(
             own_ref.at[rows],
@@ -927,7 +1408,7 @@
     local = pltpu.make_async_copy(own_ref, out_ref.at[me], local_sem)
     local.start()
     passing = []
-    for piece in range(PIECES):
+    for piece in range(GATHER_PIECES):
         rows = pl.ds(piece * count, count)
         crossing[piece].wait_recv()
         copy = push(
@@ -939,7 +1420,7 @@
         )
         copy.start()
         passing.append(copy)
-    for piece in range(PIECES):
+    for piece in range(GATHER_PIECES):
         crossing[piece].wait_send()
         passing[piece].wait()
     beside.wait()
@@ -956,14 +1437,15 @@
         out_shape=jax.ShapeDtypeStruct((4,) + own.shape, own.dtype),
         scratch_shapes=[
             dma,
-            dma((PIECES,)),
-            dma((PIECES,)),
+            dma((GATHER_PIECES,)),
+            dma((GATHER_PIECES,)),
             dma,
             dma,
-            dma((PIECES,)),
-            dma((PIECES,)),
+            dma((GATHER_PIECES,)),
+            dma((GATHER_PIECES,)),
         ],
         compiler_params=pltpu.CompilerParams(collective_id=0, has_side_effects=True),
+        cost_estimate=expected(16),
         name="gather_members",
     )(own)
 
@@ -1056,8 +1538,282 @@
         compiler_params=pltpu.CompilerParams(
             collective_id=1, has_side_effects=True, vmem_limit_bytes=VMEM_BUDGET
         ),
+        cost_estimate=expected(3),
         name="reduce_members",
     )(parts)
+
+
+def spread_kernel(
+    blocks,
+    normed_ref,
+    mixed_ref,
+    block_ref,
+    own_ref,
+    local_sem,
+    direct_send,
+    direct_recv,
+    pass_send,
+    pass_recv,
+    mixed_send,
+    mixed_recv,
+):
+    row, col = lax.axis_index("row"), lax.axis_index("col")
+    core, chip = col % 2, col // 2
+    group = block_ref.shape[0]
+    depth = mixed_ref.shape[1]
+    mesh_id = pl.DeviceIdType.MESH
+
+    def spot(of_row, of_col):
+        return pl.ds(pl.multiple_of((of_col * blocks + of_row) * depth, depth), depth)
+
+    def other(across, beyond, twin):
+        to_row = (row + across) % 2
+        to_col = ((chip + beyond) % 2) * 2 + (core + twin) % 2
+        return to_row, to_col
+
+    offsets = [(a, b, t) for a in range(2) for b in range(2) for t in range(2)][1:]
+    barrier = pltpu.get_barrier_semaphore()
+    for offset in offsets:
+        to_row, to_col = other(*offset)
+        pl.semaphore_signal(
+            barrier, inc=1, device_id={"row": to_row, "col": to_col}, device_id_type=mesh_id
+        )
+    pl.semaphore_wait(barrier, len(offsets))
+
+    mine = spot(row, col)
+    direct = []
+    for index, offset in enumerate([(0, 1, 0), (1, 0, 0), (1, 1, 0)]):
+        to_row, to_col = other(*offset)
+        copy = pltpu.make_async_remote_copy(
+            src_ref=normed_ref.at[pl.ds(to_row * group, group)],
+            dst_ref=block_ref.at[:, mine],
+            send_sem=direct_send.at[index],
+            recv_sem=direct_recv.at[index],
+            device_id={"row": to_row, "col": to_col},
+            device_id_type=mesh_id,
+        )
+        copy.start()
+        direct.append(copy)
+    side = {"row": row, "col": chip * 2 + (core + 1) % 2}
+    passing = []
+    own_block = normed_ref.at[pl.ds(row * group, group)]
+    copy = pltpu.make_async_remote_copy(
+        src_ref=own_block,
+        dst_ref=block_ref.at[:, mine],
+        send_sem=pass_send.at[3],
+        recv_sem=pass_recv.at[3],
+        device_id=side,
+        device_id_type=mesh_id,
+    )
+    copy.start()
+    passing.append(copy)
+    spread = []
+    for index, offset in enumerate(offsets):
+        to_row, to_col = other(*offset)
+        copy = pltpu.make_async_remote_copy(
+            src_ref=mixed_ref.at[to_row * 4 + to_col],
+            dst_ref=own_ref.at[mine],
+            send_sem=mixed_send.at[index],
+            recv_sem=mixed_recv.at[index],
+            device_id={"row": to_row, "col": to_col},
+            device_id_type=mesh_id,
+        )
+        copy.start()
+        spread.append(copy)
+    locals_ = [
+        pltpu.make_async_copy(own_block, block_ref.at[:, mine], local_sem.at[0]),
+        pltpu.make_async_copy(mixed_ref.at[row * 4 + col], own_ref.at[mine], local_sem.at[1]),
+    ]
+    for copy in locals_:
+        copy.start()
+    for index, offset in enumerate([(0, 1, 0), (1, 0, 0), (1, 1, 0)]):
+        from_row, from_col = other(*offset)
+        there = spot(from_row, from_col)
+        direct[index].wait_recv()
+        copy = pltpu.make_async_remote_copy(
+            src_ref=block_ref.at[:, there],
+            dst_ref=block_ref.at[:, there],
+            send_sem=pass_send.at[index],
+            recv_sem=pass_recv.at[index],
+            device_id=side,
+            device_id_type=mesh_id,
+        )
+        copy.start()
+        passing.append(copy)
+    for copy in locals_:
+        copy.wait()
+    for copy in passing + spread:
+        copy.wait()
+    for copy in direct:
+        copy.wait_send()
+
+
+def spread_sources(normed, mixed, group):
+    dma = pltpu.SemaphoreType.DMA
+    anywhere = pl.BlockSpec(memory_space=pl.ANY)
+    devices, depth, tokens = normed.shape
+    return pl.pallas_call(
+        partial(spread_kernel, devices // group),
+        in_specs=[anywhere] * 2,
+        out_specs=[anywhere] * 2,
+        out_shape=[
+            jax.ShapeDtypeStruct((group, devices * depth, tokens), normed.dtype),
+            jax.ShapeDtypeStruct((devices * depth, tokens), mixed.dtype),
+        ],
+        scratch_shapes=[
+            dma((2,)),
+            dma((3,)),
+            dma((3,)),
+            dma((4,)),
+            dma((4,)),
+            dma((7,)),
+            dma((7,)),
+        ],
+        compiler_params=pltpu.CompilerParams(collective_id=2, has_side_effects=True),
+        cost_estimate=expected(53),
+        name="spread_sources",
+    )(normed, mixed)
+
+
+def collect_kernel(
+    blocks,
+    normed_ref,
+    mixed_ref,
+    total_ref,
+    own_ref,
+    beside_ref,
+    pair_ref,
+    landed_ref,
+    local_sem,
+    side_send,
+    side_recv,
+    direct_send,
+    direct_recv,
+    mixed_send,
+    mixed_recv,
+):
+    f32, bf16 = jnp.float32, jnp.bfloat16
+    row, col = lax.axis_index("row"), lax.axis_index("col")
+    core, chip = col % 2, col // 2
+    group = normed_ref.shape[0]
+    depth = own_ref.shape[1]
+    mesh_id = pl.DeviceIdType.MESH
+
+    def spot(of_row, of_col):
+        return pl.ds(pl.multiple_of((of_col * blocks + of_row) * depth, depth), depth)
+
+    def other(across, beyond, twin):
+        to_row = (row + across) % 2
+        to_col = ((chip + beyond) % 2) * 2 + (core + twin) % 2
+        return to_row, to_col
+
+    offsets = [(a, b, t) for a in range(2) for b in range(2) for t in range(2)][1:]
+    chips = [(0, 1), (1, 0), (1, 1), (0, 0)]
+    barrier = pltpu.get_barrier_semaphore()
+    for offset in offsets:
+        to_row, to_col = other(*offset)
+        pl.semaphore_signal(
+            barrier, inc=1, device_id={"row": to_row, "col": to_col}, device_id_type=mesh_id
+        )
+    pl.semaphore_wait(barrier, len(offsets))
+
+    side = {"row": row, "col": chip * 2 + (core + 1) % 2}
+    beside, direct, spread = [], [], []
+    for index, (across, beyond) in enumerate(chips):
+        copy = pltpu.make_async_remote_copy(
+            src_ref=normed_ref.at[:, spot(*other(across, beyond, 1))],
+            dst_ref=beside_ref.at[index],
+            send_sem=side_send.at[index],
+            recv_sem=side_recv.at[index],
+            device_id=side,
+            device_id_type=mesh_id,
+        )
+        copy.start()
+        beside.append(copy)
+    for index, offset in enumerate(offsets):
+        to_row, to_col = other(*offset)
+        copy = pltpu.make_async_remote_copy(
+            src_ref=mixed_ref.at[spot(to_row, to_col)],
+            dst_ref=own_ref.at[row * 4 + col],
+            send_sem=mixed_send.at[index],
+            recv_sem=mixed_recv.at[index],
+            device_id={"row": to_row, "col": to_col},
+            device_id_type=mesh_id,
+        )
+        copy.start()
+        spread.append(copy)
+    local = pltpu.make_async_copy(
+        mixed_ref.at[spot(row, col)], own_ref.at[row * 4 + col], local_sem
+    )
+    local.start()
+    for index, (across, beyond) in enumerate(chips):
+        to_row, to_col = other(across, beyond, 0)
+        here = spot(to_row, to_col)
+        beside[index].wait_recv()
+        for step in range(group):
+            total = normed_ref[step, here, :].astype(f32) + beside_ref[index, step].astype(f32)
+            pair_ref[index, step] = total.astype(bf16)
+        if index < 3:
+            copy = pltpu.make_async_remote_copy(
+                src_ref=pair_ref.at[index],
+                dst_ref=landed_ref.at[index],
+                send_sem=direct_send.at[index],
+                recv_sem=direct_recv.at[index],
+                device_id={"row": to_row, "col": to_col},
+                device_id_type=mesh_id,
+            )
+            copy.start()
+            direct.append(copy)
+    direct[0].wait_recv()
+    near = pl.multiple_of(row * group, group)
+    far = pl.multiple_of(((row + 1) % 2) * group, group)
+    for step in range(group):
+        total_ref[near + step] = (
+            pair_ref[3, step].astype(f32) + landed_ref[0, step].astype(f32)
+        ).astype(bf16)
+    direct[1].wait_recv()
+    direct[2].wait_recv()
+    for step in range(group):
+        total_ref[far + step] = (
+            landed_ref[1, step].astype(f32) + landed_ref[2, step].astype(f32)
+        ).astype(bf16)
+    local.wait()
+    for copy in spread:
+        copy.wait()
+    for copy in beside + direct:
+        copy.wait_send()
+
+
+def collect_grads(normed, mixed, devices):
+    dma = pltpu.SemaphoreType.DMA
+    vmem = pl.BlockSpec(memory_space=pltpu.VMEM)
+    anywhere = pl.BlockSpec(memory_space=pl.ANY)
+    group, width, tokens = normed.shape
+    depth = width // devices
+    shape = jax.ShapeDtypeStruct((devices, depth, tokens), normed.dtype)
+    return pl.pallas_call(
+        partial(collect_kernel, devices // group),
+        in_specs=[vmem, anywhere],
+        out_specs=[vmem, anywhere],
+        out_shape=[shape, shape],
+        scratch_shapes=[
+            pltpu.VMEM((4, group, depth, tokens), normed.dtype),
+            pltpu.VMEM((4, group, depth, tokens), normed.dtype),
+            pltpu.VMEM((3, group, depth, tokens), normed.dtype),
+            dma,
+            dma((4,)),
+            dma((4,)),
+            dma((3,)),
+            dma((3,)),
+            dma((7,)),
+            dma((7,)),
+        ],
+        compiler_params=pltpu.CompilerParams(
+            collective_id=3, has_side_effects=True, vmem_limit_bytes=VMEM_BUDGET
+        ),
+        cost_estimate=expected(8),
+        name="collect_grads",
+    )(normed, mixed)
 
 
 def silu_slope(pre_act):
@@ -1183,12 +1939,33 @@
     parts_out = w_output.shape[2] // w_value.shape[2]
     output_local = w_output.reshape(rows, parts_out, w_value.shape[2], -1)
     output_local = [output_local[:, part].reshape(-1, w_output.shape[-1]) for part in range(parts_out)]
-    value_weights = gather_weights(local_matrix([w_value, w_shared]))
-    rest_weights = gather_weights(
-        jnp.concatenate(output_local + [local_matrix([w_reset, w_hidden, w_update])], axis=1)
-    )
-    inner_weights = gather_weights(local_matrix([w_gate, w_up]))
-    down_weights = gather_weights(local_matrix([w_down]))
+    near = rows == 2 and rows == blocks_here and cols == 4
+    n_value, n_shared, n_reset, n_hidden = (
+        weight.shape[-1] for weight in (w_value, w_shared, w_reset, w_hidden)
+    )
+    n_out = w_output.shape[-1]
+    skip_value = n_value + n_shared
+    front_weights = gather_weights(
+        jnp.concatenate(
+            [local_matrix([w_value, w_shared])]
+            + output_local
+            + [local_matrix([w_reset, w_hidden, w_update])],
+            axis=1,
+        )
+    )
+    shared_weights = front_weights[:, :, n_value:skip_value]
+    rest_weights = front_weights[:, :, skip_value:]
+    inner_local, down_local = local_matrix([w_gate, w_up]), local_matrix([w_down])
+    deep_down = w_down.shape[2]
+    if near:
+        sides = [[[], []], [[], []], [[], []]]
+        for start, count, side, lane, width, column in packed_pieces(rows, deep_down, n_out):
+            piece = down_local[start : start + count, column : column + width]
+            sides[lane // n_out][side // UNIT].append(piece)
+        columns = [jnp.concatenate(tops + bottoms, axis=0) for tops, bottoms in sides]
+        inner_weights = [gather_weights(jnp.concatenate([inner_local] + columns, axis=1))]
+    else:
+        inner_weights = [gather_weights(inner_local), gather_weights(down_local)]
     feat_share, z_share = final_gain.shape[0], query_gain.shape[0]
 
     def whole_vector(start, share):
@@ -1204,21 +1981,25 @@
     positions = jnp.concatenate([chunk * half + jnp.arange(half) for chunk, offset in pieces])
     valid_mask = (positions < block_len[my_block]).astype(jnp.float32)
 
-    send, send_plain, *saved = front_forward(
+    send_normed, send_mixed, send_plain, *saved = front_forward(
         layer_input, teacher, state_params, channel_params, bounds, places, devices
     )
-    sources = exchange(send)
     feats = layer_input.shape[0]
-    sources = sources.reshape(rows, cols, 2, feats, tokens).transpose(2, 1, 0, 3, 4)
-    sources = sources.reshape(2, devices * feats, tokens)
-    normed_low, mixed_low = sources[0], sources[1]
-    n_value, n_shared, n_reset, n_hidden = (
-        weight.shape[-1] for weight in (w_value, w_shared, w_reset, w_hidden)
-    )
-    n_out = w_output.shape[-1]
+    if near:
+        block_normed, mixed_low = spread_sources(send_normed, send_mixed, group)
+    else:
+        whole_normed = exchange(send_normed).reshape(devices * feats, tokens)
+        block_normed = lax.dynamic_slice_in_dim(
+            lax.all_gather(swap_blocks(whole_normed, rows, cols), grid, axis=0),
+            my_block * group,
+            group,
+            0,
+        )
+        mixed_low = swap_blocks(
+            exchange(send_mixed).reshape(devices * feats, tokens), rows, cols
+        )
     skip_out = parts_out * n_out
-    value_pre = project(value_weights[:, :, :n_value], normed_low)
-    shared = project(value_weights[:, :, n_value:], mixed_low)
+    shared = project(shared_weights, mixed_low)
     mixed_out = [
         contract_first(rest_weights[part, :, skip_out:], mixed_low) for part in range(rows)
     ]
@@ -1229,25 +2010,23 @@
     reset_pre = mixed_slice(0, n_reset)
     hidden_pre = mixed_slice(n_reset, n_hidden)
     update_pre = mixed_slice(n_reset + n_hidden, n_hidden)
-    values_low = silu(value_pre).astype(bf16)
     queries = (shared * query_gain_all[:, None] + query_bias_all[:, None]).astype(bf16)
     keys_low = (shared * key_gain_all[:, None]).astype(bf16)
-    key_values = jnp.concatenate([values_low, keys_low], axis=0)
-    near = rows == blocks_here and cols == 4
     if near:
-        gathered_kv = gather_members(key_values)
+        block_keys = gather_members(keys_low)
     else:
-        gathered_kv = lax.dynamic_slice_in_dim(
-            lax.all_gather(key_values, grid, axis=0), my_block * group, group, 0
-        )
-    width = values_low.shape[0]
-    send_plain, gathered_kv = barrier((send_plain, gathered_kv))
+        block_keys = lax.dynamic_slice_in_dim(
+            lax.all_gather(keys_low, grid, axis=0), my_block * group, group, 0
+        )
+    values_low, value_bends = block_values(front_weights, block_normed, n_value)
+    send_plain, block_keys = barrier((send_plain, block_keys))
     plain = exchange(send_plain)
-    plain = plain.astype(jnp.float32)
-    input_slots = plain[:, 0].reshape(devices * feats, tokens)
+    input_slots = plain[:, 0].reshape(devices * feats, tokens).astype(jnp.float32)
     teacher_slots = plain[:, 1].reshape(devices * feats, tokens)
 
-    attended, logs = attention_forward(member[None], queries, gathered_kv, group)
+    attended, logs = attention_forward(
+        member[None], queries, block_keys, values_low, group
+    )
     reset_act = silu(reset_pre)
     att_in = (attended * reset_act).astype(bf16)
     att_in = att_in.reshape(rows, cols, parts_out, -1, tokens).transpose(2, 1, 0, 3, 4)
@@ -1260,59 +2039,59 @@
     hidden_act = silu(summed)
     gate_act = jax.nn.sigmoid(update_pre)
     first_out = input_slots + gate_act * (hidden_act - input_slots)
-    mean_val = jnp.mean(first_out, axis=0)
-    inv_std = lax.rsqrt(jnp.mean(first_out * first_out, axis=0) - mean_val * mean_val + EPSILON)
-    unit_norm = (first_out - mean_val) * inv_std
-    final_norm = swap_blocks(
-        (unit_norm * gain_all[:, None] + bias_all[:, None]).astype(bf16), rows, cols
-    )
-    n_inner = w_gate.shape[-1]
-    inner_out = [contract_first(inner_weights[part], final_norm) for part in range(rows)]
-    gate_pre = jnp.concatenate([piece[:n_inner] for piece in inner_out], axis=0)
-    up_pre = jnp.concatenate([piece[n_inner:] for piece in inner_out], axis=0)
-    inner_act = swap_blocks((silu(gate_pre) * up_pre).astype(bf16), rows, cols)
-    output_slots = first_out + project(down_weights, inner_act)
-    out_error = (output_slots - teacher_slots) * valid_mask
-    loss_part = jnp.sum(out_error * out_error)
-    out_grad = out_error * (slot_count * dps / valid_total)
-
-    out_low = out_grad.astype(bf16)
-    inner_grad = swap_blocks(project_back(down_weights, out_low), cols, rows)
-    gate_grad = (inner_grad * up_pre * silu_slope(gate_pre)).astype(bf16)
-    up_grad = (inner_grad * silu(gate_pre)).astype(bf16)
-    inner_grads = jnp.concatenate(
-        [gate_grad.reshape(rows, -1, tokens), up_grad.reshape(rows, -1, tokens)], axis=1
-    )
-    norm_grad = swap_blocks(
-        project_back(inner_weights, inner_grads.reshape(-1, tokens)), cols, rows
-    )
+    factor = slot_count * dps / valid_total
+    (
+        output_low,
+        loss_rows,
+        final_norm,
+        inner_act,
+        out_low,
+        inner_grads,
+        first_grad,
+        final_gain_part,
+        final_bias_part,
+    ) = inner_layer(
+        rows,
+        cols,
+        first_out,
+        teacher_slots,
+        valid_mask[None],
+        factor[None],
+        gain_all[:, None],
+        bias_all[:, None],
+        inner_weights,
+        w_gate.shape[-1] + w_up.shape[-1],
+        rows * w_gate.shape[-1],
+    )
+    loss_part = jnp.sum(loss_rows)
+
+    def scatter_products(products):
+        shaped = products.reshape((devices,) + products.shape[2:])
+        return lax.psum_scatter(shaped, grid, scatter_dimension=0, tiled=True)[0]
 
     def scatter_weight(product_list, rank):
-        stacked = jnp.stack(product_list)
-        shaped = stacked.reshape(devices, rows * rank, stacked.shape[-1])
+        shaped = product_list.reshape(devices, rows * rank, product_list.shape[-1])
         return lax.psum_scatter(shaped, grid, scatter_dimension=0, tiled=True)[0]
 
-    down_sum = scatter_weight(weight_products(inner_act, out_low, rows), w_down.shape[2])
-    inner_sum = scatter_weight(weight_products(final_norm, inner_grads, rows), w_gate.shape[2])
-    down_sum, inner_sum, valid_all = barrier((down_sum, inner_sum, valid_all))
-    down_sum, inner_sum = lax.psum((down_sum, inner_sum), "dp")
-
-    final_gain_part = jnp.sum(norm_grad * unit_norm, axis=1)
-    final_bias_part = jnp.sum(norm_grad, axis=1)
-    unit_grad = norm_grad * gain_all[:, None]
-    first_grad = out_grad + inv_std * (
-        unit_grad
-        - jnp.mean(unit_grad, axis=0)
-        - unit_norm * jnp.mean(unit_grad * unit_norm, axis=0)
-    )
+    if near:
+        inner_products = packed_products(
+            rows, cols, final_norm, inner_grads, inner_act, out_low
+        )
+        inner_products, first_grad = barrier((inner_products, first_grad))
+        inner_sums = (scatter_products(inner_products),)
+    else:
+        inner_sums = (
+            scatter_products(local_products(rows, cols, final_norm, inner_grads)),
+            scatter_products(local_products(rows, cols, inner_act, out_low)),
+        )
     direct = exchange(
         jnp.stack(
             [
-                (first_grad * (1.0 - gate_act)).reshape(devices, feats, tokens),
-                output_slots.reshape(devices, feats, tokens),
+                (first_grad * (1.0 - gate_act)).astype(bf16).reshape(devices, feats, tokens),
+                output_low.reshape(devices, feats, tokens),
             ],
             axis=1,
-        ).astype(bf16)
+        )
     )
     update_grad = (first_grad * (hidden_act - input_slots) * gate_act * (1.0 - gate_act)).astype(
         bf16
@@ -1339,49 +2118,80 @@
             weight_products(mixed_low, mixed_grads, rows),
         )
     ]
-    query_grad, kv_parts = attention_backward(
-        member[None], queries, gathered_kv, attended_grad, logs, group
-    )
-    kv_parts, direct = barrier((kv_parts, direct))
+    rest_products, attended_grad = barrier((jnp.stack(rest_products), attended_grad))
+    rest_sum = scatter_weight(rest_products, w_value.shape[2])
+    query_grad, key_parts, value_parts = attention_backward(
+        member[None], queries, block_keys, values_low, value_bends, attended_grad, logs, group
+    )
+    key_parts, direct = barrier((key_parts, direct))
     if near:
-        kv_grads = reduce_members(kv_parts)
+        key_grad = reduce_members(key_parts)
     else:
         spread = lax.dynamic_update_slice_in_dim(
-            jnp.zeros((devices,) + kv_parts.shape[1:], bf16), kv_parts, my_block * group, 0
-        )
-        kv_grads = lax.psum_scatter(spread, grid, scatter_dimension=0, tiled=True)[0]
-    kv_grads, rest_products = barrier((kv_grads, rest_products))
-    rest_sum = scatter_weight(rest_products, w_value.shape[2])
-    rest_sum, down_sum, inner_sum = barrier((rest_sum, down_sum, inner_sum))
-    rest_sum = lax.psum(rest_sum, "dp")
-    value_grad, key_grad = kv_grads[:width].astype(jnp.float32), kv_grads[width:].astype(jnp.float32)
-    value_pre_grad = (value_grad * silu_slope(value_pre)).astype(bf16)
+            jnp.zeros((devices,) + key_parts.shape[1:], bf16), key_parts, my_block * group, 0
+        )
+        key_grad = lax.psum_scatter(spread, grid, scatter_dimension=0, tiled=True)[0]
+        key_grad = key_grad.astype(jnp.float32)
+    normed_back = block_values_back(front_weights, value_parts, n_value)
     shared_grad = (
         query_grad * query_gain_all[:, None] + key_grad * key_gain_all[:, None]
     ).astype(bf16)
     query_gain_part = jnp.sum(query_grad * shared, axis=1)
     query_bias_part = jnp.sum(query_grad, axis=1)
     key_gain_part = jnp.sum(key_grad * shared, axis=1)
-    normed_back = project_back(value_weights[:, :, :n_value], value_pre_grad)
     mixed_back = project_back(
         rest_weights[:, :, skip_out:], mixed_grads.reshape(-1, tokens)
-    ) + project_back(value_weights[:, :, n_value:], shared_grad)
-    backs = jnp.stack([normed_back, mixed_back]).astype(bf16)
-    backs = backs.reshape(2, cols, rows, feats, tokens).transpose(2, 1, 0, 3, 4)
-    backs = exchange(backs.reshape(devices, 2, feats, tokens))
-    layer_output, input_grad, state_grads, channel_grads = front_backward(
-        layer_input, state_params, channel_params, bounds, places, devices, backs, direct, saved
-    )
+    ) + project_back(shared_weights, shared_grad)
+    mixed_back = mixed_back.astype(bf16)
+    if near:
+        normed_grads, mixed_backs = collect_grads(normed_back, mixed_back, devices)
+    else:
+        spread = lax.dynamic_update_slice_in_dim(
+            jnp.zeros((devices,) + normed_back.shape[1:], bf16), normed_back, my_block * group, 0
+        )
+        spread = spread.reshape(devices, cols, rows, feats, tokens).transpose(2, 1, 0, 3, 4)
+        normed_grads = lax.psum_scatter(
+            spread.reshape((devices, devices, feats, tokens)), grid, scatter_dimension=0, tiled=True
+        )[0]
+        mixed_backs = exchange(
+            swap_blocks(mixed_back, cols, rows).reshape(devices, feats, tokens)
+        )
+    inner_sums, valid_all, normed_grads = barrier((inner_sums, valid_all, normed_grads))
+    inner_sums = lax.psum(inner_sums, "dp")
+    groups = feats // GS
+    shares = [(0, groups)]
+    if groups % 2 == 0:
+        shares = [(0, groups // 2), (groups // 2, groups // 2)]
+    filled = ()
+    for first, count in shares:
+        if filled:
+            rest_sum, inner_sums, filled = barrier((rest_sum, inner_sums, filled))
+            rest_sum = lax.psum(rest_sum, "dp")
+        filled = front_backward(
+            layer_input,
+            state_params,
+            channel_params,
+            bounds,
+            places,
+            devices,
+            normed_grads,
+            mixed_backs,
+            direct,
+            saved,
+            first,
+            count,
+            filled,
+        )
+    layer_output, input_grad, state_grads, channel_grads = filled
     param_grads = front_parameter_grads(state_grads, channel_grads, ema_rate, ema_input)
 
-    value_products = [
-        jnp.concatenate(pair, axis=1)
-        for pair in zip(
-            weight_products(normed_low, value_pre_grad, rows),
-            weight_products(mixed_low, shared_grad, rows),
-        )
-    ]
+    value_part = block_values_products(rows, block_normed, value_parts)
+    shared_part = weight_products(mixed_low, shared_grad, rows)
+    value_products = jnp.concatenate([value_part, jnp.stack(shared_part)], axis=2)
     value_sum = scatter_weight(value_products, w_value.shape[2])
+    if len(shares) == 1:
+        rest_sum, inner_sums = barrier((rest_sum, inner_sums))
+        rest_sum = lax.psum(rest_sum, "dp")
     value_sum, rest_sum = barrier((value_sum, rest_sum))
     value_sum = lax.psum(value_sum, "dp")
 
@@ -1417,8 +2227,20 @@
         axis=1,
     )
     output_g = output_g.astype(jnp.float32).reshape(w_output.shape)
-    gate_g, up_g = split_columns(inner_sum, [w_gate, w_up])
-    (down_g,) = split_columns(down_sum, [w_down])
+    gate_g, up_g = split_columns(inner_sums[0], [w_gate, w_up])
+    if near:
+        packed_down = inner_sums[0][:, w_gate.shape[-1] + w_up.shape[-1] :]
+        strips = {}
+        for start, count, side, lane, width, column in packed_pieces(rows, deep_down, n_out):
+            strips.setdefault(start, []).append(
+                packed_down[side : side + count, lane : lane + width]
+            )
+        down_g = jnp.concatenate(
+            [jnp.concatenate(strips[start], axis=1) for start in sorted(strips)], axis=0
+        )
+    else:
+        down_g = inner_sums[1]
+    down_g = down_g.astype(jnp.float32).reshape(w_down.shape)
     return (
         layer_output,
         loss_value,

time: 894 us -> 692 us (0.77)
  waiting for transfers between devices: 193 us -> 58.7 us
  Pallas kernels: 308 us -> 396 us
  matrix products: 127 us -> 63.7 us
  other arithmetic: 97.6 us -> 49 us
  local copies, waits for them, and re-layouts: 87.6 us -> 56.9 us
    pallas_call x1 -> x9, Pallas kernels: 76.6 us -> 286 us  [the longest x2 79.7 us: front_backward(): pl.pallas_call(partial(front_backward_kernel, places, units, len(filled))...]
    pallas_call x1, Pallas kernels: 97.2 us -> 10.6 us  [gather_members(): pl.pallas_call(gather_kernel, in_specs=[anywhere], out_specs=anywhere, ou...]
    all_to_all x6 -> x4, waiting for transfers between devices: 82.6 us -> 2.9 us  [exchange(): return lax.all_to_all(array_in, grid, 0, 0, tiled=True)]
    pallas_call x1, Pallas kernels: 61.9 us -> 19 us  [reduce_members(): pl.pallas_call(reduce_kernel, in_specs=[vmem], out_specs=vmem, out_shape=...]
    reduce_scatter x4 -> x2, waiting for transfers between devices: 35.8 us -> 0.03 us  [scatter_weight(): return lax.psum_scatter(shaped, grid, scatter_dimension=0, tiled=True)[0]]
    psum x1, waiting for transfers between devices: 31.2 us -> 0.01 us  [shards(): rest_sum = lax.psum(rest_sum, 'dp')]
    dot_general x14 -> x8, matrix products: 41 us -> 12.3 us  [contract_last(): lax.dot_general(left_in, right_in, (((1,), (1,)), ((), ())), preferred_el...]
    dot_general x14 -> x8, matrix products: 47.6 us -> 24.9 us  [project_back(): jnp.dot(weights[part], pieces[part], preferred_element_type=jnp.float32)]
  transfers between devices with their start and end apart: 18 -> 13, of which waited for: 7 -> 4; matrix products, arithmetic and copies ran while one was open for 29% -> 22% of each run, Pallas kernels for 35% -> 51%
where the time goes in v3:
time: 692 us; the launch traced here: 684 us
  Pallas kernels  396 us (57%)
  matrix products  63.7 us (9%)
  waiting for transfers between devices  58.7 us (8%)
  local copies, waits for them, and re-layouts  56.9 us (8%)
  other arithmetic  49 us (7%)
  between operations  20.8 us (3%)
  blocking collectives  19.8 us (3%)
  starting transfers between devices  19.3 us (3%)
    pallas_call x2, Pallas kernels, front_backward(): pl.pallas_call(partial(front_backward_kernel, places, units, len(filled))...  79.7 us
    pallas_call x1, Pallas kernels, spread_sources(): pl.pallas_call(partial(spread_kernel, devices // group), in_specs=[anywhe...  72.3 us
    pallas_call x1, Pallas kernels, collect_grads(): pl.pallas_call(partial(collect_kernel, devices // group), in_specs=[vmem,...  42.4 us
    pallas_call x1, Pallas kernels, front_forward(): pl.pallas_call(partial(front_forward_kernel, places, units), grid=(groups...  35.3 us
    psum x1, waiting for transfers between devices, shards(): value_sum = lax.psum(value_sum, 'dp')  32.2 us
    pallas_call x1, Pallas kernels, attention_backward(): pl.pallas_call(partial(attention_backward_kernel, group), in_specs=[pl.Bl...  29.6 us
    pallas_call x1, Pallas kernels, inner_layer(): pl.pallas_call(partial(inner_kernel, rows, cols, len(shaped)), in_specs=[...  28 us
    dot_general x8, matrix products, contract_first(): lax.dot_general(left_in, right_in, (((0,), (0,)), ((), ())), preferred_el...  26.5 us
  transfers between devices with their start and end apart: 13, of which 4 were waited for; matrix products, arithmetic and copies ran while one was open for 22% of the time, Pallas kernels for 51%

profile of v3, /device:TPU:0, one launch (start us, length us, event | category | flops | bytes accessed | tf_op | source)
XLA Modules:
  0.0 684.3 jit_solution(7686321965009902732)
XLA Ops:
  18.6 5.2 all-to-all-start
  29.7 35.3 %front_forward.1 = (bf16[8,128,512]{2,1,0:T(8,128)(2,1)}, bf16[8,128,512]{2,1,0:T(8,128)(2,1)}, bf16[8,2,128,512]{3,2,1,0:T(8,128)(2,1)}, f32[4,1024,128]{2,1,0:...) custom-call(s32[1,32]{1,0:T(1,128)} %bitcast.267, ...), custom_call_target="tpu_custom_call" | custom-call | flops 40249999360 | tf_op jit(solution)/shard_map/front_forward/pallas_call | solution.py:484
  65.1 72.3 %spread_sources.1 = (bf16[4,1024,512]{2,1,0:T(8,128)(2,1)}, bf16[1024,512]{1,0:T(8,128)(2,1)}) custom-call(bf16[8,128,512]{2,1,0:T(8,128)(2,1)} %get-tuple-element.80.normed_ref, bf16[8,128,512]{2,1,0:T(8,128)(2,1)} %get-tuple-element.81.mixed_ref), custom_call_target="tpu_custom_call" | custom-call | flops 60949999616 | tf_op jit(solution)/shard_map/spread_sources/pallas_call | solution.py:1655
  147.1 10.6 %gather_members.1.key_ref = bf16[4,256,512]{2,1,0:T(8,128)(2,1)} custom-call(bf16[256,512]{1,0:T(8,128)(2,1)} %get-tuple-element.184.own_ref), custom_call_target="tpu_custom_call" | custom-call | flops 18400000000 | tf_op jit(solution)/shard_map/gather_members/pallas_call | solution.py:1433
  157.7 4.6 all-to-all-start.1
  162.6 4.6 fusion.7
  167.4 6.0 fusion.5
  176.0 19.3 %block_values.1 = (bf16[4,2048,512]{2,1,0:T(8,128)(2,1)}, bf16[4,2048,512]{2,1,0:T(8,128)(2,1)}) custom-call(bf16[2,1024,4224]{2,1,0:T(8,128)(2,1)} %bitcast.186, bf16[4,1024,512]{2,1,0:T(8,128)(2,1)} %get-tuple-element.85.source_ref), custom_call_target="tpu_custom_call" | custom-call | flops 21849999360 | tf_op jit(solution)/shard_map/block_values/pallas_call | solution.py:919
  195.3 15.7 %attention_forward.1 = (f32[2048,512]{1,0:T(8,128)}, f32[512,128]{1,0:T(8,128)}) custom-call(s32[1]{0:T(128)} %bitcast.19.member_ref, bf16[256,512]{1,0:T(8,128)(2,1)} %get-tuple-element.183.query_ref, bf16[4,256,512]{2,1,0:T(8,128)(2,1)} %gather_members.1.key_ref, bf16[4,2048,512]{2,1,0:T(8,128)(2,1)} %get-tuple-element.86.value_ref), custom_call_target="tpu_custom_call" | custom-call | flops 18400000000 | tf_op jit(solution)/shard_map/attention_forward/pallas_call | solution.py:854
  210.9 4.2 multiply_convert_fusion
  215.6 3.7 fusion.19
  219.3 2.9 fusion.18
  222.3 3.1 fusion.16
  225.3 3.1 fusion.15
  228.5 2.1 fusion.39
  230.6 2.9 fusion.41
  234.4 4.4 convert_add_fusion
  238.8 13.4 %all-gather.7.cloned.1.call-done = bf16[2048,3840]{1,0:T(8,128)(2,1)} async-done(((bf16[256,3840]{1,0:T(8,128)(2,1)}), bf16[2048,3840]{1,0:T(8,128)(2,1)}) %all-gather.7.cloned.1.call-update) | async-done | bytes 15728656 | tf_op jit(solution)/shard_map/all_gather | solution.py:1922
  252.2 28.0 %inner_layer.1 = (bf16[1024,512]{1,0:T(8,128)(2,1)}, f32[1,512]{1,0:T(1,128)}, bf16[1024,512]{1,0:T(8,128)(2,1)}, bf16[2560,512]{1,0:T(8,128)(2,1)}, bf16[2,512,...) custom-call(f32[1024,512]{1,0:T(8,128)} %get-tuple-element.148.first, ...), custom_call_target="tpu_custom_call" | custom-call | flops 33350000640 | tf_op jit(solution)/shard_map/inner_layer/pallas_call | solution.py:1251
  280.3 16.9 %packed_products.1 = bf16[2,4,256,3840]{3,2,1,0:T(8,128)(2,1)} custom-call(bf16[2,4,128,512]{3,2,1,0:T(8,128)(2,1)} %bitcast.274, bf16[2,512,2560]{2,1,0:T(8,128)(2,1)} %get-tuple-element.89.inner_grad_ref, bf16[2,4,320,512]{3,2,1,0:T(8,128)(2,1)} %bitcast.273, bf16[2,512,512]{2,1,0:T(8,128)(2,1)} %get-tuple-element.91.down_grad_ref), custom_call_target="tpu_custom_call" | custom-call | flops 23000000512 | tf_op jit(solution)/shard_map/packed_products/pallas_call | solution.py:1309
  297.2 5.0 multiply_convert_fusion.3
  304.8 2.4 copy.150
  307.3 3.5 convolution_convert_fusion.5
  310.8 2.4 copy.149
  313.2 2.4 fusion.14
  315.6 2.2 fusion.17
  326.7 3.6 fusion.2
  330.6 2.4 convolution_convert_fusion
  333.1 2.4 convolution_convert_fusion.1
  337.0 5.5 pad_maximum_fusion
  345.5 3.6 all-to-all-start.2
  349.4 29.6 %attention_backward.1 = (f32[256,512]{1,0:T(8,128)}, bf16[4,256,512]{2,1,0:T(8,128)(2,1)}, bf16[4,2048,512]{2,1,0:T(8,128)(2,1)}) custom-call(s32[1]{0:T(128)} %bitcast.19.member_ref, bf16[256,512]{1,0:T(8,128)(2,1)} %get-tuple-element.183.query_ref, bf16[4,256,512]{2,1,0:T(8,128)(2,1)} %gather_members.1.key_ref, ...), custom_call_target="tpu_custom_call" | custom-call | flops 9200000000 | tf_op jit(solution)/shard_map/attention_backward/pallas_call | solution.py:878
  379.0 13.2 %block_values_back.1.normed_ref = bf16[4,1024,512]{2,1,0:T(8,128)(2,1)} custom-call(bf16[2,1024,4224]{2,1,0:T(8,128)(2,1)} %bitcast.195, bf16[4,2048,512]{2,1,0:T(8,128)(2,1)} %get-tuple-element.98.grad_ref), custom_call_target="tpu_custom_call" | custom-call | flops 5750000128 | tf_op jit(solution)/shard_map/block_values_back/pallas_call | solution.py:954
  392.1 6.7 fusion.6
  398.8 5.8 fusion.4
  404.7 19.0 %reduce_members.1 = f32[256,512]{1,0:T(8,128)} custom-call(bf16[4,256,512]{2,1,0:T(8,128)(2,1)} %get-tuple-element.102.parts_ref), custom_call_target="tpu_custom_call" | custom-call | flops 3449999872 | tf_op jit(solution)/shard_map/reduce_members/pallas_call | solution.py:1527
  426.8 2.4 add_convert_fusion.mixed_ref
  429.2 42.4 %collect_grads.1 = (bf16[8,128,512]{2,1,0:T(8,128)(2,1)}, bf16[8,128,512]{2,1,0:T(8,128)(2,1)}) custom-call(bf16[4,1024,512]{2,1,0:T(8,128)(2,1)} %block_values_back.1.normed_ref, bf16[1024,512]{1,0:T(8,128)(2,1)} %add_convert_fusion.mixed_ref), custom_call_target="tpu_custom_call" | custom-call | flops 9200000000 | tf_op jit(solution)/shard_map/collect_grads/pallas_call | solution.py:1794
  471.7 14.0 %block_values_products.1 = bf16[2,1024,1024]{2,1,0:T(8,128)(2,1)} custom-call(bf16[4,1024,512]{2,1,0:T(8,128)(2,1)} %get-tuple-element.85.source_ref, bf16[4,2048,512]{2,1,0:T(8,128)(2,1)} %get-tuple-element.98.grad_ref), custom_call_target="tpu_custom_call" | custom-call | flops 5750000128 | tf_op jit(solution)/shard_map/block_values_products/pallas_call | solution.py:983
  486.5 5.3 maximum_maximum_fusion
  495.5 4.8 all-to-all-start.3
  502.2 2.9 all-to-all-done.3
  505.1 39.9 %front_backward.2 = (f32[128,4096]{1,0:T(8,128)}, f32[128,4096]{1,0:T(8,128)}, f32[2048,8]{1,0:T(8,128)}, f32[128,8]{1,0:T(8,128)}) custom-call(s32[1,32]{1,0:T(1,128)} %bitcast.268, s32[1,32]{1,0:T(1,128)} %bitcast.270, s32[32,1]{1,0:T(8,128)} %copy-done.49, s32[32,1]{1,0:T(8,128)} %copy-done.50, f32[128,4096]{1,0:T(8,128)} %refs_4_.3, ...), custom_call_target="tpu_custom_call" | custom-call | flops 46000001024 | tf_op jit(solution)/shard_map/front_backward/pallas_call | solution.py:546
  545.0 10.0 %all-reduce.8.cloned.1.call-done = bf16[256,3840]{1,0:T(8,128)(2,1)} async-done(((bf16[256,3840]{1,0:T(8,128)(2,1)}), bf16[256,3840]{1,0:T(8,128)(2,1)}) %all-reduce.8.cloned.1.call-update) | async-done | bytes 1966096 | tf_op jit(solution)/shard_map/psum | solution.py:2160
  559.7 39.9 %front_backward.3 = (f32[128,4096]{1,0:T(8,128)}, f32[128,4096]{1,0:T(8,128)}, f32[2048,8]{1,0:T(8,128)}, f32[128,8]{1,0:T(8,128)}) custom-call(s32[1,32]{1,0:T(1,128)} %bitcast.269, s32[1,32]{1,0:T(1,128)} %bitcast.271, s32[32,1]{1,0:T(8,128)} %copy-done.49, ...), custom_call_target="tpu_custom_call", output_to_operand_aliasing={{0}: (15, {}), {1}: (16, {}), {2}: (17, {}), {3}: (18, {})} | custom-call | flops 46000001024 | tf_op jit(solution)/shard_map/front_backward/pallas_call | solution.py:546
  604.9 2.5 fusion.46
  612.3 19.8 %all-reduce = (f32[353]{0:T(512)S(1)}, f32[128]{0:T(128)}, f32[128]{0:T(128)}, f32[128,16]{0,1:T(8,128)}, f32[128,16]{0,1:T(8,128)}, /*index=5*/f32[128,16]{0,1:...) all-reduce(f32[353]{0:T(512)S(1)} %reduce_sum.59, ...), channel_id=1, replica_groups=mesh['dp'=4,'row'=2,'col'=4] {'dp'}, use_global_device_ids=true, to_apply=%region_12.13 | all-reduce | flops 10977 | bytes 87816 | tf_op jit(solution)/shard_map/psum | solution.py:2205
  639.7 32.2 %all-reduce.12.cloned.1.call-done = bf16[256,1152]{1,0:T(8,128)(2,1)} async-done(((bf16[256,1152]{1,0:T(8,128)(2,1)}), bf16[256,1152]{1,0:T(8,128)(2,1)}) %all-reduce.12.cloned.1.call-update) | async-done | bytes 589840 | tf_op jit(solution)/shard_map/psum | solution.py:2196
  (303 shorter events, 79.6 us)
Async XLA Ops:
  8.0 3.3 copy-start.48
  8.1 3.4 copy-start.43
  8.1 133.0 %all-reduce.6.cloned.1.call-start = ((), (), s32[]{:S(2)}) async-start(), calls=%async_computation.7 | async-start | bytes 2097152 | tf_op jit(solution)/shard_map/psum | solution.py:1937
  11.3 131.8 %all-gather.5.cloned.1.call-start = ((), (), s32[]{:S(2)}) async-start(), calls=%async_computation.14 | async-start | bytes 19464192 | tf_op jit(solution)/shard_map/all_gather | solution.py:1922
  14.1 238.1 %all-gather.7.cloned.1.call-start = ((), (), s32[]{:S(2)}) async-start(), calls=%async_computation.15 | async-start | bytes 17694720 | tf_op jit(solution)/shard_map/all_gather | solution.py:1922
  15.4 8.4 %copy-start.69 = (s32[2]{0:T(128)S(1)}, s32[2]{0:T(128)}, u32[]{:S(2)}) copy-start(s32[2]{0:T(128)} %param.28) | copy-start | bytes 28
  15.4 8.9 %copy-start.70 = (s32[2]{0:T(128)S(1)}, s32[2]{0:T(128)}, u32[]{:S(2)}) copy-start(s32[2]{0:T(128)} %param.29) | copy-start | bytes 28
  15.5 10.4 %copy-start.46 = (f32[128,16]{0,1:T(8,128)S(1)}, f32[128,16]{0,1:T(8,128)}, u32[]{:S(2)}) copy-start(f32[128,16]{0,1:T(8,128)} %param.32) | copy-start | bytes 24580
  15.5 10.4 %copy-start.51 = (f32[128,16]{0,1:T(8,128)S(1)}, f32[128,16]{0,1:T(8,128)}, u32[]{:S(2)}) copy-start(f32[128,16]{0,1:T(8,128)} %param.34) | copy-start | bytes 24580
  15.5 10.4 %copy-start.60 = (f32[128,16]{0,1:T(8,128)S(1)}, f32[128,16]{0,1:T(8,128)}, u32[]{:S(2)}) copy-start(f32[128,16]{0,1:T(8,128)} %param.33) | copy-start | bytes 24580
  15.5 10.7 %copy-start.53 = (f32[128]{0:T(128)S(1)}, f32[128]{0:T(128)}, u32[]{:S(2)}) copy-start(f32[128]{0:T(128)} %param.37) | copy-start | bytes 1540
  15.5 10.7 %copy-start.67 = (f32[128]{0:T(128)S(1)}, f32[128]{0:T(128)}, u32[]{:S(2)}) copy-start(f32[128]{0:T(128)} %param.30) | copy-start | bytes 1540
  15.5 10.7 %copy-start.68 = (f32[128]{0:T(128)S(1)}, f32[128]{0:T(128)}, u32[]{:S(2)}) copy-start(f32[128]{0:T(128)} %param.31) | copy-start | bytes 1540
  15.6 12.2 %copy-start.58 = (f32[128,16]{0,1:T(8,128)S(1)}, f32[128,16]{0,1:T(8,128)}, u32[]{:S(2)}) copy-start(f32[128,16]{0,1:T(8,128)} %param.35) | copy-start | bytes 24580
  15.6 12.4 %copy-start.59 = (f32[128,16]{0,1:T(8,128)S(1)}, f32[128,16]{0,1:T(8,128)}, u32[]{:S(2)}) copy-start(f32[128,16]{0,1:T(8,128)} %param.36) | copy-start | bytes 24580
  18.6 120.1 %all-to-all-start = ((f32[8,1,352]{2,1,0:T(1,128)}), f32[8,1,352]{2,1,0:T(1,128)S(1)}, u32[]{:S(2)}, u32[]{:S(2)}) async-start(f32[8,1,352]{2,1,0:T(1,128)} %broadcast_in_dim.57), calls=%async_computation | async-start | bytes 24576 | tf_op jit(solution)/shard_map/all_to_all | solution.py:1919
  25.2 4.5 copy-start.49
  137.4 7.3 %copy-start.2 = (bf16[1024,512]{1,0:T(8,128)(2,1)S(1)}, bf16[1024,512]{1,0:T(8,128)(2,1)}, u32[]{:S(2)}) copy-start(bf16[1024,512]{1,0:T(8,128)(2,1)} %get-tuple-element.82) | copy-start | bytes 3145732
  138.9 8.2 %copy-start.54 = (f32[256]{0:T(256)}, f32[256]{0:T(256)S(1)}, u32[]{:S(2)}) copy-start(f32[256]{0:T(256)S(1)} %mul.149) | copy-start | bytes 3076
  139.0 8.1 %copy-start.56 = (f32[256]{0:T(256)}, f32[256]{0:T(256)S(1)}, u32[]{:S(2)}) copy-start(f32[256]{0:T(256)S(1)} %mul.145) | copy-start | bytes 3076
  157.7 72.8 %all-to-all-start.1 = ((bf16[8,2,128,512]{3,2,1,0:T(8,128)(2,1)}), bf16[8,2,128,512]{3,2,1,0:T(8,128)(2,1)}, u32[]{:S(2)}, u32[]{:S(2)}) async-start(bf16[8,2,128,512]{3,2,1,0:T(8,128)(2,1)} %get-tuple-element.83), calls=%async_computation.1 | async-start | bytes 4194304 | tf_op jit(solution)/shard_map/all_to_all | solution.py:1919
  162.3 309.3 %reduce-scatter.4.cloned.1.call-start = ((), (), s32[]{:S(2)}) async-start(), calls=%async_computation.8 | async-start | bytes 17694720 | tf_op jit(solution)/shard_map/reduce_scatter | solution.py:2070
  167.2 6.2 copy-start.14
  215.6 3.7 copy-start.33
  215.6 9.8 %copy-start.31 = (bf16[1,4,2,128,512]{4,3,2,1,0:T(8,128)(2,1)}, bf16[1,4,2,128,512]{4,3,2,1,0:T(8,128)(2,1)S(1)}, u32[]{:S(2)}) copy-start(bf16[1,4,2,128,512]{4,3,2,1,0:T(8,128)(2,1)S(1)} %get-tuple-element.161) | copy-start | bytes 3145732
  222.3 6.2 copy-start.17
  230.6 3.9 copy-start.7
  230.6 3.9 copy-start.8
  230.6 3.9 copy-start.19
  230.6 3.8 copy-start.20
  297.1 247.9 %reduce-scatter.6.cloned.1.call-start = ((), (), s32[]{:S(2)}) async-start(), calls=%async_computation.9 | async-start | bytes 14155776 | tf_op jit(solution)/shard_map/reduce_scatter | solution.py:2074
  297.2 6.0 copy-start.34
  322.4 3.5 copy-start.3
  326.7 3.6 copy-start.18
  345.5 59.1 %all-to-all-start.2 = ((bf16[8,2,128,512]{3,2,1,0:T(8,128)(2,1)}), bf16[8,2,128,512]{3,2,1,0:T(8,128)(2,1)S(1)}, u32[]{:S(2)}, u32[]{:S(2)}) async-start(bf16[8,2,128,512]{3,2,1,0:T(8,128)(2,1)} %pad_maximum_fusion.4), calls=%async_computation.3 | async-start | bytes 4194304 | tf_op jit(solution)/shard_map/all_to_all | solution.py:1919
  349.1 205.9 %all-reduce.8.cloned.1.call-start = ((), (), s32[]{:S(2)}) async-start(), calls=%async_computation.10 | async-start | bytes 3932160 | tf_op jit(solution)/shard_map/psum | solution.py:2160
  392.1 6.7 copy-start.12
  404.7 19.1 %copy-start.27 = (bf16[8,2,128,512]{3,2,1,0:T(8,128)(2,1)}, bf16[8,2,128,512]{3,2,1,0:T(8,128)(2,1)S(1)}, u32[]{:S(2)}) copy-start(bf16[8,2,128,512]{3,2,1,0:T(8,128)(2,1)S(1)} %all-to-all-done.2.refs_9_) | copy-start | bytes 6291460
  404.7 19.1 %copy-start.24 = (f32[128,512]{1,0:T(8,128)S(1)}, f32[128,512]{1,0:T(8,128)}, u32[]{:S(2)}) copy-start(f32[128,512]{1,0:T(8,128)} %copy-done.23) | copy-start | bytes 786436
  404.7 19.1 %copy-start.26 = (f32[128,512]{1,0:T(8,128)S(1)}, f32[128,512]{1,0:T(8,128)}, u32[]{:S(2)}) copy-start(f32[128,512]{1,0:T(8,128)} %copy-done.25) | copy-start | bytes 786436
  404.7 19.1 %copy-start.55 = (f32[256]{0:T(256)S(1)}, f32[256]{0:T(256)}, u32[]{:S(2)}) copy-start(f32[256]{0:T(256)} %copy-done.54) | copy-start | bytes 3076
  404.7 19.1 %copy-start.57 = (f32[256]{0:T(256)S(1)}, f32[256]{0:T(256)}, u32[]{:S(2)}) copy-start(f32[256]{0:T(256)} %copy-done.56) | copy-start | bytes 3076
  471.7 162.8 %reduce-scatter.8.cloned.1.call-start = ((), (), s32[]{:S(2)}) async-start(), calls=%async_computation.11 | async-start | bytes 5308416 | tf_op jit(solution)/shard_map/reduce_scatter | solution.py:2074
  495.5 9.6 %all-to-all-start.3 = ((f32[8,1,353]{2,1,0:T(1,128)}), f32[8,1,353]{2,1,0:T(1,128)S(1)}, u32[]{:S(2)}, u32[]{:S(2)}) async-start(f32[8,1,353]{2,1,0:T(1,128)} %copy.157), calls=%async_computation.5 | async-start | bytes 24576 | tf_op jit(solution)/shard_map/all_to_all | solution.py:1919
  500.4 134.1 %all-reduce.10.cloned.1.call-start = ((), (), s32[]{:S(2)}) async-start(), calls=%async_computation.12 | async-start | bytes 3145728 | tf_op jit(solution)/shard_map/psum | solution.py:2169
  500.9 4.2 copy-start.50
  559.5 112.4 %all-reduce.12.cloned.1.call-start = ((), (), s32[]{:S(2)}) async-start(), calls=%async_computation.13 | async-start | bytes 1179648 | tf_op jit(solution)/shard_map/psum | solution.py:2196
  601.6 3.3 copy-start
  (38 other events, 76.1 us)
Sparse Core Ops, SparseCore 0:
  11.8 54.5 all-reduce.5
  471.8 83.2 all-reduce.7
  559.6 69.3 all-reduce.9
  634.6 37.2 all-reduce.11
Sparse Core Ops, SparseCore 1:
  14.2 128.3 all-gather.4
  144.4 107.7 all-gather.6
  297.2 136.7 reduce-scatter.3
  437.9 93.4 reduce-scatter.5
  535.3 53.8 reduce-scatter.7
